TPU v7x, 512 devices: a whole 4x8x8 slice. The times are simulated.
512 devices in a mesh: mut: 32 (over x_lo, z, core), test: 16 (over x_hi, y).
Axes of the slice: x: 4 (x_hi: 2, x_lo: 2; x = x_hi * 2 + x_lo), y: 8, z: 8, core: 2. Of those that a mesh axis runs over, the one named last changes fastest.
Arguments:
- input_activation: bfloat16 [2048, 28, 1024], P(('mut', 'test')), may hold values from -18 to 18
- ground_truth_class: int32 [2048], replicated, may hold values from 0 to 999
- remaining_pictures: int32 [128, 224], P('mut', 'test'), may hold values from 0 to 127, as said below
- learned_narrowing_kernel: bfloat16 [1024, 256], replicated, may hold values from -0.1875 to 0.1875
- learned_widening_kernel: bfloat16 [256, 1024], replicated, may hold values from -0.375 to 0.375
- narrowing_perturbation: bfloat16 [128, 1024, 256], P('mut', 'test'), may hold values from -0.09375 to 0.09375
- widening_perturbation: bfloat16 [128, 256, 1024], P('mut', None, 'test'), may hold values from -0.1875 to 0.1875
- perturbation_strength: float32 [128, 2], P('mut'), may hold values from 0.25 to 2
- readout_matrix: bfloat16 [1024, 1000], replicated, may hold values from -1 to 1
Outputs:
- kill: float32 [128, 2, 224], P('mut', None, 'test')
Inputs may be any that keep to these rules, and one draw needn't show every extreme that they name: `remaining_pictures`: entry t * 14 + j of a mutant's row names an image of test shard t; image i of a shard lies on the device at mut index i // 4. Among the entries of one mut index's 4 mutants in one test shard, at most 2 lie on any one device's images, and some device takes exactly 2.
All inputs are finite; a program needn't handle non-finite values.
Results may differ from a plain program's by a relative error of at most 0.0003.
Values may be sent and summed in bfloat16 or wider, within the bound.
No kernel may reach another device: no remote copies, remote signals or barrier semaphores. Data moves between devices by JAX's collectives and lax.ppermute only.
A program may use at most 64 MiB of HBM per device.

v0:
```python
import jax
import jax.numpy as jnp
from jax import lax
from jax.sharding import PartitionSpec as P


def on_device(
    input_activation,
    ground_truth_class,
    remaining_pictures,
    learned_narrowing_kernel,
    learned_widening_kernel,
    narrowing_perturbation,
    widening_perturbation,
    perturbation_strength,
    readout_matrix,
):
    n_test = lax.axis_size("test")
    variants_per_processor, remaining_flags = remaining_pictures.shape
    img_dev = input_activation.shape[0]
    steps = perturbation_strength.shape[1]
    width = learned_narrowing_kernel.shape[1]
    full_first, full_last = (
        lax.all_gather(narrowing_perturbation, "test", axis=1, tiled=True),
        lax.all_gather(widening_perturbation, "test", axis=2, tiled=True),
    )
    wanted_entries_sequence = remaining_pictures.reshape(-1)
    shard_index = lax.axis_index("test")
    whole = (
        wanted_entries_sequence // img_dev * n_test + shard_index
    ) * img_dev + wanted_entries_sequence % img_dev
    target_class_slice_full = jnp.take(ground_truth_class, whole)
    shard_images = lax.all_gather(input_activation, "mut", axis=0, tiled=True)
    selected_entries = jnp.take(shard_images, wanted_entries_sequence, axis=0)
    column = jnp.arange(readout_matrix.shape[1], dtype=jnp.int32)
    results = []
    for variant_member in range(variants_per_processor):
        bottleneck_unit = selected_entries[
            variant_member * remaining_flags : (variant_member + 1) * remaining_flags
        ]
        rows = bottleneck_unit.reshape(-1, bottleneck_unit.shape[2])
        target_class_slice = target_class_slice_full[
            variant_member * remaining_flags : (variant_member + 1) * remaining_flags
        ]
        first_list = []
        for step in range(steps):
            first_list.append(
                (
                    learned_narrowing_kernel.astype(jnp.float32)
                    + perturbation_strength[variant_member, step]
                    * full_first[variant_member].astype(jnp.float32)
                ).astype(jnp.bfloat16)
            )
        stacked_first = jnp.concatenate(first_list, axis=1)
        hidden_all = jnp.maximum(
            jnp.dot(rows, stacked_first, preferred_element_type=jnp.float32), 0.0
        ).astype(jnp.bfloat16)
        kills = []
        for step in range(steps):
            w_last = (
                learned_widening_kernel.astype(jnp.float32)
                + perturbation_strength[variant_member, step]
                * full_last[variant_member].astype(jnp.float32)
            ).astype(jnp.bfloat16)
            hidden = hidden_all[:, step * width : (step + 1) * width]
            out_rows = jnp.maximum(
                jnp.dot(hidden, w_last, preferred_element_type=jnp.float32)
                + rows.astype(jnp.float32),
                0.0,
            )
            pooled = jnp.mean(out_rows.reshape(bottleneck_unit.shape), axis=1).astype(jnp.bfloat16)
            logits = jnp.dot(pooled, readout_matrix, preferred_element_type=jnp.float32)
            top = jnp.max(logits, axis=1, keepdims=True)
            total = top[:, 0] + jnp.log(jnp.sum(jnp.exp(logits - top), axis=1))
            chosen = jnp.sum(
                jnp.where(column[None, :] == target_class_slice[:, None], logits, 0.0), axis=1
            )
            kills.append(total - chosen)
        results.append(jnp.stack(kills))
    return jnp.stack(results)


def solution(mesh):
    return jax.shard_map(
        on_device,
        mesh=mesh,
        in_specs=(
            P(("mut", "test"), None, None),
            P(),
            P("mut", "test"),
            P(),
            P(),
            P("mut", "test", None),
            P("mut", None, "test"),
            P("mut", None),
            P(),
        ),
        out_specs=P("mut", None, "test"),
        check_vma=False,
    )
```

profile of v0, /device:TPU:56, one launch (start us, length us, event | category | flops | bytes accessed | tf_op | source)
XLA Modules:
  0.0 363.7 jit_solution(7135138168026623373)
XLA Ops:
  6.6 0.7 all-gather.6.cloned.1.call-update
  7.3 0.0 all-gather.4.cloned.1.call-start
  7.3 1.8 copy.17
  9.1 0.0 all-gather.8.cloned.1.call-start
  9.1 0.7 all-gather.8.cloned.1.call-update
  9.8 0.8 reshape.436
  10.6 0.8 reshape.435
  11.4 1.2 copy.18
  12.7 0.8 gather_fusion.1
  13.4 0.7 fusion.121
  14.2 0.1 fusion.122
  14.2 90.0 %all-gather.6.cloned.1.call-done = bf16[4,1024,256]{2,1,0:T(8,128)(2,1)} async-done(((bf16[4,64,256]{2,1,0:T(8,128)(2,1)}), bf16[4,1024,256]{2,1,0:T(8,128)(2,1)}) %all-gather.6.cloned.1.call-update) | async-done | bytes 2097168 | tf_op jit(solution)/shard_map/all_gather | solution.py:24
  104.2 9.5 %fusion.28 = (bf16[1024,256]{1,0:T(8,128)(2,1)}, bf16[1024,256]{1,0:T(8,128)(2,1)}, bf16[1024,256]{1,0:T(8,128)(2,1)}, bf16[1024,256]{1,0:T(8,128)(2,1)}, bf16[1...) fusion(bf16[1024,256]{1,0:T(8,128)(2,1)S(1)} %copy-done.2, ...), kind=kLoop, calls=%fused_computation.75 | loop fusion | flops 7602176 | bytes 6815776 | tf_op jit(solution)/shard_map/convert_element_type | solution.py:52
  113.7 66.4 %all-gather.4.cloned.1.call-done = bf16[128,28,1024]{2,1,0:T(8,128)(2,1)} async-done(((bf16[4,28,1024]{2,1,0:T(8,128)(2,1)}), bf16[128,28,1024]{2,1,0:T(8,128)(2,1)}) %all-gather.4.cloned.1.call-update) | async-done | bytes 7340048 | tf_op jit(solution)/shard_map/all_gather | solution.py:33
  180.1 6.1 %gather_fusion = bf16[56,28,1024]{2,1,0:T(8,128)(2,1)} fusion(bf16[128,28,1024]{2,1,0:T(8,128)(2,1)} %all-gather.4.cloned.1.call-done, s32[1024]{0:T(1024)S(1)} %pad_clamp_fusion.1), kind=kCustom, calls=%fused_computation | custom fusion | bytes 6422752 | tf_op jit(solution)/shard_map/jit(_take)/gather | solution.py:34
  186.2 2.4 broadcast_select_fusion
  188.6 1.9 fusion.120
  190.5 1.3 reshape.446
  191.8 2.6 fusion.11
  194.3 78.1 %all-gather.8.cloned.1.call-done = bf16[4,256,1024]{1,2,0:T(8,128)(2,1)} async-done(((bf16[4,256,64]{1,2,0:T(8,128)(2,1)}), bf16[4,256,1024]{1,2,0:T(8,128)(2,1)}) %all-gather.8.cloned.1.call-update) | async-done | bytes 2097168 | tf_op jit(solution)/shard_map/all_gather | solution.py:25
  272.4 3.4 fusion.6
  275.8 2.6 reshape.447
  278.4 3.3 fusion.7
  281.7 2.6 reshape.448
  284.4 1.8 reduce_sum.234
  286.1 1.8 reduce_sum.237
  287.9 0.8 fusion.123
  288.7 1.4 fusion.124
  290.1 1.3 reshape.443
  291.4 1.8 fusion.10
  293.2 0.8 copy-done.5
  294.0 3.3 fusion.5
  297.3 2.6 reshape.445
  299.9 1.8 reduce_sum.231
  301.7 1.4 fusion.126
  303.1 3.3 fusion.4
  306.4 2.6 reshape.444
  309.0 1.8 reduce_sum.228
  310.8 1.4 fusion.125
  312.2 1.3 reshape.440
  313.5 1.8 fusion.9
  315.3 0.8 copy-done.7
  316.0 3.2 fusion.2
  319.3 2.6 reshape.441
  321.9 1.8 reduce_sum.222
  323.7 1.4 fusion.127
  325.1 3.2 fusion.3
  328.4 2.6 reshape.442
  331.0 1.8 reduce_sum.225
  332.8 1.4 fusion.128
  334.2 1.3 reshape.437
  335.5 1.8 fusion.8
  337.3 0.8 copy-done.3
  338.0 3.3 fusion.1
  341.3 2.6 reshape.439
  343.9 1.8 reduce_sum.219
  345.7 1.4 fusion.130
  347.1 3.3 fusion
  350.4 2.6 reshape.438
  353.1 1.8 reduce_sum.216
  354.9 0.8 fusion.129
  355.7 0.3 exponential_reduce_fusion.1
  356.1 0.3 exponential_reduce_fusion.5
  356.5 0.6 pad_maximum_fusion
  (48 shorter events, 0.3 us)
Async XLA Ops:
  6.5 281.4 %copy-start = (bf16[1024,1000]{0,1:T(8,128)(2,1)S(1)}, bf16[1024,1000]{0,1:T(8,128)(2,1)}, u32[]{:S(2)}) copy-start(bf16[1024,1000]{0,1:T(8,128)(2,1)} %param.17) | copy-start | bytes 6144004
  6.5 6.1 %copy-start.1 = (s32[2048]{0:T(1024)S(1)}, s32[2048]{0:T(1024)}, u32[]{:S(2)}) copy-start(s32[2048]{0:T(1024)} %param.10) | copy-start | bytes 24580
  6.5 6.9 %copy-start.15 = (f32[4,2]{0,1:T(2,128)S(1)}, f32[4,2]{0,1:T(2,128)}, u32[]{:S(2)}) copy-start(f32[4,2]{0,1:T(2,128)} %param.16) | copy-start | bytes 100
  6.5 97.7 %copy-start.2 = (bf16[1024,256]{1,0:T(8,128)(2,1)S(1)}, bf16[1024,256]{1,0:T(8,128)(2,1)}, u32[]{:S(2)}) copy-start(bf16[1024,256]{1,0:T(8,128)(2,1)} %param.12) | copy-start | bytes 1572868
  6.5 97.7 %all-gather.6.cloned.1.call-start = ((), (), s32[]{:S(2)}) async-start(), calls=%async_computation.1 | async-start | bytes 2228224 | tf_op jit(solution)/shard_map/all_gather | solution.py:24
  7.3 172.8 %all-gather.4.cloned.1.call-start = ((), (), s32[]{:S(2)}) async-start(), calls=%async_computation | async-start | bytes 8650752 | tf_op jit(solution)/shard_map/all_gather | solution.py:33
  9.1 263.3 %all-gather.8.cloned.1.call-start = ((), (), s32[]{:S(2)}) async-start(), calls=%async_computation.2 | async-start | bytes 2228224 | tf_op jit(solution)/shard_map/all_gather | solution.py:25
  293.2 0.8 copy-start.5
  301.7 1.4 copy-start.6
  315.3 0.8 copy-start.7
  323.7 1.4 copy-start.8
  337.3 0.8 copy-start.3
  345.7 1.4 copy-start.4
  353.1 2.6 copy-start.9
  353.1 2.6 copy-start.12
  353.1 2.6 copy-start.13
  353.1 3.1 copy-start.10
  353.1 3.1 copy-start.11
  353.1 3.1 copy-start.14
Sparse Core Ops, SparseCore 0:
  10.6 93.6 all-gather.5
  106.4 73.6 all-gather.3
  183.3 89.1 all-gather.7
where the time goes:
time: 367 us; the launch traced here: 364 us
  waiting for transfers between devices  236 us (64%)
  matrix products  44.1 us (12%)
  local copies, waits for them, and re-layouts  42.6 us (12%)
  other arithmetic  27.5 us (7%)
  between operations  13.5 us (4%)
    all_gather x1, waiting for transfers between devices, on_device(): lax.all_gather(narrowing_perturbation, 'test', axis=1, tiled=True)  90 us
    all_gather x1, waiting for transfers between devices, on_device(): lax.all_gather(widening_perturbation, 'test', axis=2, tiled=True)  78.1 us
    all_gather x1, waiting for transfers between devices, on_device(): shard_images = lax.all_gather(input_activation, 'mut', axis=0, tiled=True)  66.4 us
    dot_general x8, matrix products, on_device(): jnp.dot(hidden, w_last, preferred_element_type=jnp.float32)  26.3 us
    reshape x8, local copies, waits for them, and re-layouts, on_device(): out_rows.reshape(bottleneck_unit.shape)  21.1 us
    reduce_sum x8, other arithmetic, on_device(): jnp.mean(out_rows.reshape(bottleneck_unit.shape), axis=1)  14.3 us
    dot_general x8, matrix products, on_device(): logits = jnp.dot(pooled, readout_matrix, preferred_element_type=jnp.float32)  9.9 us
    convert_element_type x1, other arithmetic, on_device(): first_list.append((learned_narrowing_kernel.astype(jnp.float32) + perturb...  9.47 us
  transfers between devices with their start and end apart: 3, of which 3 were waited for; matrix products, arithmetic and copies ran while one was open for 8% of the time, Pallas kernels for 0%

commit v1 on v0

v1 whole, which is shorter than its diff:
```python
import jax
import jax.numpy as jnp
from jax import lax
from jax.experimental import pallas as pl
from jax.experimental.pallas import tpu as pltpu
from jax.sharding import Mesh, PartitionSpec as P

N_Y = 8
N_TEST = 16
IMG_DEV = 4
PIX = 28
SLOT = 32
SURV = 14
MUT_DEV = 4
STEPS = 2
C = 1024
B = 256
CHUNK = C // N_TEST
ROWS = SURV * SLOT


def build_weights(origin_ref, strength_ref, first_base_ref, last_base_ref, *refs):
    pieces = refs[:N_TEST]
    first_ref, last_ref = refs[N_TEST:]
    member = pl.program_id(0)
    for number in range(N_TEST):
        row = pl.multiple_of(origin_ref[number] * CHUNK, CHUNK)
        for kind, base_ref in enumerate((first_base_ref, last_base_ref)):
            base = base_ref[pl.ds(row, CHUNK), :].astype(jnp.float32)
            change = pieces[number][0, kind].astype(jnp.float32)
            for step in range(STEPS):
                value = (base + strength_ref[member, step] * change).astype(jnp.bfloat16)
                if kind == 0:
                    first_ref[0, pl.ds(row, CHUNK), step * B : (step + 1) * B] = value
                else:
                    last_ref[0, step, pl.ds(row, CHUNK), :] = value


def score(
    start_ref,
    images_ref,
    first_ref,
    last_ref,
    keep_low_ref,
    keep_high_ref,
    label_ref,
    readout_hbm_ref,
    out_ref,
    x_ref,
    pooled_ref,
    readout_ref,
    image_sem,
    readout_sem,
):
    member = pl.program_id(0)

    @pl.when(member == 0)
    def _():
        for variant in range(MUT_DEV):
            for entry in range(SURV):
                start = pl.multiple_of(start_ref[variant * SURV + entry], 8)
                pltpu.make_async_copy(
                    images_ref.at[pl.ds(start, SLOT)],
                    x_ref.at[variant, pl.ds(entry * SLOT, SLOT)],
                    image_sem.at[variant],
                ).start()
        pltpu.make_async_copy(readout_hbm_ref, readout_ref, readout_sem).start()
        pooled_ref[...] = jnp.zeros_like(pooled_ref)

    pltpu.make_async_copy(
        images_ref.at[pl.ds(0, ROWS)], x_ref.at[member], image_sem.at[member]
    ).wait()
    rows = x_ref[member]
    hidden = jnp.maximum(
        jnp.dot(rows, first_ref[0], preferred_element_type=jnp.float32), 0.0
    ).astype(jnp.bfloat16)
    for step in range(STEPS):
        expanded = lax.dot_general(
            hidden[:, step * B : (step + 1) * B],
            last_ref[0, step],
            (((1,), (1,)), ((), ())),
            preferred_element_type=jnp.float32,
        )
        out_rows = jnp.maximum(expanded + rows.astype(jnp.float32), 0.0)
        tiles = out_rows.reshape(SURV, SLOT // 8, 8, C)
        total = (
            tiles[:, 0] * keep_low_ref[0][:, :, :1]
            + tiles[:, 1]
            + tiles[:, 2]
            + tiles[:, 3] * keep_high_ref[0][:, :, :1]
        )
        pooled = (jnp.sum(total, axis=1) / PIX).astype(jnp.bfloat16)
        pooled_ref[member * STEPS + step, :SURV, :] = pooled

    @pl.when(member == MUT_DEV - 1)
    def _():
        pltpu.make_async_copy(readout_hbm_ref, readout_ref, readout_sem).wait()
        logits = jnp.dot(
            pooled_ref[...].reshape(MUT_DEV * STEPS * 16, C),
            readout_ref[...],
            preferred_element_type=jnp.float32,
        )
        top = jnp.max(logits, axis=1, keepdims=True)
        total = top + jnp.log(jnp.sum(jnp.exp(logits - top), axis=1, keepdims=True))
        column = lax.broadcasted_iota(jnp.int32, logits.shape, 1)
        chosen = jnp.sum(
            jnp.where(column == label_ref[...], logits, 0.0), axis=1, keepdims=True
        )
        kill = total - chosen
        shape = (MUT_DEV * STEPS * 16, 128)
        diagonal = lax.broadcasted_iota(jnp.int32, shape, 1) == (
            lax.broadcasted_iota(jnp.int32, shape, 0) % 16
        )
        spread = jnp.where(diagonal, jnp.broadcast_to(kill, shape), 0.0)
        lined = jnp.sum(spread.reshape(MUT_DEV * STEPS, 16, 128), axis=1)
        for variant in range(MUT_DEV):
            out_ref[variant] = lined[variant * STEPS : (variant + 1) * STEPS, :SURV]


def on_device(
    input_activation,
    ground_truth_class,
    remaining_pictures,
    learned_narrowing_kernel,
    learned_widening_kernel,
    narrowing_perturbation,
    widening_perturbation,
    perturbation_strength,
    readout_matrix,
):
    swap = [(0, 1), (1, 0)]
    up = [(i, (i + 1) % N_Y) for i in range(N_Y)]
    down = [(i, (i - 1) % N_Y) for i in range(N_Y)]
    my_xl = lax.axis_index("xl")
    my_xh = lax.axis_index("xh")
    my_y = lax.axis_index("y")

    own_rows = input_activation.reshape(IMG_DEV * PIX, C)
    partner_rows = lax.ppermute(own_rows, "xl", swap)
    images = lax.all_gather(
        jnp.concatenate([own_rows, partner_rows]), ("z", "core"), axis=0, tiled=True
    )

    message = jnp.stack(
        [narrowing_perturbation, jnp.transpose(widening_perturbation, (0, 2, 1))], axis=1
    )
    other = lax.ppermute(message, "xh", swap)
    pieces, origins = [], []
    for plane, seed in ((my_xh, message), (1 - my_xh, other)):
        pieces.append(seed)
        origins.append(plane * N_Y + my_y)
        going_up = going_down = seed
        for hop in range(1, 5):
            going_up = lax.ppermute(going_up, "y", up)
            pieces.append(going_up)
            origins.append(plane * N_Y + (my_y - hop) % N_Y)
            if hop < 4:
                going_down = lax.ppermute(going_down, "y", down)
                pieces.append(going_down)
                origins.append(plane * N_Y + (my_y + hop) % N_Y)
    origin = jnp.stack(origins).astype(jnp.int32)

    smem = pl.BlockSpec(memory_space=pltpu.SMEM)
    hbm = pl.BlockSpec(memory_space=pl.ANY)
    piece_spec = pl.BlockSpec((1, 2, CHUNK, B), lambda m: (m, 0, 0, 0))
    first_spec = pl.BlockSpec((1, C, STEPS * B), lambda m: (m, 0, 0))
    last_spec = pl.BlockSpec((1, STEPS, C, B), lambda m: (m, 0, 0, 0))
    base_spec = pl.BlockSpec((C, B), lambda m: (0, 0))
    first_all, last_all = pl.pallas_call(
        build_weights,
        grid=(MUT_DEV,),
        in_specs=[smem, smem, base_spec, base_spec] + [piece_spec] * N_TEST,
        out_specs=[first_spec, last_spec],
        out_shape=[
            jax.ShapeDtypeStruct((MUT_DEV, C, STEPS * B), jnp.bfloat16),
            jax.ShapeDtypeStruct((MUT_DEV, STEPS, C, B), jnp.bfloat16),
        ],
        compiler_params=pltpu.CompilerParams(vmem_limit_bytes=40 * 2**20),
    )(
        origin,
        perturbation_strength,
        learned_narrowing_kernel,
        learned_widening_kernel.T,
        *pieces,
    )

    wanted = remaining_pictures.reshape(-1)
    holder = wanted // IMG_DEV
    within = wanted % IMG_DEV
    shard = my_xh * N_Y + my_y
    label = jnp.take(ground_truth_class, (holder * N_TEST + shard) * IMG_DEV + within)
    slot = (holder // 16 != my_xl).astype(jnp.int32)
    start = (
        ((holder % 16) * 2 + slot) * (IMG_DEV * PIX) + (within // 2) * (2 * PIX) + (within % 2) * 24
    )
    odd = (within % 2).reshape(MUT_DEV, SURV, 1, 1)
    sublane = jnp.arange(8, dtype=jnp.int32).reshape(1, 1, 8, 1)
    keep_shape = (MUT_DEV, SURV, 8, 128)
    keep_low = jnp.broadcast_to(
        jnp.where((odd == 0) | (sublane >= 4), 1.0, 0.0), keep_shape
    ).astype(jnp.float32)
    keep_high = jnp.broadcast_to(
        jnp.where((odd == 1) | (sublane < 4), 1.0, 0.0), keep_shape
    ).astype(jnp.float32)
    label_rows = jnp.broadcast_to(
        jnp.pad(label.reshape(MUT_DEV, 1, SURV), ((0, 0), (0, 0), (0, 2))), (MUT_DEV, STEPS, 16)
    ).reshape(MUT_DEV * STEPS * 16, 1)

    keep_spec = pl.BlockSpec((1, SURV, 8, 128), lambda m: (m, 0, 0, 0))
    return pl.pallas_call(
        score,
        grid=(MUT_DEV,),
        in_specs=[
            smem,
            hbm,
            first_spec,
            last_spec,
            keep_spec,
            keep_spec,
            pl.BlockSpec((MUT_DEV * STEPS * 16, 1), lambda m: (0, 0)),
            hbm,
        ],
        out_specs=pl.BlockSpec((MUT_DEV, STEPS, SURV), lambda m: (0, 0, 0)),
        out_shape=jax.ShapeDtypeStruct((MUT_DEV, STEPS, SURV), jnp.float32),
        scratch_shapes=[
            pltpu.VMEM((MUT_DEV, ROWS, C), jnp.bfloat16),
            pltpu.VMEM((MUT_DEV * STEPS, 16, C), jnp.bfloat16),
            pltpu.VMEM((C, readout_matrix.shape[1]), jnp.bfloat16),
            pltpu.SemaphoreType.DMA((MUT_DEV,)),
            pltpu.SemaphoreType.DMA,
        ],
        compiler_params=pltpu.CompilerParams(vmem_limit_bytes=48 * 2**20),
    )(start, images, first_all, last_all, keep_low, keep_high, label_rows, readout_matrix)


def solution(mesh):
    fine = Mesh(mesh.devices.reshape(2, 8, 2, 2, N_Y), ("xl", "z", "core", "xh", "y"))
    mut = ("xl", "z", "core")
    test = ("xh", "y")
    return jax.shard_map(
        on_device,
        mesh=fine,
        in_specs=(
            P(mut + test, None, None),
            P(),
            P(mut, test),
            P(),
            P(),
            P(mut, test, None),
            P(mut, None, test),
            P(mut, None),
            P(),
        ),
        out_specs=P(mut, None, test),
        check_vma=False,
    )
```

time: 367 us -> 118 us (0.32)
  the two profiles are of different devices: /device:TPU:56 before, /device:TPU:4 now
where the time goes in v1:
time: 118 us; the launch traced here: 116 us
  starting transfers between devices  53.4 us (45%)
  local copies, waits for them, and re-layouts  20.9 us (18%)
  Pallas kernels  14.3 us (12%)
  between operations  13.9 us (12%)
  waiting for transfers between devices  9.64 us (8%)
  other arithmetic  4.04 us (3%)
    ppermute x6, starting transfers between devices, on_device(): going_down = lax.ppermute(going_down, 'y', down)  28.4 us
    unnamed x42, local copies, waits for them, and re-layouts  17.3 us
    ppermute x8, starting transfers between devices, on_device(): going_up = lax.ppermute(going_up, 'y', up)  15.4 us
    pallas_call x1, Pallas kernels, on_device(): pl.pallas_call(score, grid=(MUT_DEV,), in_specs=[smem, hbm, first_spec, l...  9.97 us
    ppermute x1, starting transfers between devices, on_device(): other = lax.ppermute(message, 'xh', swap)  6.47 us
    ppermute x1, waiting for transfers between devices, on_device(): partner_rows = lax.ppermute(own_rows, 'xl', swap)  6.12 us
    pallas_call x1, Pallas kernels, on_device(): pl.pallas_call(build_weights, grid=(MUT_DEV,), in_specs=[smem, smem, base...  4.29 us
    ppermute x8, waiting for transfers between devices, on_device(): going_up = lax.ppermute(going_up, 'y', up)  3.48 us
  transfers between devices with their start and end apart: 17, of which 3 were waited for; matrix products, arithmetic and copies ran while one was open for 9% of the time, Pallas kernels for 4%

profile of v1, /device:TPU:4, one launch (start us, length us, event | category | flops | bytes accessed | tf_op | source)
XLA Modules:
  0.0 116.2 jit_solution(213592176810295755)
XLA Ops:
  6.5 1.0 copy.15
  7.6 0.0 copy-start.3
  7.7 3.2 %collective-permute-start = (bf16[112,1024]{1,0:T(8,128)(2,1)S(1)}, bf16[112,1024]{1,0:T(8,128)(2,1)S(1)}, u32[]{:S(2)}, u32[]{:S(2)}) collective-permute-start(bf16[112,1024]{1,0:T(8,128)(2,1)S(1)} %reshape.209), channel_id=1, source_target_pairs={{0,256},{256,0},{1,257},{257,1},{2,258},{258,2},{3,259},{259,3},{4... | collective-permute-start | bytes 688136 | tf_op jit(solution)/shard_map/ppermute | solution.py:139
  10.9 6.1 %collective-permute-done = bf16[112,1024]{1,0:T(8,128)(2,1)S(1)} collective-permute-done((bf16[112,1024]{1,0:T(8,128)(2,1)S(1)}, bf16[112,1024]{1,0:T(8,128)(2,1)S(1)}, u32[]{:S(2)}, u32[]{:S(2)}) %collective-permute-start) | collective-permute-done | bytes 229408 | tf_op jit(solution)/shard_map/ppermute | solution.py:139
  17.0 0.8 pad_maximum_fusion
  17.8 0.0 all-gather.2.cloned.1.call-update
  17.9 1.0 pad_maximum_fusion.1.refs_0_
  18.9 6.5 %collective-permute-start.8 = (bf16[4,2,64,256]{3,2,1,0:T(8,128)(2,1)S(1)}, bf16[4,2,64,256]{3,2,1,0:T(8,128)(2,1)S(1)}, u32[]{:S(2)}, u32[]{:S(2)}) collective-permute-start(bf16[4,2,64,256]{3,2,1,0:T(8,128)(2,1)S(1)} %pad_maximum_fusion.1.refs_0_), channel_id=1, source_target_pairs={{0,8},{8,0},{1,9},{9,1},{2,10},{10,2},{3,11},{11,3},{4,12},{12,4},... | collective-permute-start | bytes 786440 | tf_op jit(solution)/shard_map/ppermute | solution.py:147
  25.3 1.9 %collective-permute-start.1 = (bf16[4,2,64,256]{3,2,1,0:T(8,128)(2,1)S(1)}, bf16[4,2,64,256]{3,2,1,0:T(8,128)(2,1)S(1)}, u32[]{:S(2)}, u32[]{:S(2)}) collective-permute-start(bf16[4,2,64,256]{3,2,1,0:T(8,128)(2,1)S(1)} %pad_maximum_fusion.1.refs_0_), channel_id=1, source_target_pairs={{0,1},{1,2},{2,3},{3,4},{4,5},{5,6},{6,7},{7,0},{8,9},{9,10},{10,1... | collective-permute-start | bytes 786440 | tf_op jit(solution)/shard_map/ppermute | solution.py:154
  27.3 5.1 %collective-permute-start.2 = (bf16[4,2,64,256]{3,2,1,0:T(8,128)(2,1)S(1)}, bf16[4,2,64,256]{3,2,1,0:T(8,128)(2,1)S(1)}, u32[]{:S(2)}, u32[]{:S(2)}) collective-permute-start(bf16[4,2,64,256]{3,2,1,0:T(8,128)(2,1)S(1)} %pad_maximum_fusion.1.refs_0_), channel_id=1, source_target_pairs={{0,7},{1,0},{2,1},{3,2},{4,3},{5,4},{6,5},{7,6},{8,15},{9,8},{10,9... | collective-permute-start | bytes 786440 | tf_op jit(solution)/shard_map/ppermute | solution.py:158
  32.4 0.8 reshape.210
  33.2 0.8 reshape.208
  34.0 0.7 broadcast_compare_fusion
  34.7 0.0 collective-permute-done.8.refs_8_
  34.7 1.9 %collective-permute-start.9 = (bf16[4,2,64,256]{3,2,1,0:T(8,128)(2,1)S(1)}, bf16[4,2,64,256]{3,2,1,0:T(8,128)(2,1)S(1)}, u32[]{:S(2)}, u32[]{:S(2)}) collective-permute-start(bf16[4,2,64,256]{3,2,1,0:T(8,128)(2,1)S(1)} %collective-permute-done.8.refs_8_), channel_id=1, source_target_pairs={{0,1},{1,2},{2,3},{3,4},{4,5},{5,6},{6,7},{7,0},{8,9},{9,10},{10,1... | collective-permute-start | bytes 786440 | tf_op jit(solution)/shard_map/ppermute | solution.py:154
  36.7 0.8 gather_fusion
  37.4 0.1 gather.7
  37.5 0.7 select_bitcast_fusion
  38.2 5.1 %collective-permute-start.10 = (bf16[4,2,64,256]{3,2,1,0:T(8,128)(2,1)S(1)}, bf16[4,2,64,256]{3,2,1,0:T(8,128)(2,1)S(1)}, u32[]{:S(2)}, u32[]{:S(2)}) collective-permute-start(bf16[4,2,64,256]{3,2,1,0:T(8,128)(2,1)S(1)} %collective-permute-done.8.refs_8_), channel_id=1, source_target_pairs={{0,7},{1,0},{2,1},{3,2},{4,3},{5,4},{6,5},{7,6},{8,15},{9,8},{10,9... | collective-permute-start | bytes 786440 | tf_op jit(solution)/shard_map/ppermute | solution.py:158
  43.4 0.0 collective-permute-done.1.refs_1_
  43.4 1.9 %collective-permute-start.3 = (bf16[4,2,64,256]{3,2,1,0:T(8,128)(2,1)S(1)}, bf16[4,2,64,256]{3,2,1,0:T(8,128)(2,1)S(1)}, u32[]{:S(2)}, u32[]{:S(2)}) collective-permute-start(bf16[4,2,64,256]{3,2,1,0:T(8,128)(2,1)S(1)} %collective-permute-done.1.refs_1_), channel_id=1, source_target_pairs={{0,1},{1,2},{2,3},{3,4},{4,5},{5,6},{6,7},{7,0},{8,9},{9,10},{10,1... | collective-permute-start | bytes 786440 | tf_op jit(solution)/shard_map/ppermute | solution.py:154
  45.3 0.0 collective-permute-done.9.refs_9_
  45.3 1.9 %collective-permute-start.11 = (bf16[4,2,64,256]{3,2,1,0:T(8,128)(2,1)S(1)}, bf16[4,2,64,256]{3,2,1,0:T(8,128)(2,1)S(1)}, u32[]{:S(2)}, u32[]{:S(2)}) collective-permute-start(bf16[4,2,64,256]{3,2,1,0:T(8,128)(2,1)S(1)} %collective-permute-done.9.refs_9_), channel_id=1, source_target_pairs={{0,1},{1,2},{2,3},{3,4},{4,5},{5,6},{6,7},{7,0},{8,9},{9,10},{10,1... | collective-permute-start | bytes 786440 | tf_op jit(solution)/shard_map/ppermute | solution.py:154
  47.3 0.0 collective-permute-done.2.refs_2_
  47.3 5.1 %collective-permute-start.4 = (bf16[4,2,64,256]{3,2,1,0:T(8,128)(2,1)S(1)}, bf16[4,2,64,256]{3,2,1,0:T(8,128)(2,1)}, u32[]{:S(2)}, u32[]{:S(2)}) collective-permute-start(bf16[4,2,64,256]{3,2,1,0:T(8,128)(2,1)S(1)} %collective-permute-done.2.refs_2_), channel_id=1, source_target_pairs={{0,7},{1,0},{2,1},{3,2},{4,3},{5,4},{6,5},{7,6},{8,15},{9,8},{10,9... | collective-permute-start | bytes 786440 | tf_op jit(solution)/shard_map/ppermute | solution.py:158
  52.4 0.0 collective-permute-done.10.refs_10_
  52.5 3.9 %collective-permute-start.12 = (bf16[4,2,64,256]{3,2,1,0:T(8,128)(2,1)S(1)}, bf16[4,2,64,256]{3,2,1,0:T(8,128)(2,1)}, u32[]{:S(2)}, u32[]{:S(2)}) collective-permute-start(bf16[4,2,64,256]{3,2,1,0:T(8,128)(2,1)S(1)} %collective-permute-done.10.refs_10_), channel_id=1, source_target_pairs={{0,7},{1,0},{2,1},{3,2},{4,3},{5,4},{6,5},{7,6},{8,15},{9,8},{10,9... | collective-permute-start | bytes 786440 | tf_op jit(solution)/shard_map/ppermute | solution.py:158
  56.4 0.0 collective-permute-done.3.refs_3_
  56.4 1.9 %collective-permute-start.5 = (bf16[4,2,64,256]{3,2,1,0:T(8,128)(2,1)S(1)}, bf16[4,2,64,256]{3,2,1,0:T(8,128)(2,1)}, u32[]{:S(2)}, u32[]{:S(2)}) collective-permute-start(bf16[4,2,64,256]{3,2,1,0:T(8,128)(2,1)S(1)} %collective-permute-done.3.refs_3_), channel_id=1, source_target_pairs={{0,1},{1,2},{2,3},{3,4},{4,5},{5,6},{6,7},{7,0},{8,9},{9,10},{10,1... | collective-permute-start | bytes 786440 | tf_op jit(solution)/shard_map/ppermute | solution.py:154
  58.3 0.7 copy-done.14
  59.0 0.0 collective-permute-done.11.refs_11_
  59.0 1.9 %collective-permute-start.13 = (bf16[4,2,64,256]{3,2,1,0:T(8,128)(2,1)S(1)}, bf16[4,2,64,256]{3,2,1,0:T(8,128)(2,1)}, u32[]{:S(2)}, u32[]{:S(2)}) collective-permute-start(bf16[4,2,64,256]{3,2,1,0:T(8,128)(2,1)S(1)} %collective-permute-done.11.refs_11_), channel_id=1, source_target_pairs={{0,1},{1,2},{2,3},{3,4},{4,5},{5,6},{6,7},{7,0},{8,9},{9,10},{10,1... | collective-permute-start | bytes 786440 | tf_op jit(solution)/shard_map/ppermute | solution.py:154
  61.0 0.7 copy-done.16
  61.7 0.1 or_select_fusion.1
  61.8 0.0 collective-permute-done.4.refs_4_
  61.8 5.1 %collective-permute-start.6 = (bf16[4,2,64,256]{3,2,1,0:T(8,128)(2,1)}, bf16[4,2,64,256]{3,2,1,0:T(8,128)(2,1)}, u32[]{:S(2)}, u32[]{:S(2)}) collective-permute-start(bf16[4,2,64,256]{3,2,1,0:T(8,128)(2,1)} %collective-permute-done.4.refs_4_), channel_id=1, source_target_pairs={{0,7},{1,0},{2,1},{3,2},{4,3},{5,4},{6,5},{7,6},{8,15},{9,8},{10,9... | collective-permute-start | bytes 786440 | tf_op jit(solution)/shard_map/ppermute | solution.py:158
  66.9 0.0 collective-permute-done.12.refs_12_
  66.9 3.9 %collective-permute-start.14 = (bf16[4,2,64,256]{3,2,1,0:T(8,128)(2,1)}, bf16[4,2,64,256]{3,2,1,0:T(8,128)(2,1)}, u32[]{:S(2)}, u32[]{:S(2)}) collective-permute-start(bf16[4,2,64,256]{3,2,1,0:T(8,128)(2,1)} %collective-permute-done.12.refs_12_), channel_id=1, source_target_pairs={{0,7},{1,0},{2,1},{3,2},{4,3},{5,4},{6,5},{7,6},{8,15},{9,8},{10,9... | collective-permute-start | bytes 786440 | tf_op jit(solution)/shard_map/ppermute | solution.py:158
  70.8 0.0 collective-permute-done.5.refs_5_
  70.9 1.9 %collective-permute-start.7 = (bf16[4,2,64,256]{3,2,1,0:T(8,128)(2,1)}, bf16[4,2,64,256]{3,2,1,0:T(8,128)(2,1)}, u32[]{:S(2)}, u32[]{:S(2)}) collective-permute-start(bf16[4,2,64,256]{3,2,1,0:T(8,128)(2,1)} %collective-permute-done.5.refs_5_), channel_id=1, source_target_pairs={{0,1},{1,2},{2,3},{3,4},{4,5},{5,6},{6,7},{7,0},{8,9},{9,10},{10,1... | collective-permute-start | bytes 786440 | tf_op jit(solution)/shard_map/ppermute | solution.py:154
  72.8 1.9 %collective-permute-start.15 = (bf16[4,2,64,256]{3,2,1,0:T(8,128)(2,1)}, bf16[4,2,64,256]{3,2,1,0:T(8,128)(2,1)}, u32[]{:S(2)}, u32[]{:S(2)}) collective-permute-start(bf16[4,2,64,256]{3,2,1,0:T(8,128)(2,1)} %collective-permute-done.13.refs_13_), channel_id=1, source_target_pairs={{0,1},{1,2},{2,3},{3,4},{4,5},{5,6},{6,7},{7,0},{8,9},{9,10},{10,1... | collective-permute-start | bytes 786440 | tf_op jit(solution)/shard_map/ppermute | solution.py:154
  74.8 1.3 %copy.16 = bf16[256,1024]{0,1:T(8,128)(2,1)S(1)} copy(bf16[256,1024]{1,0:T(8,128)(2,1)} %param.13) | data formatting | bytes 1048576 | tf_op args[4]
  76.1 0.1 copy.17.strength_ref
  76.2 0.1 reshape.220.label_ref
  76.3 2.9 %copy.19.readout_hbm_ref = bf16[1024,1000]{1,0:T(8,128)(2,1)S(1)} copy(bf16[1024,1000]{0,1:T(8,128)(2,1)} %param.17) | data formatting | bytes 4096000 | tf_op args[8]
  79.2 0.1 stack.76.origin_ref
  79.3 0.7 or_select_fusion
  80.0 0.0 collective-permute-done.6.refs_6_
  80.0 0.0 collective-permute-done.14.refs_14_
  80.0 0.7 collective-permute-done.7.refs_7_
  80.7 2.8 %collective-permute-done.15.refs_15_ = bf16[4,2,64,256]{3,2,1,0:T(8,128)(2,1)} collective-permute-done((bf16[4,2,64,256]{3,2,1,0:T(8,128)(2,1)}, bf16[4,2,64,256]{3,2,1,0:T(8,128)(2,1)}, u32[]{:S(2)}, u32[]{:S(2)}) %collective-permute-start.15) | collective-permute-done | bytes 262176 | tf_op jit(solution)/shard_map/ppermute | solution.py:154
  83.5 0.9 copy-done.5
  84.4 0.9 copy-done.7
  85.4 0.9 copy-done.9
  86.3 0.9 copy-done.11
  87.3 0.9 copy-done.13
  88.2 0.9 copy-done.15
  89.2 0.9 copy-done.17
  90.1 4.3 %shard_map.91 = (bf16[4,1024,512]{2,1,0:T(8,128)(2,1)S(1)}, bf16[4,2,1024,256]{3,2,1,0:T(8,128)(2,1)S(1)}) custom-call(s32[16]{0:T(128)S(1)} %stack.76.origin_ref, f32[4,2]{1,0:T(4,128)S(1)} %copy.17.strength_ref, bf16[1024,256]{1,0:T(8,128)(2,1)S(1)} %copy-done.3, bf16[1024,256]{1,0:T(8,128)(2,1)S(1)} %bitcast.27, ...), custom_call_target="tpu_custom_call" | custom-call | tf_op jit(solution)/shard_map/pallas_call | solution.py:169
  94.4 2.0 %copy-done.1 = bf16[4,1024,512]{2,1,0:T(8,128)(2,1)} copy-done((bf16[4,1024,512]{2,1,0:T(8,128)(2,1)}, bf16[4,1024,512]{2,1,0:T(8,128)(2,1)S(1)}, u32[]{:S(2)}) %copy-start.1) | copy-done | bytes 4194328
  96.4 1.9 %copy-done.2 = bf16[4,2,1024,256]{3,2,1,0:T(8,128)(2,1)} copy-done((bf16[4,2,1024,256]{3,2,1,0:T(8,128)(2,1)}, bf16[4,2,1024,256]{3,2,1,0:T(8,128)(2,1)S(1)}, u32[]{:S(2)}) %copy-start.2) | copy-done | bytes 4194328
  98.4 0.1 broadcast_in_dim.35.keep_low_ref
  98.5 0.9 broadcast_in_dim.36.keep_high_ref
  99.4 10.0 %shard_map.92 = f32[4,2,14]{2,1,0:T(2,128)} custom-call(s32[56]{0:T(128)S(1)} %fusion.10.start_ref, bf16[3584,1024]{1,0:T(8,128)(2,1)} %all-gather.2.cloned.1.call-done.images_ref, bf16[4,1024,512]{2,1,0:T(8,128)(2,1)} %copy-done.1, bf16[4,2,1024,256]{3,2,1,0:T(8,128)(2,1)} %copy-done.2, f32[4,14,8,128]{3,2,1,0:T(8,128)S(1)} %broadcast_in_dim.35.keep_low_ref, ...), custom_call_target="tpu_custom_call" | custom-call | tf_op jit(solution)/shard_map/pallas_call | solution.py:210
  (38 shorter events, 0.2 us)
Async XLA Ops:
  6.5 30.1 %copy-start = (s32[2048]{0:T(1024)S(1)}, s32[2048]{0:T(1024)}, u32[]{:S(2)}) copy-start(s32[2048]{0:T(1024)} %param.10) | copy-start | bytes 24580
  6.5 69.6 %copy-start.18 = (f32[4,2]{0,1:T(2,128)S(1)}, f32[4,2]{0,1:T(2,128)}, u32[]{:S(2)}) copy-start(f32[4,2]{0,1:T(2,128)} %param.16) | copy-start | bytes 100
  6.5 91.8 %all-gather.2.cloned.1.call-start = ((), (), s32[]{:S(2)}) async-start(), calls=%async_computation | async-start | bytes 7798784 | tf_op jit(solution)/shard_map/all_gather | solution.py:140
  7.6 75.9 %copy-start.3 = (bf16[1024,256]{1,0:T(8,128)(2,1)S(1)}, bf16[1024,256]{1,0:T(8,128)(2,1)}, u32[]{:S(2)}) copy-start(bf16[1024,256]{1,0:T(8,128)(2,1)} %first_base_ref.1) | copy-start | bytes 1572868
  7.7 9.4 %collective-permute-start = (bf16[112,1024]{1,0:T(8,128)(2,1)S(1)}, bf16[112,1024]{1,0:T(8,128)(2,1)S(1)}, u32[]{:S(2)}, u32[]{:S(2)}) collective-permute-start(bf16[112,1024]{1,0:T(8,128)(2,1)S(1)} %reshape.209), channel_id=1, source_target_pairs={{0,256},{256,0},{1,257},{257,1},{2,258},{258,2},{3,259},{259,3},{4... | collective-permute-start | bytes 688136 | tf_op jit(solution)/shard_map/ppermute | solution.py:139
  18.9 15.8 %collective-permute-start.8 = (bf16[4,2,64,256]{3,2,1,0:T(8,128)(2,1)S(1)}, bf16[4,2,64,256]{3,2,1,0:T(8,128)(2,1)S(1)}, u32[]{:S(2)}, u32[]{:S(2)}) collective-permute-start(bf16[4,2,64,256]{3,2,1,0:T(8,128)(2,1)S(1)} %pad_maximum_fusion.1.refs_0_), channel_id=1, source_target_pairs={{0,8},{8,0},{1,9},{9,1},{2,10},{10,2},{3,11},{11,3},{4,12},{12,4},... | collective-permute-start | bytes 786440 | tf_op jit(solution)/shard_map/ppermute | solution.py:147
  25.3 18.0 %collective-permute-start.1 = (bf16[4,2,64,256]{3,2,1,0:T(8,128)(2,1)S(1)}, bf16[4,2,64,256]{3,2,1,0:T(8,128)(2,1)S(1)}, u32[]{:S(2)}, u32[]{:S(2)}) collective-permute-start(bf16[4,2,64,256]{3,2,1,0:T(8,128)(2,1)S(1)} %pad_maximum_fusion.1.refs_0_), channel_id=1, source_target_pairs={{0,1},{1,2},{2,3},{3,4},{4,5},{5,6},{6,7},{7,0},{8,9},{9,10},{10,1... | collective-permute-start | bytes 786440 | tf_op jit(solution)/shard_map/ppermute | solution.py:154
  27.3 20.0 %collective-permute-start.2 = (bf16[4,2,64,256]{3,2,1,0:T(8,128)(2,1)S(1)}, bf16[4,2,64,256]{3,2,1,0:T(8,128)(2,1)S(1)}, u32[]{:S(2)}, u32[]{:S(2)}) collective-permute-start(bf16[4,2,64,256]{3,2,1,0:T(8,128)(2,1)S(1)} %pad_maximum_fusion.1.refs_0_), channel_id=1, source_target_pairs={{0,7},{1,0},{2,1},{3,2},{4,3},{5,4},{6,5},{7,6},{8,15},{9,8},{10,9... | collective-permute-start | bytes 786440 | tf_op jit(solution)/shard_map/ppermute | solution.py:158
  34.7 41.5 %copy-start.4 = (bf16[4,2,64,256]{3,2,1,0:T(8,128)(2,1)}, bf16[4,2,64,256]{3,2,1,0:T(8,128)(2,1)S(1)}, u32[]{:S(2)}) copy-start(bf16[4,2,64,256]{3,2,1,0:T(8,128)(2,1)S(1)} %collective-permute-done.8.refs_8_) | copy-start | bytes 786436
  34.7 10.6 %collective-permute-start.9 = (bf16[4,2,64,256]{3,2,1,0:T(8,128)(2,1)S(1)}, bf16[4,2,64,256]{3,2,1,0:T(8,128)(2,1)S(1)}, u32[]{:S(2)}, u32[]{:S(2)}) collective-permute-start(bf16[4,2,64,256]{3,2,1,0:T(8,128)(2,1)S(1)} %collective-permute-done.8.refs_8_), channel_id=1, source_target_pairs={{0,1},{1,2},{2,3},{3,4},{4,5},{5,6},{6,7},{7,0},{8,9},{9,10},{10,1... | collective-permute-start | bytes 786440 | tf_op jit(solution)/shard_map/ppermute | solution.py:154
  38.2 14.2 %collective-permute-start.10 = (bf16[4,2,64,256]{3,2,1,0:T(8,128)(2,1)S(1)}, bf16[4,2,64,256]{3,2,1,0:T(8,128)(2,1)S(1)}, u32[]{:S(2)}, u32[]{:S(2)}) collective-permute-start(bf16[4,2,64,256]{3,2,1,0:T(8,128)(2,1)S(1)} %collective-permute-done.8.refs_8_), channel_id=1, source_target_pairs={{0,7},{1,0},{2,1},{3,2},{4,3},{5,4},{6,5},{7,6},{8,15},{9,8},{10,9... | collective-permute-start | bytes 786440 | tf_op jit(solution)/shard_map/ppermute | solution.py:158
  43.4 32.8 %copy-start.6 = (bf16[4,2,64,256]{3,2,1,0:T(8,128)(2,1)}, bf16[4,2,64,256]{3,2,1,0:T(8,128)(2,1)S(1)}, u32[]{:S(2)}) copy-start(bf16[4,2,64,256]{3,2,1,0:T(8,128)(2,1)S(1)} %collective-permute-done.1.refs_1_) | copy-start | bytes 786436
  43.4 13.0 %collective-permute-start.3 = (bf16[4,2,64,256]{3,2,1,0:T(8,128)(2,1)S(1)}, bf16[4,2,64,256]{3,2,1,0:T(8,128)(2,1)S(1)}, u32[]{:S(2)}, u32[]{:S(2)}) collective-permute-start(bf16[4,2,64,256]{3,2,1,0:T(8,128)(2,1)S(1)} %collective-permute-done.1.refs_1_), channel_id=1, source_target_pairs={{0,1},{1,2},{2,3},{3,4},{4,5},{5,6},{6,7},{7,0},{8,9},{9,10},{10,1... | collective-permute-start | bytes 786440 | tf_op jit(solution)/shard_map/ppermute | solution.py:154
  45.3 30.9 %copy-start.10 = (bf16[4,2,64,256]{3,2,1,0:T(8,128)(2,1)}, bf16[4,2,64,256]{3,2,1,0:T(8,128)(2,1)S(1)}, u32[]{:S(2)}) copy-start(bf16[4,2,64,256]{3,2,1,0:T(8,128)(2,1)S(1)} %collective-permute-done.9.refs_9_) | copy-start | bytes 786436
  45.3 13.7 %collective-permute-start.11 = (bf16[4,2,64,256]{3,2,1,0:T(8,128)(2,1)S(1)}, bf16[4,2,64,256]{3,2,1,0:T(8,128)(2,1)S(1)}, u32[]{:S(2)}, u32[]{:S(2)}) collective-permute-start(bf16[4,2,64,256]{3,2,1,0:T(8,128)(2,1)S(1)} %collective-permute-done.9.refs_9_), channel_id=1, source_target_pairs={{0,1},{1,2},{2,3},{3,4},{4,5},{5,6},{6,7},{7,0},{8,9},{9,10},{10,1... | collective-permute-start | bytes 786440 | tf_op jit(solution)/shard_map/ppermute | solution.py:154
  47.3 28.9 %copy-start.8 = (bf16[4,2,64,256]{3,2,1,0:T(8,128)(2,1)}, bf16[4,2,64,256]{3,2,1,0:T(8,128)(2,1)S(1)}, u32[]{:S(2)}) copy-start(bf16[4,2,64,256]{3,2,1,0:T(8,128)(2,1)S(1)} %collective-permute-done.2.refs_2_) | copy-start | bytes 786436
  47.3 14.5 %collective-permute-start.4 = (bf16[4,2,64,256]{3,2,1,0:T(8,128)(2,1)S(1)}, bf16[4,2,64,256]{3,2,1,0:T(8,128)(2,1)}, u32[]{:S(2)}, u32[]{:S(2)}) collective-permute-start(bf16[4,2,64,256]{3,2,1,0:T(8,128)(2,1)S(1)} %collective-permute-done.2.refs_2_), channel_id=1, source_target_pairs={{0,7},{1,0},{2,1},{3,2},{4,3},{5,4},{6,5},{7,6},{8,15},{9,8},{10,9... | collective-permute-start | bytes 786440 | tf_op jit(solution)/shard_map/ppermute | solution.py:158
  52.5 23.8 %copy-start.12 = (bf16[4,2,64,256]{3,2,1,0:T(8,128)(2,1)}, bf16[4,2,64,256]{3,2,1,0:T(8,128)(2,1)S(1)}, u32[]{:S(2)}) copy-start(bf16[4,2,64,256]{3,2,1,0:T(8,128)(2,1)S(1)} %collective-permute-done.10.refs_10_) | copy-start | bytes 786436
  52.5 14.4 %collective-permute-start.12 = (bf16[4,2,64,256]{3,2,1,0:T(8,128)(2,1)S(1)}, bf16[4,2,64,256]{3,2,1,0:T(8,128)(2,1)}, u32[]{:S(2)}, u32[]{:S(2)}) collective-permute-start(bf16[4,2,64,256]{3,2,1,0:T(8,128)(2,1)S(1)} %collective-permute-done.10.refs_10_), channel_id=1, source_target_pairs={{0,7},{1,0},{2,1},{3,2},{4,3},{5,4},{6,5},{7,6},{8,15},{9,8},{10,9... | collective-permute-start | bytes 786440 | tf_op jit(solution)/shard_map/ppermute | solution.py:158
  56.4 14.4 %collective-permute-start.5 = (bf16[4,2,64,256]{3,2,1,0:T(8,128)(2,1)S(1)}, bf16[4,2,64,256]{3,2,1,0:T(8,128)(2,1)}, u32[]{:S(2)}, u32[]{:S(2)}) collective-permute-start(bf16[4,2,64,256]{3,2,1,0:T(8,128)(2,1)S(1)} %collective-permute-done.3.refs_3_), channel_id=1, source_target_pairs={{0,1},{1,2},{2,3},{3,4},{4,5},{5,6},{6,7},{7,0},{8,9},{9,10},{10,1... | collective-permute-start | bytes 786440 | tf_op jit(solution)/shard_map/ppermute | solution.py:154
  58.3 0.7 copy-start.14
  59.0 13.7 %collective-permute-start.13 = (bf16[4,2,64,256]{3,2,1,0:T(8,128)(2,1)S(1)}, bf16[4,2,64,256]{3,2,1,0:T(8,128)(2,1)}, u32[]{:S(2)}, u32[]{:S(2)}) collective-permute-start(bf16[4,2,64,256]{3,2,1,0:T(8,128)(2,1)S(1)} %collective-permute-done.11.refs_11_), channel_id=1, source_target_pairs={{0,1},{1,2},{2,3},{3,4},{4,5},{5,6},{6,7},{7,0},{8,9},{9,10},{10,1... | collective-permute-start | bytes 786440 | tf_op jit(solution)/shard_map/ppermute | solution.py:154
  61.0 0.7 copy-start.16
  61.8 18.2 %collective-permute-start.6 = (bf16[4,2,64,256]{3,2,1,0:T(8,128)(2,1)}, bf16[4,2,64,256]{3,2,1,0:T(8,128)(2,1)}, u32[]{:S(2)}, u32[]{:S(2)}) collective-permute-start(bf16[4,2,64,256]{3,2,1,0:T(8,128)(2,1)} %collective-permute-done.4.refs_4_), channel_id=1, source_target_pairs={{0,7},{1,0},{2,1},{3,2},{4,3},{5,4},{6,5},{7,6},{8,15},{9,8},{10,9... | collective-permute-start | bytes 786440 | tf_op jit(solution)/shard_map/ppermute | solution.py:158
  66.9 13.1 %collective-permute-start.14 = (bf16[4,2,64,256]{3,2,1,0:T(8,128)(2,1)}, bf16[4,2,64,256]{3,2,1,0:T(8,128)(2,1)}, u32[]{:S(2)}, u32[]{:S(2)}) collective-permute-start(bf16[4,2,64,256]{3,2,1,0:T(8,128)(2,1)} %collective-permute-done.12.refs_12_), channel_id=1, source_target_pairs={{0,7},{1,0},{2,1},{3,2},{4,3},{5,4},{6,5},{7,6},{8,15},{9,8},{10,9... | collective-permute-start | bytes 786440 | tf_op jit(solution)/shard_map/ppermute | solution.py:158
  70.9 9.8 %collective-permute-start.7 = (bf16[4,2,64,256]{3,2,1,0:T(8,128)(2,1)}, bf16[4,2,64,256]{3,2,1,0:T(8,128)(2,1)}, u32[]{:S(2)}, u32[]{:S(2)}) collective-permute-start(bf16[4,2,64,256]{3,2,1,0:T(8,128)(2,1)} %collective-permute-done.5.refs_5_), channel_id=1, source_target_pairs={{0,1},{1,2},{2,3},{3,4},{4,5},{5,6},{6,7},{7,0},{8,9},{9,10},{10,1... | collective-permute-start | bytes 786440 | tf_op jit(solution)/shard_map/ppermute | solution.py:154
  72.8 10.7 %collective-permute-start.15 = (bf16[4,2,64,256]{3,2,1,0:T(8,128)(2,1)}, bf16[4,2,64,256]{3,2,1,0:T(8,128)(2,1)}, u32[]{:S(2)}, u32[]{:S(2)}) collective-permute-start(bf16[4,2,64,256]{3,2,1,0:T(8,128)(2,1)} %collective-permute-done.13.refs_13_), channel_id=1, source_target_pairs={{0,1},{1,2},{2,3},{3,4},{4,5},{5,6},{6,7},{7,0},{8,9},{9,10},{10,1... | collective-permute-start | bytes 786440 | tf_op jit(solution)/shard_map/ppermute | solution.py:154
  83.5 1.0 copy-start.5
  84.4 0.9 copy-start.7
  85.4 0.9 copy-start.9
  86.3 0.9 copy-start.11
  87.3 0.9 copy-start.13
  88.2 0.9 copy-start.15
  89.2 0.9 copy-start.17
  94.4 2.0 %copy-start.1 = (bf16[4,1024,512]{2,1,0:T(8,128)(2,1)}, bf16[4,1024,512]{2,1,0:T(8,128)(2,1)S(1)}, u32[]{:S(2)}) copy-start(bf16[4,1024,512]{2,1,0:T(8,128)(2,1)S(1)} %get-tuple-element.7.first_ref) | copy-start | bytes 12582916
  96.4 1.9 %copy-start.2 = (bf16[4,2,1024,256]{3,2,1,0:T(8,128)(2,1)}, bf16[4,2,1024,256]{3,2,1,0:T(8,128)(2,1)S(1)}, u32[]{:S(2)}) copy-start(bf16[4,2,1024,256]{3,2,1,0:T(8,128)(2,1)S(1)} %get-tuple-element.8.last_ref) | copy-start | bytes 12582916
Sparse Core Ops, SparseCore 0:
  18.0 59.0 all-gather.1

commit v2 on v1

v2 whole, which is shorter than its diff:
```python
import jax
import jax.numpy as jnp
from jax import lax
from jax.experimental import pallas as pl
from jax.experimental.pallas import tpu as pltpu
from jax.sharding import Mesh, PartitionSpec as P

N_Y = 8
N_TEST = 16
IMG_DEV = 4
PIX = 28
SLOT = 32
SURV = 14
MUT_DEV = 4
STEPS = 2
C = 1024
B = 256
CHUNK = C // N_TEST
ROWS = SURV * SLOT
OFFSETS = (0, -1, -2, -3, 1, 2, 3, 4)


def in_hbm(value):
    return pltpu.with_memory_space_constraint(value, pltpu.HBM)


def build_weights(strength_ref, first_base_ref, last_base_ref, *refs):
    whole = refs[: N_TEST - 2]
    halves = refs[N_TEST - 2 : N_TEST + 2]
    first_ref, last_ref = refs[N_TEST + 2 :]
    member = pl.program_id(0)
    my_xh = lax.axis_index("xh")
    my_y = lax.axis_index("y")
    for number in range(N_TEST):
        plane = my_xh if number % 2 == 0 else 1 - my_xh
        origin = plane * N_Y + (my_y + OFFSETS[number // 2]) % N_Y
        row = pl.multiple_of(origin * CHUNK, CHUNK)
        for kind, base_ref in enumerate((first_base_ref, last_base_ref)):
            base = base_ref[pl.ds(row, CHUNK), :].astype(jnp.float32)
            if number < N_TEST - 2:
                change = whole[number][0, kind]
            else:
                low, high = halves[(number % 2) * 2 : (number % 2) * 2 + 2]
                change = jnp.where(member < MUT_DEV // 2, low[0, kind], high[0, kind])
            change = change.astype(jnp.float32)
            for step in range(STEPS):
                value = (base + strength_ref[step, member] * change).astype(jnp.bfloat16)
                if kind == 0:
                    first_ref[0, pl.ds(row, CHUNK), step * B : (step + 1) * B] = value
                else:
                    last_ref[0, step, pl.ds(row, CHUNK), :] = value


def score(
    wanted_ref,
    class_ref,
    images_ref,
    first_ref,
    last_ref,
    readout_hbm_ref,
    out_ref,
    x_ref,
    pooled_ref,
    keep_ref,
    label_ref,
    readout_ref,
    image_sem,
    readout_sem,
):
    member = pl.program_id(0)

    @pl.when(member == 0)
    def _():
        my_xl = lax.axis_index("xl")
        shard = lax.axis_index("xh") * N_Y + lax.axis_index("y")
        sublane = lax.broadcasted_iota(jnp.int32, (8, 128), 0)
        for variant in range(MUT_DEV):
            for entry in range(SURV):
                wanted = wanted_ref[variant, entry]
                holder = wanted // IMG_DEV
                within = wanted % IMG_DEV
                slot = jnp.where(holder // 16 != my_xl, 1, 0)
                start = (
                    ((holder % 16) * 2 + slot) * (IMG_DEV * PIX)
                    + (within // 2) * (2 * PIX)
                    + (within % 2) * 24
                )
                pltpu.make_async_copy(
                    images_ref.at[pl.ds(pl.multiple_of(start, 8), SLOT)],
                    x_ref.at[variant, pl.ds(entry * SLOT, SLOT)],
                    image_sem.at[variant],
                ).start()
        pltpu.make_async_copy(readout_hbm_ref, readout_ref, readout_sem).start()
        pooled_ref[...] = jnp.zeros_like(pooled_ref)
        label_ref[...] = jnp.zeros_like(label_ref)
        for variant in range(MUT_DEV):
            for entry in range(SURV):
                wanted = wanted_ref[variant, entry]
                holder = wanted // IMG_DEV
                within = wanted % IMG_DEV
                odd = within % 2
                keep_ref[variant, 0, entry] = jnp.where(sublane >= odd * 4, 1.0, 0.0)
                keep_ref[variant, 1, entry] = jnp.where(sublane < 4 + odd * 4, 1.0, 0.0)
                label = class_ref[(holder * N_TEST + shard) * IMG_DEV + within]
                for step in range(STEPS):
                    row = (variant * STEPS + step) * 16 + entry
                    label_ref[row : row + 1, :] = jnp.full((1, 128), label, jnp.int32)

    pltpu.make_async_copy(
        images_ref.at[pl.ds(0, ROWS)], x_ref.at[member], image_sem.at[member]
    ).wait()
    rows = x_ref[member]
    hidden = jnp.maximum(
        jnp.dot(rows, first_ref[0], preferred_element_type=jnp.float32), 0.0
    ).astype(jnp.bfloat16)
    for step in range(STEPS):
        expanded = lax.dot_general(
            hidden[:, step * B : (step + 1) * B],
            last_ref[0, step],
            (((1,), (1,)), ((), ())),
            preferred_element_type=jnp.float32,
        )
        out_rows = jnp.maximum(expanded + rows.astype(jnp.float32), 0.0)
        tiles = out_rows.reshape(SURV, SLOT // 8, 8, C)
        total = (
            tiles[:, 0] * keep_ref[member, 0][:, :, :1]
            + tiles[:, 1]
            + tiles[:, 2]
            + tiles[:, 3] * keep_ref[member, 1][:, :, :1]
        )
        pooled = (jnp.sum(total, axis=1) / PIX).astype(jnp.bfloat16)
        pooled_ref[member * STEPS + step, :SURV, :] = pooled

    @pl.when(member == MUT_DEV - 1)
    def _():
        pltpu.make_async_copy(readout_hbm_ref, readout_ref, readout_sem).wait()
        logits = lax.dot_general(
            pooled_ref[...].reshape(MUT_DEV * STEPS * 16, C),
            readout_ref[...],
            (((1,), (1,)), ((), ())),
            preferred_element_type=jnp.float32,
        )
        top = jnp.max(logits, axis=1, keepdims=True)
        total = top + jnp.log(jnp.sum(jnp.exp(logits - top), axis=1, keepdims=True))
        column = lax.broadcasted_iota(jnp.int32, logits.shape, 1)
        chosen = jnp.sum(
            jnp.where(column == label_ref[:, :1], logits, 0.0), axis=1, keepdims=True
        )
        kill = total - chosen
        shape = (MUT_DEV * STEPS * 16, 128)
        diagonal = lax.broadcasted_iota(jnp.int32, shape, 1) == (
            lax.broadcasted_iota(jnp.int32, shape, 0) % 16
        )
        spread = jnp.where(diagonal, jnp.broadcast_to(kill, shape), 0.0)
        lined = jnp.sum(spread.reshape(MUT_DEV * STEPS, 16, 128), axis=1)
        for variant in range(MUT_DEV):
            out_ref[variant] = lined[variant * STEPS : (variant + 1) * STEPS, :SURV]


def on_device(
    input_activation,
    ground_truth_class,
    remaining_pictures,
    learned_narrowing_kernel,
    learned_widening_kernel,
    narrowing_perturbation,
    widening_perturbation,
    perturbation_strength,
    readout_matrix,
):
    swap = [(0, 1), (1, 0)]
    up = [(i, (i + 1) % N_Y) for i in range(N_Y)]
    down = [(i, (i - 1) % N_Y) for i in range(N_Y)]

    own_rows = input_activation.reshape(IMG_DEV * PIX, C)
    message = jnp.stack(
        [narrowing_perturbation, jnp.transpose(widening_perturbation, (0, 2, 1))], axis=1
    )
    own_rows, message = lax.optimization_barrier((own_rows, message))
    partner_rows = lax.ppermute(own_rows, "xl", swap)
    first_up = lax.ppermute(message, "y", up)
    partner_rows, first_up = lax.optimization_barrier((partner_rows, first_up))
    images = lax.all_gather(
        jnp.concatenate([own_rows, partner_rows]), ("z", "core"), axis=0, tiled=True
    )

    other = lax.ppermute(message, "xh", swap)
    flows = []
    for seed in (message, other):
        rising = [first_up if seed is message else lax.ppermute(seed, "y", up)]
        falling = [lax.ppermute(seed, "y", down)]
        for _ in range(2):
            rising.append(lax.ppermute(rising[-1], "y", up))
            falling.append(lax.ppermute(falling[-1], "y", down))
        half = MUT_DEV // 2
        low = lax.ppermute(rising[-1][:half], "y", up)
        high = lax.ppermute(falling[-1][half:], "y", down)
        flows.append(([seed] + rising + falling, [low, high]))
    pieces = [flows[number % 2][0][number // 2] for number in range(N_TEST - 2)]
    pieces += flows[0][1] + flows[1][1]

    smem = pl.BlockSpec(memory_space=pltpu.SMEM)
    hbm = pl.BlockSpec(memory_space=pl.ANY)
    piece = (1, 2, CHUNK, B)
    whole_spec = pl.BlockSpec(piece, lambda m: (m, 0, 0, 0))
    low_spec = pl.BlockSpec(piece, lambda m: (jnp.minimum(m, MUT_DEV // 2 - 1), 0, 0, 0))
    high_spec = pl.BlockSpec(piece, lambda m: (jnp.maximum(m - MUT_DEV // 2, 0), 0, 0, 0))
    first_spec = pl.BlockSpec((1, C, STEPS * B), lambda m: (m, 0, 0))
    last_spec = pl.BlockSpec((1, STEPS, C, B), lambda m: (m, 0, 0, 0))
    base_spec = pl.BlockSpec((C, B), lambda m: (0, 0))
    first_all, last_all = pl.pallas_call(
        build_weights,
        grid=(MUT_DEV,),
        in_specs=[smem, base_spec, base_spec]
        + [whole_spec] * (N_TEST - 2)
        + [low_spec, high_spec] * 2,
        out_specs=[first_spec, last_spec],
        out_shape=[
            pltpu.HBM((MUT_DEV, C, STEPS * B), jnp.bfloat16),
            pltpu.HBM((MUT_DEV, STEPS, C, B), jnp.bfloat16),
        ],
        compiler_params=pltpu.CompilerParams(vmem_limit_bytes=14 * 2**20),
    )(
        perturbation_strength.T,
        in_hbm(learned_narrowing_kernel),
        learned_widening_kernel.T,
        *[in_hbm(value) for value in pieces],
    )

    return pl.pallas_call(
        score,
        grid=(MUT_DEV,),
        in_specs=[smem, smem, hbm, first_spec, last_spec, hbm],
        out_specs=pl.BlockSpec((MUT_DEV, STEPS, SURV), lambda m: (0, 0, 0)),
        out_shape=jax.ShapeDtypeStruct((MUT_DEV, STEPS, SURV), jnp.float32),
        scratch_shapes=[
            pltpu.VMEM((MUT_DEV, ROWS, C), jnp.bfloat16),
            pltpu.VMEM((MUT_DEV * STEPS, 16, C), jnp.bfloat16),
            pltpu.VMEM((MUT_DEV, 2, SURV, 8, 128), jnp.float32),
            pltpu.VMEM((MUT_DEV * STEPS * 16, 128), jnp.int32),
            pltpu.VMEM((readout_matrix.shape[1], C), jnp.bfloat16),
            pltpu.SemaphoreType.DMA((MUT_DEV,)),
            pltpu.SemaphoreType.DMA,
        ],
        compiler_params=pltpu.CompilerParams(vmem_limit_bytes=26 * 2**20),
    )(
        remaining_pictures,
        ground_truth_class,
        in_hbm(images),
        in_hbm(first_all),
        in_hbm(last_all),
        in_hbm(readout_matrix.T),
    )


def solution(mesh):
    fine = Mesh(mesh.devices.reshape(2, 8, 2, 2, N_Y), ("xl", "z", "core", "xh", "y"))
    mut = ("xl", "z", "core")
    test = ("xh", "y")
    return jax.shard_map(
        on_device,
        mesh=fine,
        in_specs=(
            P(mut + test, None, None),
            P(),
            P(mut, test),
            P(),
            P(),
            P(mut, test, None),
            P(mut, None, test),
            P(mut, None),
            P(),
        ),
        out_specs=P(mut, None, test),
        check_vma=False,
    )
```

time: 118 us -> 116 us (0.983)
  the two profiles are of different devices: /device:TPU:4 before, /device:TPU:56 now
where the time goes in v2:
time: 116 us; the launch traced here: 115 us
  starting transfers between devices  60 us (52%)
  Pallas kernels  17.9 us (15%)
  waiting for transfers between devices  17.2 us (15%)
  between operations  13.9 us (12%)
  local copies, waits for them, and re-layouts  4.3 us (4%)
  other arithmetic  1.85 us (2%)
    ppermute x4, starting transfers between devices, on_device(): rising.append(lax.ppermute(rising[-1], 'y', up))  17.8 us
    pallas_call x1, Pallas kernels, on_device(): pl.pallas_call(score, grid=(MUT_DEV,), in_specs=[smem, smem, hbm, first_s...  10.7 us
    ppermute x2, starting transfers between devices, on_device(): low = lax.ppermute(rising[-1][:half], 'y', up)  10.3 us
    ppermute x4, starting transfers between devices, on_device(): falling.append(lax.ppermute(falling[-1], 'y', down))  8.47 us
    ppermute x1, starting transfers between devices, on_device(): first_up = lax.ppermute(message, 'y', up)  7.18 us
    pallas_call x1, Pallas kernels, on_device(): pl.pallas_call(build_weights, grid=(MUT_DEV,), in_specs=[smem, base_spec,...  7.17 us
    ppermute x2, starting transfers between devices, on_device(): falling = [lax.ppermute(seed, 'y', down)]  6.77 us
    ppermute x2, waiting for transfers between devices, on_device(): high = lax.ppermute(falling[-1][half:], 'y', down)  6.2 us
  transfers between devices with their start and end apart: 19, of which 3 were waited for; matrix products, arithmetic and copies ran while one was open for 3% of the time, Pallas kernels for 6%

profile of v2, /device:TPU:56, one launch (start us, length us, event | category | flops | bytes accessed | tf_op | source)
XLA Modules:
  0.0 115.2 jit_solution(17129419953462825281)
XLA Ops:
  6.5 1.1 copy.12
  7.7 1.0 pad_maximum_fusion.1.refs_0_
  8.7 0.0 copy-start
  8.7 0.0 copy-start.1
  8.7 7.2 %collective-permute-start.1 = (bf16[4,2,64,256]{3,2,1,0:T(8,128)(2,1)S(1)}, bf16[4,2,64,256]{3,2,1,0:T(8,128)(2,1)S(1)}, u32[]{:S(2)}, u32[]{:S(2)}) collective-permute-start(bf16[4,2,64,256]{3,2,1,0:T(8,128)(2,1)S(1)} %pad_maximum_fusion.1.refs_0_), channel_id=1, source_target_pairs={{0,1},{1,2},{2,3},{3,4},{4,5},{5,6},{6,7},{7,0},{8,9},{9,10},{10,1... | collective-permute-start | bytes 786440 | tf_op jit(solution)/shard_map/ppermute | solution.py:181
  15.9 1.9 %collective-permute-start = (bf16[112,1024]{1,0:T(8,128)(2,1)S(1)}, bf16[112,1024]{1,0:T(8,128)(2,1)S(1)}, u32[]{:S(2)}, u32[]{:S(2)}) collective-permute-start(bf16[112,1024]{1,0:T(8,128)(2,1)S(1)} %reshape.3), channel_id=1, source_target_pairs={{0,256},{256,0},{1,257},{257,1},{2,258},{258,2},{3,259},{259,3},{4... | collective-permute-start | bytes 688136 | tf_op jit(solution)/shard_map/ppermute | solution.py:180
  17.8 6.0 %collective-permute-done = bf16[112,1024]{1,0:T(8,128)(2,1)S(1)} collective-permute-done((bf16[112,1024]{1,0:T(8,128)(2,1)S(1)}, bf16[112,1024]{1,0:T(8,128)(2,1)S(1)}, u32[]{:S(2)}, u32[]{:S(2)}) %collective-permute-start) | collective-permute-done | bytes 229408 | tf_op jit(solution)/shard_map/ppermute | solution.py:180
  23.8 0.0 collective-permute-done.1.refs_2_
  23.8 0.9 pad_maximum_fusion
  24.7 0.0 all-gather.2.cloned.1.call-update
  24.7 1.9 %collective-permute-start.2 = (bf16[4,2,64,256]{3,2,1,0:T(8,128)(2,1)S(1)}, bf16[4,2,64,256]{3,2,1,0:T(8,128)(2,1)S(1)}, u32[]{:S(2)}, u32[]{:S(2)}) collective-permute-start(bf16[4,2,64,256]{3,2,1,0:T(8,128)(2,1)S(1)} %pad_maximum_fusion.1.refs_0_), channel_id=1, source_target_pairs={{0,8},{8,0},{1,9},{9,1},{2,10},{10,2},{3,11},{11,3},{4,12},{12,4},... | collective-permute-start | bytes 786440 | tf_op jit(solution)/shard_map/ppermute | solution.py:187
  26.6 2.8 %collective-permute-start.8 = (bf16[4,2,64,256]{3,2,1,0:T(8,128)(2,1)S(1)}, bf16[4,2,64,256]{3,2,1,0:T(8,128)(2,1)S(1)}, u32[]{:S(2)}, u32[]{:S(2)}) collective-permute-start(bf16[4,2,64,256]{3,2,1,0:T(8,128)(2,1)S(1)} %pad_maximum_fusion.1.refs_0_), channel_id=1, source_target_pairs={{0,7},{1,0},{2,1},{3,2},{4,3},{5,4},{6,5},{7,6},{8,15},{9,8},{10,9... | collective-permute-start | bytes 786440 | tf_op jit(solution)/shard_map/ppermute | solution.py:191
  29.5 5.0 %collective-permute-done.2.refs_1_ = bf16[4,2,64,256]{3,2,1,0:T(8,128)(2,1)S(1)} collective-permute-done((bf16[4,2,64,256]{3,2,1,0:T(8,128)(2,1)S(1)}, bf16[4,2,64,256]{3,2,1,0:T(8,128)(2,1)S(1)}, u32[]{:S(2)}, u32[]{:S(2)}) %collective-permute-start.2) | collective-permute-done | bytes 262176 | tf_op jit(solution)/shard_map/ppermute | solution.py:187
  34.5 1.9 %collective-permute-start.3 = (bf16[4,2,64,256]{3,2,1,0:T(8,128)(2,1)S(1)}, bf16[4,2,64,256]{3,2,1,0:T(8,128)(2,1)S(1)}, u32[]{:S(2)}, u32[]{:S(2)}) collective-permute-start(bf16[4,2,64,256]{3,2,1,0:T(8,128)(2,1)S(1)} %collective-permute-done.2.refs_1_), channel_id=1, source_target_pairs={{0,1},{1,2},{2,3},{3,4},{4,5},{5,6},{6,7},{7,0},{8,9},{9,10},{10,1... | collective-permute-start | bytes 786440 | tf_op jit(solution)/shard_map/ppermute | solution.py:190
  36.4 3.9 %collective-permute-start.9 = (bf16[4,2,64,256]{3,2,1,0:T(8,128)(2,1)S(1)}, bf16[4,2,64,256]{3,2,1,0:T(8,128)(2,1)S(1)}, u32[]{:S(2)}, u32[]{:S(2)}) collective-permute-start(bf16[4,2,64,256]{3,2,1,0:T(8,128)(2,1)S(1)} %collective-permute-done.2.refs_1_), channel_id=1, source_target_pairs={{0,7},{1,0},{2,1},{3,2},{4,3},{5,4},{6,5},{7,6},{8,15},{9,8},{10,9... | collective-permute-start | bytes 786440 | tf_op jit(solution)/shard_map/ppermute | solution.py:191
  40.3 3.1 %collective-permute-start.4 = (bf16[4,2,64,256]{3,2,1,0:T(8,128)(2,1)S(1)}, bf16[4,2,64,256]{3,2,1,0:T(8,128)(2,1)S(1)}, u32[]{:S(2)}, u32[]{:S(2)}) collective-permute-start(bf16[4,2,64,256]{3,2,1,0:T(8,128)(2,1)S(1)} %collective-permute-done.1.refs_2_), channel_id=1, source_target_pairs={{0,1},{1,2},{2,3},{3,4},{4,5},{5,6},{6,7},{7,0},{8,9},{9,10},{10,1... | collective-permute-start | bytes 786440 | tf_op jit(solution)/shard_map/ppermute | solution.py:193
  43.5 0.0 collective-permute-done.8.refs_8_
  43.5 0.0 copy-start.11
  43.5 2.7 %collective-permute-start.10 = (bf16[4,2,64,256]{3,2,1,0:T(8,128)(2,1)S(1)}, bf16[4,2,64,256]{3,2,1,0:T(8,128)(2,1)S(1)}, u32[]{:S(2)}, u32[]{:S(2)}) collective-permute-start(bf16[4,2,64,256]{3,2,1,0:T(8,128)(2,1)S(1)} %collective-permute-done.8.refs_8_), channel_id=1, source_target_pairs={{0,7},{1,0},{2,1},{3,2},{4,3},{5,4},{6,5},{7,6},{8,15},{9,8},{10,9... | collective-permute-start | bytes 786440 | tf_op jit(solution)/shard_map/ppermute | solution.py:194
  46.2 0.0 collective-permute-done.3.refs_3_
  46.2 0.0 copy-start.12
  46.2 4.4 %collective-permute-start.5 = (bf16[4,2,64,256]{3,2,1,0:T(8,128)(2,1)S(1)}, bf16[4,2,64,256]{3,2,1,0:T(8,128)(2,1)S(1)}, u32[]{:S(2)}, u32[]{:S(2)}) collective-permute-start(bf16[4,2,64,256]{3,2,1,0:T(8,128)(2,1)S(1)} %collective-permute-done.3.refs_3_), channel_id=1, source_target_pairs={{0,1},{1,2},{2,3},{3,4},{4,5},{5,6},{6,7},{7,0},{8,9},{9,10},{10,1... | collective-permute-start | bytes 786440 | tf_op jit(solution)/shard_map/ppermute | solution.py:193
  50.6 0.0 collective-permute-done.9.refs_9_
  50.6 1.9 %collective-permute-start.11 = (bf16[4,2,64,256]{3,2,1,0:T(8,128)(2,1)S(1)}, bf16[4,2,64,256]{3,2,1,0:T(8,128)(2,1)S(1)}, u32[]{:S(2)}, u32[]{:S(2)}) collective-permute-start(bf16[4,2,64,256]{3,2,1,0:T(8,128)(2,1)S(1)} %collective-permute-done.9.refs_9_), channel_id=1, source_target_pairs={{0,7},{1,0},{2,1},{3,2},{4,3},{5,4},{6,5},{7,6},{8,15},{9,8},{10,9... | collective-permute-start | bytes 786440 | tf_op jit(solution)/shard_map/ppermute | solution.py:194
  52.5 0.0 collective-permute-done.4.refs_4_
  52.5 0.0 copy-start.14
  52.5 5.1 %collective-permute-start.6 = (bf16[4,2,64,256]{3,2,1,0:T(8,128)(2,1)S(1)}, bf16[4,2,64,256]{3,2,1,0:T(8,128)(2,1)S(1)}, u32[]{:S(2)}, u32[]{:S(2)}) collective-permute-start(bf16[4,2,64,256]{3,2,1,0:T(8,128)(2,1)S(1)} %collective-permute-done.4.refs_4_), channel_id=1, source_target_pairs={{0,1},{1,2},{2,3},{3,4},{4,5},{5,6},{6,7},{7,0},{8,9},{9,10},{10,1... | collective-permute-start | bytes 786440 | tf_op jit(solution)/shard_map/ppermute | solution.py:193
  57.7 0.0 collective-permute-done.10.refs_10_
  57.7 1.9 %collective-permute-start.12 = (bf16[4,2,64,256]{3,2,1,0:T(8,128)(2,1)S(1)}, bf16[4,2,64,256]{3,2,1,0:T(8,128)(2,1)S(1)}, u32[]{:S(2)}, u32[]{:S(2)}) collective-permute-start(bf16[4,2,64,256]{3,2,1,0:T(8,128)(2,1)S(1)} %collective-permute-done.10.refs_10_), channel_id=1, source_target_pairs={{0,7},{1,0},{2,1},{3,2},{4,3},{5,4},{6,5},{7,6},{8,15},{9,8},{10,9... | collective-permute-start | bytes 786440 | tf_op jit(solution)/shard_map/ppermute | solution.py:194
  59.6 0.0 collective-permute-done.5.refs_5_
  59.6 0.0 copy-start.16
  59.7 5.1 %collective-permute-start.7 = (bf16[4,2,64,256]{3,2,1,0:T(8,128)(2,1)S(1)}, bf16[4,2,64,256]{3,2,1,0:T(8,128)(2,1)S(1)}, u32[]{:S(2)}, u32[]{:S(2)}) collective-permute-start(bf16[4,2,64,256]{3,2,1,0:T(8,128)(2,1)S(1)} %collective-permute-done.5.refs_5_), channel_id=1, source_target_pairs={{0,1},{1,2},{2,3},{3,4},{4,5},{5,6},{6,7},{7,0},{8,9},{9,10},{10,1... | collective-permute-start | bytes 786440 | tf_op jit(solution)/shard_map/ppermute | solution.py:193
  64.8 0.0 collective-permute-done.11.refs_11_
  64.8 1.9 %collective-permute-start.13 = (bf16[4,2,64,256]{3,2,1,0:T(8,128)(2,1)S(1)}, bf16[4,2,64,256]{3,2,1,0:T(8,128)(2,1)S(1)}, u32[]{:S(2)}, u32[]{:S(2)}) collective-permute-start(bf16[4,2,64,256]{3,2,1,0:T(8,128)(2,1)S(1)} %collective-permute-done.11.refs_11_), channel_id=1, source_target_pairs={{0,7},{1,0},{2,1},{3,2},{4,3},{5,4},{6,5},{7,6},{8,15},{9,8},{10,9... | collective-permute-start | bytes 786440 | tf_op jit(solution)/shard_map/ppermute | solution.py:194
  66.8 0.0 collective-permute-done.6.refs_6_
  66.8 0.0 copy-start.4
  66.8 0.7 slice.16
  67.5 5.1 %collective-permute-start.14 = (bf16[2,2,64,256]{3,2,1,0:T(8,128)(2,1)}, bf16[2,2,64,256]{3,2,1,0:T(8,128)(2,1)S(1)}, u32[]{:S(2)}, u32[]{:S(2)}) collective-permute-start(bf16[2,2,64,256]{3,2,1,0:T(8,128)(2,1)} %slice.16), channel_id=1, source_target_pairs={{0,1},{1,2},{2,3},{3,4},{4,5},{5,6},{6,7},{7,0},{8,9},{9,10},{10,1... | collective-permute-start | bytes 393224 | tf_op jit(solution)/shard_map/ppermute | solution.py:196
  72.6 0.0 collective-permute-done.12.refs_12_
  72.7 0.7 slice.17
  73.4 1.9 %collective-permute-start.15 = (bf16[2,2,64,256]{3,2,1,0:T(8,128)(2,1)}, bf16[2,2,64,256]{3,2,1,0:T(8,128)(2,1)}, u32[]{:S(2)}, u32[]{:S(2)}) collective-permute-start(bf16[2,2,64,256]{3,2,1,0:T(8,128)(2,1)} %slice.17), channel_id=1, source_target_pairs={{0,7},{1,0},{2,1},{3,2},{4,3},{5,4},{6,5},{7,6},{8,15},{9,8},{10,9... | collective-permute-start | bytes 393224 | tf_op jit(solution)/shard_map/ppermute | solution.py:197
  75.3 0.0 collective-permute-done.7.refs_7_
  75.3 0.7 slice.18
  76.1 5.1 %collective-permute-start.16 = (bf16[2,2,64,256]{3,2,1,0:T(8,128)(2,1)}, bf16[2,2,64,256]{3,2,1,0:T(8,128)(2,1)}, u32[]{:S(2)}, u32[]{:S(2)}) collective-permute-start(bf16[2,2,64,256]{3,2,1,0:T(8,128)(2,1)} %slice.18), channel_id=1, source_target_pairs={{0,1},{1,2},{2,3},{3,4},{4,5},{5,6},{6,7},{7,0},{8,9},{9,10},{10,1... | collective-permute-start | bytes 393224 | tf_op jit(solution)/shard_map/ppermute | solution.py:196
  81.2 0.0 collective-permute-done.13.refs_13_
  81.2 0.0 copy-start.7
  81.2 0.7 slice.19
  81.9 1.9 %collective-permute-start.17 = (bf16[2,2,64,256]{3,2,1,0:T(8,128)(2,1)}, bf16[2,2,64,256]{3,2,1,0:T(8,128)(2,1)}, u32[]{:S(2)}, u32[]{:S(2)}) collective-permute-start(bf16[2,2,64,256]{3,2,1,0:T(8,128)(2,1)} %slice.19), channel_id=1, source_target_pairs={{0,7},{1,0},{2,1},{3,2},{4,3},{5,4},{6,5},{7,6},{8,15},{9,8},{10,9... | collective-permute-start | bytes 393224 | tf_op jit(solution)/shard_map/ppermute | solution.py:197
  83.9 0.2 copy.13
  84.1 0.0 collective-permute-done.14.refs_14_
  84.1 0.0 collective-permute-done.15.refs_15_
  84.1 0.0 collective-permute-done.16.refs_16_
  84.1 6.2 %collective-permute-done.17.refs_17_ = bf16[2,2,64,256]{3,2,1,0:T(8,128)(2,1)} collective-permute-done((bf16[2,2,64,256]{3,2,1,0:T(8,128)(2,1)}, bf16[2,2,64,256]{3,2,1,0:T(8,128)(2,1)}, u32[]{:S(2)}, u32[]{:S(2)}) %collective-permute-start.17) | collective-permute-done | bytes 131104 | tf_op jit(solution)/shard_map/ppermute | solution.py:197
  90.3 0.0 copy-done.10
  90.3 0.0 copy-done.11
  90.3 0.0 copy-done.12
  90.4 0.0 copy-done.4
  90.4 0.0 copy-done.5
  90.4 0.0 copy-done.6
  90.4 0.0 copy-done.7
  90.4 0.0 copy-done.18
  90.4 7.2 %shard_map.91 = (bf16[4,1024,512]{2,1,0:T(8,128)(2,1)}, bf16[4,2,1024,256]{3,2,1,0:T(8,128)(2,1)}) custom-call(f32[2,4]{1,0:T(2,128)S(1)} %bitcast.8, bf16[1024,256]{1,0:T(8,128)(2,1)} %first_base_ref.1, bf16[1024,256]{1,0:T(8,128)(2,1)S(1)} %bitcast.7, bf16[4,2,64,256]{3,2,1,0:T(8,128)(2,1)} %copy-done.3, bf16[4,2,64,256]{3,2,1,0:T(8,128)(2,1)} %copy-done.10, ...), custom_call_target="tpu_custom_call" | custom-call | tf_op jit(solution)/shard_map/pallas_call | solution.py:211
  97.6 0.0 all-gather.2.cloned.1.call-done.images_ref
  97.6 10.7 %shard_map.92 = f32[4,2,14]{2,1,0:T(2,128)} custom-call(s32[4,14]{1,0:T(4,128)S(1)} %copy-done.1, s32[2048]{0:T(1024)S(1)} %copy-done, bf16[3584,1024]{1,0:T(8,128)(2,1)} %all-gather.2.cloned.1.call-done.images_ref, bf16[4,1024,512]{2,1,0:T(8,128)(2,1)} %get-tuple-element.15.first_ref, bf16[4,2,1024,256]{3,2,1,0:T(8,128)(2,1)} %get-tuple-element.16.last_ref, ...), custom_call_target="tpu_custom_call" | custom-call | tf_op jit(solution)/shard_map/pallas_call | solution.py:230
  (24 shorter events, 0.1 us)
Async XLA Ops:
  6.5 77.3 %copy-start.8 = (bf16[256,1024]{1,0:T(8,128)(2,1)S(1)}, bf16[256,1024]{1,0:T(8,128)(2,1)}, u32[]{:S(2)}) copy-start(bf16[256,1024]{1,0:T(8,128)(2,1)} %param.13) | copy-start | bytes 1572868
  6.5 83.9 %copy-start.2 = (f32[4,2]{0,1:T(2,128)S(1)}, f32[4,2]{0,1:T(2,128)}, u32[]{:S(2)}) copy-start(f32[4,2]{0,1:T(2,128)} %param.16) | copy-start | bytes 100
  6.5 91.1 %all-gather.2.cloned.1.call-start = ((), (), s32[]{:S(2)}) async-start(), calls=%async_computation | async-start | bytes 7798784 | tf_op jit(solution)/shard_map/all_gather | solution.py:183
  8.7 81.7 %copy-start.3 = (bf16[4,2,64,256]{3,2,1,0:T(8,128)(2,1)}, bf16[4,2,64,256]{3,2,1,0:T(8,128)(2,1)S(1)}, u32[]{:S(2)}) copy-start(bf16[4,2,64,256]{3,2,1,0:T(8,128)(2,1)S(1)} %pad_maximum_fusion.1.refs_0_) | copy-start | bytes 786436
  8.7 88.9 %copy-start = (s32[2048]{0:T(1024)S(1)}, s32[2048]{0:T(1024)}, u32[]{:S(2)}) copy-start(s32[2048]{0:T(1024)} %class_ref.1) | copy-start | bytes 24580
  8.7 88.9 %copy-start.1 = (s32[4,14]{1,0:T(4,128)S(1)}, s32[4,14]{1,0:T(4,128)}, u32[]{:S(2)}) copy-start(s32[4,14]{1,0:T(4,128)} %wanted_ref.1) | copy-start | bytes 676
  8.7 15.1 %collective-permute-start.1 = (bf16[4,2,64,256]{3,2,1,0:T(8,128)(2,1)S(1)}, bf16[4,2,64,256]{3,2,1,0:T(8,128)(2,1)S(1)}, u32[]{:S(2)}, u32[]{:S(2)}) collective-permute-start(bf16[4,2,64,256]{3,2,1,0:T(8,128)(2,1)S(1)} %pad_maximum_fusion.1.refs_0_), channel_id=1, source_target_pairs={{0,1},{1,2},{2,3},{3,4},{4,5},{5,6},{6,7},{7,0},{8,9},{9,10},{10,1... | collective-permute-start | bytes 786440 | tf_op jit(solution)/shard_map/ppermute | solution.py:181
  15.9 7.9 %collective-permute-start = (bf16[112,1024]{1,0:T(8,128)(2,1)S(1)}, bf16[112,1024]{1,0:T(8,128)(2,1)S(1)}, u32[]{:S(2)}, u32[]{:S(2)}) collective-permute-start(bf16[112,1024]{1,0:T(8,128)(2,1)S(1)} %reshape.3), channel_id=1, source_target_pairs={{0,256},{256,0},{1,257},{257,1},{2,258},{258,2},{3,259},{259,3},{4... | collective-permute-start | bytes 688136 | tf_op jit(solution)/shard_map/ppermute | solution.py:180
  23.8 66.5 %copy-start.9 = (bf16[4,2,64,256]{3,2,1,0:T(8,128)(2,1)}, bf16[4,2,64,256]{3,2,1,0:T(8,128)(2,1)S(1)}, u32[]{:S(2)}) copy-start(bf16[4,2,64,256]{3,2,1,0:T(8,128)(2,1)S(1)} %collective-permute-done.1.refs_2_) | copy-start | bytes 786436
  24.7 9.8 %collective-permute-start.2 = (bf16[4,2,64,256]{3,2,1,0:T(8,128)(2,1)S(1)}, bf16[4,2,64,256]{3,2,1,0:T(8,128)(2,1)S(1)}, u32[]{:S(2)}, u32[]{:S(2)}) collective-permute-start(bf16[4,2,64,256]{3,2,1,0:T(8,128)(2,1)S(1)} %pad_maximum_fusion.1.refs_0_), channel_id=1, source_target_pairs={{0,8},{8,0},{1,9},{9,1},{2,10},{10,2},{3,11},{11,3},{4,12},{12,4},... | collective-permute-start | bytes 786440 | tf_op jit(solution)/shard_map/ppermute | solution.py:187
  26.6 16.8 %collective-permute-start.8 = (bf16[4,2,64,256]{3,2,1,0:T(8,128)(2,1)S(1)}, bf16[4,2,64,256]{3,2,1,0:T(8,128)(2,1)S(1)}, u32[]{:S(2)}, u32[]{:S(2)}) collective-permute-start(bf16[4,2,64,256]{3,2,1,0:T(8,128)(2,1)S(1)} %pad_maximum_fusion.1.refs_0_), channel_id=1, source_target_pairs={{0,7},{1,0},{2,1},{3,2},{4,3},{5,4},{6,5},{7,6},{8,15},{9,8},{10,9... | collective-permute-start | bytes 786440 | tf_op jit(solution)/shard_map/ppermute | solution.py:191
  34.5 55.9 %copy-start.10 = (bf16[4,2,64,256]{3,2,1,0:T(8,128)(2,1)}, bf16[4,2,64,256]{3,2,1,0:T(8,128)(2,1)S(1)}, u32[]{:S(2)}) copy-start(bf16[4,2,64,256]{3,2,1,0:T(8,128)(2,1)S(1)} %collective-permute-done.2.refs_1_) | copy-start | bytes 786436
  34.5 11.7 %collective-permute-start.3 = (bf16[4,2,64,256]{3,2,1,0:T(8,128)(2,1)S(1)}, bf16[4,2,64,256]{3,2,1,0:T(8,128)(2,1)S(1)}, u32[]{:S(2)}, u32[]{:S(2)}) collective-permute-start(bf16[4,2,64,256]{3,2,1,0:T(8,128)(2,1)S(1)} %collective-permute-done.2.refs_1_), channel_id=1, source_target_pairs={{0,1},{1,2},{2,3},{3,4},{4,5},{5,6},{6,7},{7,0},{8,9},{9,10},{10,1... | collective-permute-start | bytes 786440 | tf_op jit(solution)/shard_map/ppermute | solution.py:190
  36.4 14.2 %collective-permute-start.9 = (bf16[4,2,64,256]{3,2,1,0:T(8,128)(2,1)S(1)}, bf16[4,2,64,256]{3,2,1,0:T(8,128)(2,1)S(1)}, u32[]{:S(2)}, u32[]{:S(2)}) collective-permute-start(bf16[4,2,64,256]{3,2,1,0:T(8,128)(2,1)S(1)} %collective-permute-done.2.refs_1_), channel_id=1, source_target_pairs={{0,7},{1,0},{2,1},{3,2},{4,3},{5,4},{6,5},{7,6},{8,15},{9,8},{10,9... | collective-permute-start | bytes 786440 | tf_op jit(solution)/shard_map/ppermute | solution.py:191
  40.3 12.2 %collective-permute-start.4 = (bf16[4,2,64,256]{3,2,1,0:T(8,128)(2,1)S(1)}, bf16[4,2,64,256]{3,2,1,0:T(8,128)(2,1)S(1)}, u32[]{:S(2)}, u32[]{:S(2)}) collective-permute-start(bf16[4,2,64,256]{3,2,1,0:T(8,128)(2,1)S(1)} %collective-permute-done.1.refs_2_), channel_id=1, source_target_pairs={{0,1},{1,2},{2,3},{3,4},{4,5},{5,6},{6,7},{7,0},{8,9},{9,10},{10,1... | collective-permute-start | bytes 786440 | tf_op jit(solution)/shard_map/ppermute | solution.py:193
  43.5 46.9 %copy-start.11 = (bf16[4,2,64,256]{3,2,1,0:T(8,128)(2,1)}, bf16[4,2,64,256]{3,2,1,0:T(8,128)(2,1)S(1)}, u32[]{:S(2)}) copy-start(bf16[4,2,64,256]{3,2,1,0:T(8,128)(2,1)S(1)} %collective-permute-done.8.refs_8_) | copy-start | bytes 786436
  43.5 14.2 %collective-permute-start.10 = (bf16[4,2,64,256]{3,2,1,0:T(8,128)(2,1)S(1)}, bf16[4,2,64,256]{3,2,1,0:T(8,128)(2,1)S(1)}, u32[]{:S(2)}, u32[]{:S(2)}) collective-permute-start(bf16[4,2,64,256]{3,2,1,0:T(8,128)(2,1)S(1)} %collective-permute-done.8.refs_8_), channel_id=1, source_target_pairs={{0,7},{1,0},{2,1},{3,2},{4,3},{5,4},{6,5},{7,6},{8,15},{9,8},{10,9... | collective-permute-start | bytes 786440 | tf_op jit(solution)/shard_map/ppermute | solution.py:194
  46.2 44.1 %copy-start.12 = (bf16[4,2,64,256]{3,2,1,0:T(8,128)(2,1)}, bf16[4,2,64,256]{3,2,1,0:T(8,128)(2,1)S(1)}, u32[]{:S(2)}) copy-start(bf16[4,2,64,256]{3,2,1,0:T(8,128)(2,1)S(1)} %collective-permute-done.3.refs_3_) | copy-start | bytes 786436
  46.2 13.4 %collective-permute-start.5 = (bf16[4,2,64,256]{3,2,1,0:T(8,128)(2,1)S(1)}, bf16[4,2,64,256]{3,2,1,0:T(8,128)(2,1)S(1)}, u32[]{:S(2)}, u32[]{:S(2)}) collective-permute-start(bf16[4,2,64,256]{3,2,1,0:T(8,128)(2,1)S(1)} %collective-permute-done.3.refs_3_), channel_id=1, source_target_pairs={{0,1},{1,2},{2,3},{3,4},{4,5},{5,6},{6,7},{7,0},{8,9},{9,10},{10,1... | collective-permute-start | bytes 786440 | tf_op jit(solution)/shard_map/ppermute | solution.py:193
  50.6 14.2 %copy-start.13 = (bf16[4,2,64,256]{3,2,1,0:T(8,128)(2,1)}, bf16[4,2,64,256]{3,2,1,0:T(8,128)(2,1)S(1)}, u32[]{:S(2)}) copy-start(bf16[4,2,64,256]{3,2,1,0:T(8,128)(2,1)S(1)} %collective-permute-done.9.refs_9_) | copy-start | bytes 786436
  50.6 14.2 %collective-permute-start.11 = (bf16[4,2,64,256]{3,2,1,0:T(8,128)(2,1)S(1)}, bf16[4,2,64,256]{3,2,1,0:T(8,128)(2,1)S(1)}, u32[]{:S(2)}, u32[]{:S(2)}) collective-permute-start(bf16[4,2,64,256]{3,2,1,0:T(8,128)(2,1)S(1)} %collective-permute-done.9.refs_9_), channel_id=1, source_target_pairs={{0,7},{1,0},{2,1},{3,2},{4,3},{5,4},{6,5},{7,6},{8,15},{9,8},{10,9... | collective-permute-start | bytes 786440 | tf_op jit(solution)/shard_map/ppermute | solution.py:194
  52.5 12.3 %copy-start.14 = (bf16[4,2,64,256]{3,2,1,0:T(8,128)(2,1)}, bf16[4,2,64,256]{3,2,1,0:T(8,128)(2,1)S(1)}, u32[]{:S(2)}) copy-start(bf16[4,2,64,256]{3,2,1,0:T(8,128)(2,1)S(1)} %collective-permute-done.4.refs_4_) | copy-start | bytes 786436
  52.5 14.2 %collective-permute-start.6 = (bf16[4,2,64,256]{3,2,1,0:T(8,128)(2,1)S(1)}, bf16[4,2,64,256]{3,2,1,0:T(8,128)(2,1)S(1)}, u32[]{:S(2)}, u32[]{:S(2)}) collective-permute-start(bf16[4,2,64,256]{3,2,1,0:T(8,128)(2,1)S(1)} %collective-permute-done.4.refs_4_), channel_id=1, source_target_pairs={{0,1},{1,2},{2,3},{3,4},{4,5},{5,6},{6,7},{7,0},{8,9},{9,10},{10,1... | collective-permute-start | bytes 786440 | tf_op jit(solution)/shard_map/ppermute | solution.py:193
  57.7 24.2 %copy-start.15 = (bf16[4,2,64,256]{3,2,1,0:T(8,128)(2,1)}, bf16[4,2,64,256]{3,2,1,0:T(8,128)(2,1)S(1)}, u32[]{:S(2)}) copy-start(bf16[4,2,64,256]{3,2,1,0:T(8,128)(2,1)S(1)} %collective-permute-done.10.refs_10_) | copy-start | bytes 786436
  57.7 14.9 %collective-permute-start.12 = (bf16[4,2,64,256]{3,2,1,0:T(8,128)(2,1)S(1)}, bf16[4,2,64,256]{3,2,1,0:T(8,128)(2,1)S(1)}, u32[]{:S(2)}, u32[]{:S(2)}) collective-permute-start(bf16[4,2,64,256]{3,2,1,0:T(8,128)(2,1)S(1)} %collective-permute-done.10.refs_10_), channel_id=1, source_target_pairs={{0,7},{1,0},{2,1},{3,2},{4,3},{5,4},{6,5},{7,6},{8,15},{9,8},{10,9... | collective-permute-start | bytes 786440 | tf_op jit(solution)/shard_map/ppermute | solution.py:194
  59.6 22.3 %copy-start.16 = (bf16[4,2,64,256]{3,2,1,0:T(8,128)(2,1)}, bf16[4,2,64,256]{3,2,1,0:T(8,128)(2,1)S(1)}, u32[]{:S(2)}) copy-start(bf16[4,2,64,256]{3,2,1,0:T(8,128)(2,1)S(1)} %collective-permute-done.5.refs_5_) | copy-start | bytes 786436
  59.7 15.7 %collective-permute-start.7 = (bf16[4,2,64,256]{3,2,1,0:T(8,128)(2,1)S(1)}, bf16[4,2,64,256]{3,2,1,0:T(8,128)(2,1)S(1)}, u32[]{:S(2)}, u32[]{:S(2)}) collective-permute-start(bf16[4,2,64,256]{3,2,1,0:T(8,128)(2,1)S(1)} %collective-permute-done.5.refs_5_), channel_id=1, source_target_pairs={{0,1},{1,2},{2,3},{3,4},{4,5},{5,6},{6,7},{7,0},{8,9},{9,10},{10,1... | collective-permute-start | bytes 786440 | tf_op jit(solution)/shard_map/ppermute | solution.py:193
  64.8 17.1 %copy-start.17 = (bf16[4,2,64,256]{3,2,1,0:T(8,128)(2,1)}, bf16[4,2,64,256]{3,2,1,0:T(8,128)(2,1)S(1)}, u32[]{:S(2)}) copy-start(bf16[4,2,64,256]{3,2,1,0:T(8,128)(2,1)S(1)} %collective-permute-done.11.refs_11_) | copy-start | bytes 786436
  64.8 16.3 %collective-permute-start.13 = (bf16[4,2,64,256]{3,2,1,0:T(8,128)(2,1)S(1)}, bf16[4,2,64,256]{3,2,1,0:T(8,128)(2,1)S(1)}, u32[]{:S(2)}, u32[]{:S(2)}) collective-permute-start(bf16[4,2,64,256]{3,2,1,0:T(8,128)(2,1)S(1)} %collective-permute-done.11.refs_11_), channel_id=1, source_target_pairs={{0,7},{1,0},{2,1},{3,2},{4,3},{5,4},{6,5},{7,6},{8,15},{9,8},{10,9... | collective-permute-start | bytes 786440 | tf_op jit(solution)/shard_map/ppermute | solution.py:194
  66.8 23.6 %copy-start.4 = (bf16[4,2,64,256]{3,2,1,0:T(8,128)(2,1)}, bf16[4,2,64,256]{3,2,1,0:T(8,128)(2,1)S(1)}, u32[]{:S(2)}) copy-start(bf16[4,2,64,256]{3,2,1,0:T(8,128)(2,1)S(1)} %collective-permute-done.6.refs_6_) | copy-start | bytes 786436
  67.5 16.6 %collective-permute-start.14 = (bf16[2,2,64,256]{3,2,1,0:T(8,128)(2,1)}, bf16[2,2,64,256]{3,2,1,0:T(8,128)(2,1)S(1)}, u32[]{:S(2)}, u32[]{:S(2)}) collective-permute-start(bf16[2,2,64,256]{3,2,1,0:T(8,128)(2,1)} %slice.16), channel_id=1, source_target_pairs={{0,1},{1,2},{2,3},{3,4},{4,5},{5,6},{6,7},{7,0},{8,9},{9,10},{10,1... | collective-permute-start | bytes 393224 | tf_op jit(solution)/shard_map/ppermute | solution.py:196
  72.7 17.7 %copy-start.5 = (bf16[4,2,64,256]{3,2,1,0:T(8,128)(2,1)}, bf16[4,2,64,256]{3,2,1,0:T(8,128)(2,1)S(1)}, u32[]{:S(2)}) copy-start(bf16[4,2,64,256]{3,2,1,0:T(8,128)(2,1)S(1)} %collective-permute-done.12.refs_12_) | copy-start | bytes 786436
  73.4 10.7 %collective-permute-start.15 = (bf16[2,2,64,256]{3,2,1,0:T(8,128)(2,1)}, bf16[2,2,64,256]{3,2,1,0:T(8,128)(2,1)}, u32[]{:S(2)}, u32[]{:S(2)}) collective-permute-start(bf16[2,2,64,256]{3,2,1,0:T(8,128)(2,1)} %slice.17), channel_id=1, source_target_pairs={{0,7},{1,0},{2,1},{3,2},{4,3},{5,4},{6,5},{7,6},{8,15},{9,8},{10,9... | collective-permute-start | bytes 393224 | tf_op jit(solution)/shard_map/ppermute | solution.py:197
  75.3 15.1 %copy-start.6 = (bf16[4,2,64,256]{3,2,1,0:T(8,128)(2,1)}, bf16[4,2,64,256]{3,2,1,0:T(8,128)(2,1)S(1)}, u32[]{:S(2)}) copy-start(bf16[4,2,64,256]{3,2,1,0:T(8,128)(2,1)S(1)} %collective-permute-done.7.refs_7_) | copy-start | bytes 786436
  76.1 8.1 %collective-permute-start.16 = (bf16[2,2,64,256]{3,2,1,0:T(8,128)(2,1)}, bf16[2,2,64,256]{3,2,1,0:T(8,128)(2,1)}, u32[]{:S(2)}, u32[]{:S(2)}) collective-permute-start(bf16[2,2,64,256]{3,2,1,0:T(8,128)(2,1)} %slice.18), channel_id=1, source_target_pairs={{0,1},{1,2},{2,3},{3,4},{4,5},{5,6},{6,7},{7,0},{8,9},{9,10},{10,1... | collective-permute-start | bytes 393224 | tf_op jit(solution)/shard_map/ppermute | solution.py:196
  81.2 9.2 %copy-start.7 = (bf16[4,2,64,256]{3,2,1,0:T(8,128)(2,1)}, bf16[4,2,64,256]{3,2,1,0:T(8,128)(2,1)S(1)}, u32[]{:S(2)}) copy-start(bf16[4,2,64,256]{3,2,1,0:T(8,128)(2,1)S(1)} %collective-permute-done.13.refs_13_) | copy-start | bytes 786436
  81.9 8.4 %collective-permute-start.17 = (bf16[2,2,64,256]{3,2,1,0:T(8,128)(2,1)}, bf16[2,2,64,256]{3,2,1,0:T(8,128)(2,1)}, u32[]{:S(2)}, u32[]{:S(2)}) collective-permute-start(bf16[2,2,64,256]{3,2,1,0:T(8,128)(2,1)} %slice.19), channel_id=1, source_target_pairs={{0,7},{1,0},{2,1},{3,2},{4,3},{5,4},{6,5},{7,6},{8,15},{9,8},{10,9... | collective-permute-start | bytes 393224 | tf_op jit(solution)/shard_map/ppermute | solution.py:197
  84.1 6.3 %copy-start.18 = (bf16[2,2,64,256]{3,2,1,0:T(8,128)(2,1)}, bf16[2,2,64,256]{3,2,1,0:T(8,128)(2,1)S(1)}, u32[]{:S(2)}) copy-start(bf16[2,2,64,256]{3,2,1,0:T(8,128)(2,1)S(1)} %collective-permute-done.14.refs_14_) | copy-start | bytes 393220
Sparse Core Ops, SparseCore 0:
  24.8 54.9 all-gather.1

commit v3 on v0

v3 whole, which is shorter than its diff:
```python
import jax
import jax.numpy as jnp
from jax import lax
from jax.experimental import pallas as pl
from jax.experimental.pallas import tpu as pltpu
from jax.sharding import Mesh, PartitionSpec as P

N_Y = 8
N_TEST = 16
IMG_DEV = 4
PIX = 28
SLOT = 32
SURV = 14
MUT_DEV = 4
STEPS = 2
C = 1024
B = 256
CHUNK = C // N_TEST
ROWS = SURV * SLOT
OFFSETS = (0, -1, -2, -3, 1, 2, 3, 4)


def in_hbm(value):
    return pltpu.with_memory_space_constraint(value, pltpu.HBM)


def in_vmem(value):
    return pltpu.with_memory_space_constraint(value, pltpu.VMEM)


def score(*refs):
    wanted_ref, class_ref, strength_ref, images_ref, readout_hbm_ref = refs[:5]
    base_ref = refs[5]
    pieces = refs[6 : 6 + N_TEST]
    out_ref = refs[6 + N_TEST]
    x_ref, pooled_ref, keep_ref, label_ref, readout_ref = refs[7 + N_TEST : 12 + N_TEST]
    first_refs = refs[12 + N_TEST : 14 + N_TEST]
    last_refs = refs[14 + N_TEST : 16 + N_TEST]
    image_sem, readout_sem = refs[16 + N_TEST :]
    my_xl = lax.axis_index("xl")
    my_xh = lax.axis_index("xh")
    my_y = lax.axis_index("y")
    shard = my_xh * N_Y + my_y

    for variant in range(MUT_DEV):
        for entry in range(SURV):
            wanted = wanted_ref[variant, entry]
            holder = wanted // IMG_DEV
            within = wanted % IMG_DEV
            slot = jnp.where(holder // 16 != my_xl, 1, 0)
            start = (
                ((holder % 16) * 2 + slot) * (IMG_DEV * PIX)
                + (within // 2) * (2 * PIX)
                + (within % 2) * 24
            )
            pltpu.make_async_copy(
                images_ref.at[pl.ds(pl.multiple_of(start, 8), SLOT)],
                x_ref.at[variant, pl.ds(entry * SLOT, SLOT)],
                image_sem.at[variant],
            ).start()
    pltpu.make_async_copy(readout_hbm_ref, readout_ref, readout_sem).start()

    rows_of = []
    for number in range(N_TEST):
        plane = my_xh if number % 2 == 0 else 1 - my_xh
        origin = plane * N_Y + (my_y + OFFSETS[number // 2] + N_Y) % N_Y
        rows_of.append(pl.multiple_of(origin * CHUNK, CHUNK))

    def build(member):
        for number in range(N_TEST):
            row = rows_of[number]
            for kind in range(2):
                base = base_ref[kind, pl.ds(row, CHUNK), :].astype(jnp.float32)
                change = pieces[number][member, kind].astype(jnp.float32)
                for step in range(STEPS):
                    value = (base + strength_ref[step, member] * change).astype(jnp.bfloat16)
                    if kind == 0:
                        first_refs[member % 2][pl.ds(row, CHUNK), step * B : (step + 1) * B] = value
                    else:
                        last_refs[member % 2][step, pl.ds(row, CHUNK), :] = value

    build(0)
    pooled_ref[...] = jnp.zeros_like(pooled_ref)
    label_ref[...] = jnp.zeros_like(label_ref)
    sublane = lax.broadcasted_iota(jnp.int32, (8, B), 0)
    for variant in range(MUT_DEV):
        for entry in range(SURV):
            wanted = wanted_ref[variant, entry]
            within = wanted % IMG_DEV
            odd = within % 2
            keep_ref[variant, 0, entry] = jnp.where(sublane >= odd * 4, 1.0, 0.0)
            keep_ref[variant, 1, entry] = jnp.where(sublane < 4 + odd * 4, 1.0, 0.0)
            label = class_ref[((wanted // IMG_DEV) * N_TEST + shard) * IMG_DEV + within]
            for step in range(STEPS):
                row = (variant * STEPS + step) * 16 + entry
                label_ref[row : row + 1, :] = jnp.full((1, 128), label, jnp.int32)

    for member in range(MUT_DEV):
        pltpu.make_async_copy(
            images_ref.at[pl.ds(0, ROWS)], x_ref.at[member], image_sem.at[member]
        ).wait()
        if member + 1 < MUT_DEV:
            build(member + 1)
        for step in range(STEPS):
            hidden = jnp.maximum(
                jnp.dot(
                    x_ref[member],
                    first_refs[member % 2][:, step * B : (step + 1) * B],
                    preferred_element_type=jnp.float32,
                ),
                0.0,
            ).astype(jnp.bfloat16)
            for part in range(C // B):
                columns = slice(part * B, (part + 1) * B)
                expanded = lax.dot_general(
                    hidden,
                    last_refs[member % 2][step, columns, :],
                    (((1,), (1,)), ((), ())),
                    preferred_element_type=jnp.float32,
                )
                out_rows = jnp.maximum(expanded + x_ref[member, :, columns].astype(jnp.float32), 0.0)
                tiles = out_rows.reshape(SURV, SLOT // 8, 8, B)
                total = (
                    tiles[:, 0] * keep_ref[member, 0]
                    + tiles[:, 1]
                    + tiles[:, 2]
                    + tiles[:, 3] * keep_ref[member, 1]
                )
                pooled = (jnp.sum(total, axis=1) / PIX).astype(jnp.bfloat16)
                pooled_ref[member * STEPS + step, :SURV, columns] = pooled

    pltpu.make_async_copy(readout_hbm_ref, readout_ref, readout_sem).wait()
    logits = lax.dot_general(
        pooled_ref[...].reshape(MUT_DEV * STEPS * 16, C),
        readout_ref[...],
        (((1,), (1,)), ((), ())),
        preferred_element_type=jnp.float32,
    )
    top = jnp.max(logits, axis=1, keepdims=True)
    total = top + jnp.log(jnp.sum(jnp.exp(logits - top), axis=1, keepdims=True))
    column = lax.broadcasted_iota(jnp.int32, logits.shape, 1)
    chosen = jnp.sum(jnp.where(column == label_ref[:, :1], logits, 0.0), axis=1, keepdims=True)
    kill = total - chosen
    shape = (MUT_DEV * STEPS * 16, 128)
    diagonal = lax.broadcasted_iota(jnp.int32, shape, 1) == (
        lax.broadcasted_iota(jnp.int32, shape, 0) % 16
    )
    spread = jnp.where(diagonal, jnp.broadcast_to(kill, shape), 0.0)
    lined = jnp.sum(spread.reshape(MUT_DEV * STEPS, 16, 128), axis=1)
    for variant in range(MUT_DEV):
        out_ref[variant] = lined[variant * STEPS : (variant + 1) * STEPS, :SURV]


def on_device(
    input_activation,
    ground_truth_class,
    remaining_pictures,
    learned_narrowing_kernel,
    learned_widening_kernel,
    narrowing_perturbation,
    widening_perturbation,
    perturbation_strength,
    readout_matrix,
):
    swap = [(0, 1), (1, 0)]
    up = [(i, (i + 1) % N_Y) for i in range(N_Y)]
    down = [(i, (i - 1) % N_Y) for i in range(N_Y)]

    own_rows = input_activation.reshape(IMG_DEV * PIX, C)
    message = jnp.stack(
        [narrowing_perturbation, jnp.transpose(widening_perturbation, (0, 2, 1))], axis=1
    )
    own_rows, message = lax.optimization_barrier((own_rows, message))
    partner_rows = lax.ppermute(own_rows, "xl", swap)
    first_up = lax.ppermute(message, "y", up)
    partner_rows, first_up = lax.optimization_barrier((partner_rows, first_up))
    images = lax.all_gather(
        jnp.concatenate([own_rows, partner_rows]), ("z", "core"), axis=0, tiled=True
    )

    other = lax.ppermute(message, "xh", swap)
    flows = []
    for number, seed in enumerate((message, other)):
        rising = [first_up if number == 0 else lax.ppermute(seed, "y", up)]
        falling = [lax.ppermute(seed, "y", down)]
        for _ in range(2):
            rising.append(lax.ppermute(rising[-1], "y", up))
            falling.append(lax.ppermute(falling[-1], "y", down))
        if number == 0:
            farthest = lax.ppermute(rising[-1], "y", up)
        else:
            farthest = lax.ppermute(falling[-1], "y", down)
        flows.append([seed] + rising + falling + [farthest])
    pieces = [flows[number % 2][number // 2] for number in range(N_TEST)]

    bases = jnp.stack([learned_narrowing_kernel, learned_widening_kernel.T])
    smem = pl.BlockSpec(memory_space=pltpu.SMEM)
    vmem = pl.BlockSpec(memory_space=pltpu.VMEM)
    hbm = pl.BlockSpec(memory_space=pl.ANY)
    return pl.pallas_call(
        score,
        in_specs=[smem, smem, smem, hbm, hbm, vmem] + [vmem] * N_TEST,
        out_specs=vmem,
        out_shape=jax.ShapeDtypeStruct((MUT_DEV, STEPS, SURV), jnp.float32),
        scratch_shapes=[
            pltpu.VMEM((MUT_DEV, ROWS, C), jnp.bfloat16),
            pltpu.VMEM((MUT_DEV * STEPS, 16, C), jnp.bfloat16),
            pltpu.VMEM((MUT_DEV, 2, SURV, 8, B), jnp.float32),
            pltpu.VMEM((MUT_DEV * STEPS * 16, 128), jnp.int32),
            pltpu.VMEM((readout_matrix.shape[1], C), jnp.bfloat16),
            pltpu.VMEM((C, STEPS * B), jnp.bfloat16),
            pltpu.VMEM((C, STEPS * B), jnp.bfloat16),
            pltpu.VMEM((STEPS, C, B), jnp.bfloat16),
            pltpu.VMEM((STEPS, C, B), jnp.bfloat16),
            pltpu.SemaphoreType.DMA((MUT_DEV,)),
            pltpu.SemaphoreType.DMA,
        ],
        compiler_params=pltpu.CompilerParams(vmem_limit_bytes=24 * 2**20),
    )(
        remaining_pictures,
        ground_truth_class,
        perturbation_strength.T,
        in_hbm(images),
        in_hbm(readout_matrix.T),
        in_vmem(bases),
        *[in_vmem(value) for value in pieces],
    )


def solution(mesh):
    fine = Mesh(mesh.devices.reshape(2, 8, 2, 2, N_Y), ("xl", "z", "core", "xh", "y"))
    mut = ("xl", "z", "core")
    test = ("xh", "y")
    return jax.shard_map(
        on_device,
        mesh=fine,
        in_specs=(
            P(mut + test, None, None),
            P(),
            P(mut, test),
            P(),
            P(),
            P(mut, test, None),
            P(mut, None, test),
            P(mut, None),
            P(),
        ),
        out_specs=P(mut, None, test),
        check_vma=False,
    )
```

time: 367 us -> 106 us (0.29)
  waiting for transfers between devices: 236 us -> 18.3 us
  starting transfers between devices: 0.11 us -> 51.5 us
  matrix products: 44.1 us -> 0 us
  local copies, waits for them, and re-layouts: 42.6 us -> 5.17 us
  other arithmetic: 27.5 us -> 3.19 us
  Pallas kernels: 0 us -> 13.3 us
    all_gather x3 -> x1, waiting for transfers between devices: 234 us -> 0.01 us  [on_device(): lax.all_gather(jnp.concatenate([own_rows, partner_rows]), ('z', 'core'),...]
    ppermute x0 -> x16, starting transfers between devices: none -> 51.5 us  [the longest x4 18.1 us: on_device(): rising.append(lax.ppermute(rising[-1], 'y', up))]
    dot_general x20 -> x0, matrix products: 44.1 us -> none  [the longest x8 26.3 us: on_device(): jnp.dot(hidden, w_last, preferred_element_type=jnp.float32)]
    reshape x14 -> x1, local copies, waits for them, and re-layouts: 27.8 us -> 0.05 us  [on_device(): own_rows = input_activation.reshape(IMG_DEV * PIX, C)]
    ppermute x0 -> x16, waiting for transfers between devices: none -> 18.3 us  [the longest x1 7.84 us: on_device(): other = lax.ppermute(message, 'xh', swap)]
    reduce_sum x10 -> x0, other arithmetic: 14.9 us -> none  [the longest x8 14.3 us: on_device(): jnp.mean(out_rows.reshape(bottleneck_unit.shape), axis=1)]
    pallas_call x0 -> x1, Pallas kernels: none -> 13.3 us  [on_device(): pl.pallas_call(score, in_specs=[smem, smem, smem, hbm, hbm, vmem] + [vmem...]
    convert_element_type x1 -> x0, other arithmetic: 9.47 us -> none  [on_device(): first_list.append((learned_narrowing_kernel.astype(jnp.float32) + perturb...]
  transfers between devices with their start and end apart: 3 -> 17, of which waited for: 3 -> 3; matrix products, arithmetic and copies ran while one was open for 8% -> 3% of each run, Pallas kernels for 0% -> 0%
where the time goes in v3:
time: 106 us; the launch traced here: 105 us
  starting transfers between devices  51.5 us (49%)
  waiting for transfers between devices  18.3 us (17%)
  between operations  13.7 us (13%)
  Pallas kernels  13.3 us (13%)
  local copies, waits for them, and re-layouts  5.17 us (5%)
  other arithmetic  3.19 us (3%)
    ppermute x4, starting transfers between devices, on_device(): rising.append(lax.ppermute(rising[-1], 'y', up))  18.1 us
    pallas_call x1, Pallas kernels, on_device(): pl.pallas_call(score, in_specs=[smem, smem, smem, hbm, hbm, vmem] + [vmem...  13.3 us
    ppermute x1, waiting for transfers between devices, on_device(): other = lax.ppermute(message, 'xh', swap)  7.84 us
    ppermute x4, starting transfers between devices, on_device(): falling.append(lax.ppermute(falling[-1], 'y', down))  7.68 us
    ppermute x1, starting transfers between devices, on_device(): first_up = lax.ppermute(message, 'y', up)  7.05 us
    ppermute x1, waiting for transfers between devices, on_device(): partner_rows = lax.ppermute(own_rows, 'xl', swap)  5.99 us
    ppermute x1, starting transfers between devices, on_device(): rising = [first_up if number == 0 else lax.ppermute(seed, 'y', up)]  5.13 us
    unnamed x8, local copies, waits for them, and re-layouts  5.12 us
  transfers between devices with their start and end apart: 17, of which 3 were waited for; matrix products, arithmetic and copies ran while one was open for 3% of the time, Pallas kernels for 0%

profile of v3, /device:TPU:56, one launch (start us, length us, event | category | flops | bytes accessed | tf_op | source)
XLA Modules:
  0.0 105.1 jit_solution(19240849343478815)
XLA Ops:
  6.5 0.0 all-gather.2.cloned.1.call-start
  6.5 1.0 copy.12
  7.6 1.0 pad_maximum_fusion.2.refs_6_
  8.6 7.0 %collective-permute-start.1 = (bf16[4,2,64,256]{3,2,1,0:T(8,128)(2,1)S(1)}, bf16[4,2,64,256]{3,2,1,0:T(8,128)(2,1)S(1)}, u32[]{:S(2)}, u32[]{:S(2)}) collective-permute-start(bf16[4,2,64,256]{3,2,1,0:T(8,128)(2,1)S(1)} %pad_maximum_fusion.2.refs_6_), channel_id=1, source_target_pairs={{0,1},{1,2},{2,3},{3,4},{4,5},{5,6},{6,7},{7,0},{8,9},{9,10},{10,1... | collective-permute-start | bytes 786440 | tf_op jit(solution)/shard_map/ppermute | solution.py:175
  15.7 1.9 %collective-permute-start = (bf16[112,1024]{1,0:T(8,128)(2,1)S(1)}, bf16[112,1024]{1,0:T(8,128)(2,1)S(1)}, u32[]{:S(2)}, u32[]{:S(2)}) collective-permute-start(bf16[112,1024]{1,0:T(8,128)(2,1)S(1)} %reshape.3), channel_id=1, source_target_pairs={{0,256},{256,0},{1,257},{257,1},{2,258},{258,2},{3,259},{259,3},{4... | collective-permute-start | bytes 688136 | tf_op jit(solution)/shard_map/ppermute | solution.py:174
  17.6 6.0 %collective-permute-done = bf16[112,1024]{1,0:T(8,128)(2,1)S(1)} collective-permute-done((bf16[112,1024]{1,0:T(8,128)(2,1)S(1)}, bf16[112,1024]{1,0:T(8,128)(2,1)S(1)}, u32[]{:S(2)}, u32[]{:S(2)}) %collective-permute-start) | collective-permute-done | bytes 229408 | tf_op jit(solution)/shard_map/ppermute | solution.py:174
  23.6 0.0 collective-permute-done.1.refs_8_
  23.6 0.9 pad_maximum_fusion.1
  24.4 0.0 all-gather.2.cloned.1.call-update
  24.5 1.9 %collective-permute-start.2 = (bf16[4,2,64,256]{3,2,1,0:T(8,128)(2,1)S(1)}, bf16[4,2,64,256]{3,2,1,0:T(8,128)(2,1)S(1)}, u32[]{:S(2)}, u32[]{:S(2)}) collective-permute-start(bf16[4,2,64,256]{3,2,1,0:T(8,128)(2,1)S(1)} %pad_maximum_fusion.2.refs_6_), channel_id=1, source_target_pairs={{0,8},{8,0},{1,9},{9,1},{2,10},{10,2},{3,11},{11,3},{4,12},{12,4},... | collective-permute-start | bytes 786440 | tf_op jit(solution)/shard_map/ppermute | solution.py:181
  26.4 7.8 %collective-permute-done.2.refs_7_ = bf16[4,2,64,256]{3,2,1,0:T(8,128)(2,1)S(1)} collective-permute-done((bf16[4,2,64,256]{3,2,1,0:T(8,128)(2,1)S(1)}, bf16[4,2,64,256]{3,2,1,0:T(8,128)(2,1)S(1)}, u32[]{:S(2)}, u32[]{:S(2)}) %collective-permute-start.2) | collective-permute-done | bytes 262176 | tf_op jit(solution)/shard_map/ppermute | solution.py:181
  34.2 1.9 %collective-permute-start.9 = (bf16[4,2,64,256]{3,2,1,0:T(8,128)(2,1)S(1)}, bf16[4,2,64,256]{3,2,1,0:T(8,128)(2,1)S(1)}, u32[]{:S(2)}, u32[]{:S(2)}) collective-permute-start(bf16[4,2,64,256]{3,2,1,0:T(8,128)(2,1)S(1)} %collective-permute-done.2.refs_7_), channel_id=1, source_target_pairs={{0,7},{1,0},{2,1},{3,2},{4,3},{5,4},{6,5},{7,6},{8,15},{9,8},{10,9... | collective-permute-start | bytes 786440 | tf_op jit(solution)/shard_map/ppermute | solution.py:185
  36.2 1.9 %collective-permute-start.8 = (bf16[4,2,64,256]{3,2,1,0:T(8,128)(2,1)S(1)}, bf16[4,2,64,256]{3,2,1,0:T(8,128)(2,1)S(1)}, u32[]{:S(2)}, u32[]{:S(2)}) collective-permute-start(bf16[4,2,64,256]{3,2,1,0:T(8,128)(2,1)S(1)} %pad_maximum_fusion.2.refs_6_), channel_id=1, source_target_pairs={{0,7},{1,0},{2,1},{3,2},{4,3},{5,4},{6,5},{7,6},{8,15},{9,8},{10,9... | collective-permute-start | bytes 786440 | tf_op jit(solution)/shard_map/ppermute | solution.py:185
  38.1 5.1 %collective-permute-start.3 = (bf16[4,2,64,256]{3,2,1,0:T(8,128)(2,1)S(1)}, bf16[4,2,64,256]{3,2,1,0:T(8,128)(2,1)S(1)}, u32[]{:S(2)}, u32[]{:S(2)}) collective-permute-start(bf16[4,2,64,256]{3,2,1,0:T(8,128)(2,1)S(1)} %collective-permute-done.2.refs_7_), channel_id=1, source_target_pairs={{0,1},{1,2},{2,3},{3,4},{4,5},{5,6},{6,7},{7,0},{8,9},{9,10},{10,1... | collective-permute-start | bytes 786440 | tf_op jit(solution)/shard_map/ppermute | solution.py:184
  43.2 3.9 %collective-permute-start.4 = (bf16[4,2,64,256]{3,2,1,0:T(8,128)(2,1)S(1)}, bf16[4,2,64,256]{3,2,1,0:T(8,128)(2,1)S(1)}, u32[]{:S(2)}, u32[]{:S(2)}) collective-permute-start(bf16[4,2,64,256]{3,2,1,0:T(8,128)(2,1)S(1)} %collective-permute-done.1.refs_8_), channel_id=1, source_target_pairs={{0,1},{1,2},{2,3},{3,4},{4,5},{5,6},{6,7},{7,0},{8,9},{9,10},{10,1... | collective-permute-start | bytes 786440 | tf_op jit(solution)/shard_map/ppermute | solution.py:187
  47.2 0.0 collective-permute-done.9.refs_15_
  47.2 1.9 %collective-permute-start.11 = (bf16[4,2,64,256]{3,2,1,0:T(8,128)(2,1)S(1)}, bf16[4,2,64,256]{3,2,1,0:T(8,128)(2,1)S(1)}, u32[]{:S(2)}, u32[]{:S(2)}) collective-permute-start(bf16[4,2,64,256]{3,2,1,0:T(8,128)(2,1)S(1)} %collective-permute-done.9.refs_15_), channel_id=1, source_target_pairs={{0,7},{1,0},{2,1},{3,2},{4,3},{5,4},{6,5},{7,6},{8,15},{9,8},{10,9... | collective-permute-start | bytes 786440 | tf_op jit(solution)/shard_map/ppermute | solution.py:188
  49.1 0.0 collective-permute-done.8.refs_14_
  49.1 1.9 %collective-permute-start.10 = (bf16[4,2,64,256]{3,2,1,0:T(8,128)(2,1)S(1)}, bf16[4,2,64,256]{3,2,1,0:T(8,128)(2,1)S(1)}, u32[]{:S(2)}, u32[]{:S(2)}) collective-permute-start(bf16[4,2,64,256]{3,2,1,0:T(8,128)(2,1)S(1)} %collective-permute-done.8.refs_14_), channel_id=1, source_target_pairs={{0,7},{1,0},{2,1},{3,2},{4,3},{5,4},{6,5},{7,6},{8,15},{9,8},{10,9... | collective-permute-start | bytes 786440 | tf_op jit(solution)/shard_map/ppermute | solution.py:188
  51.0 0.0 collective-permute-done.3.refs_9_
  51.0 5.1 %collective-permute-start.5 = (bf16[4,2,64,256]{3,2,1,0:T(8,128)(2,1)S(1)}, bf16[4,2,64,256]{3,2,1,0:T(8,128)(2,1)}, u32[]{:S(2)}, u32[]{:S(2)}) collective-permute-start(bf16[4,2,64,256]{3,2,1,0:T(8,128)(2,1)S(1)} %collective-permute-done.3.refs_9_), channel_id=1, source_target_pairs={{0,1},{1,2},{2,3},{3,4},{4,5},{5,6},{6,7},{7,0},{8,9},{9,10},{10,1... | collective-permute-start | bytes 786440 | tf_op jit(solution)/shard_map/ppermute | solution.py:187
  56.2 0.0 collective-permute-done.4.refs_10_
  56.2 3.9 %collective-permute-start.6 = (bf16[4,2,64,256]{3,2,1,0:T(8,128)(2,1)S(1)}, bf16[4,2,64,256]{3,2,1,0:T(8,128)(2,1)}, u32[]{:S(2)}, u32[]{:S(2)}) collective-permute-start(bf16[4,2,64,256]{3,2,1,0:T(8,128)(2,1)S(1)} %collective-permute-done.4.refs_10_), channel_id=1, source_target_pairs={{0,1},{1,2},{2,3},{3,4},{4,5},{5,6},{6,7},{7,0},{8,9},{9,10},{10,1... | collective-permute-start | bytes 786440 | tf_op jit(solution)/shard_map/ppermute | solution.py:187
  60.1 0.0 collective-permute-done.11.refs_17_
  60.1 1.9 %collective-permute-start.13 = (bf16[4,2,64,256]{3,2,1,0:T(8,128)(2,1)S(1)}, bf16[4,2,64,256]{3,2,1,0:T(8,128)(2,1)}, u32[]{:S(2)}, u32[]{:S(2)}) collective-permute-start(bf16[4,2,64,256]{3,2,1,0:T(8,128)(2,1)S(1)} %collective-permute-done.11.refs_17_), channel_id=1, source_target_pairs={{0,7},{1,0},{2,1},{3,2},{4,3},{5,4},{6,5},{7,6},{8,15},{9,8},{10,9... | collective-permute-start | bytes 786440 | tf_op jit(solution)/shard_map/ppermute | solution.py:188
  62.1 0.0 collective-permute-done.10.refs_16_
  62.1 1.9 %collective-permute-start.12 = (bf16[4,2,64,256]{3,2,1,0:T(8,128)(2,1)S(1)}, bf16[4,2,64,256]{3,2,1,0:T(8,128)(2,1)}, u32[]{:S(2)}, u32[]{:S(2)}) collective-permute-start(bf16[4,2,64,256]{3,2,1,0:T(8,128)(2,1)S(1)} %collective-permute-done.10.refs_16_), channel_id=1, source_target_pairs={{0,7},{1,0},{2,1},{3,2},{4,3},{5,4},{6,5},{7,6},{8,15},{9,8},{10,9... | collective-permute-start | bytes 786440 | tf_op jit(solution)/shard_map/ppermute | solution.py:188
  64.0 0.0 collective-permute-done.5.refs_11_
  64.0 5.1 %collective-permute-start.7 = (bf16[4,2,64,256]{3,2,1,0:T(8,128)(2,1)}, bf16[4,2,64,256]{3,2,1,0:T(8,128)(2,1)}, u32[]{:S(2)}, u32[]{:S(2)}) collective-permute-start(bf16[4,2,64,256]{3,2,1,0:T(8,128)(2,1)} %collective-permute-done.5.refs_11_), channel_id=1, source_target_pairs={{0,1},{1,2},{2,3},{3,4},{4,5},{5,6},{6,7},{7,0},{8,9},{9,10},{10,1... | collective-permute-start | bytes 786440 | tf_op jit(solution)/shard_map/ppermute | solution.py:187
  69.2 0.0 collective-permute-done.6.refs_12_
  69.2 3.9 %collective-permute-start.14 = (bf16[4,2,64,256]{3,2,1,0:T(8,128)(2,1)}, bf16[4,2,64,256]{3,2,1,0:T(8,128)(2,1)}, u32[]{:S(2)}, u32[]{:S(2)}) collective-permute-start(bf16[4,2,64,256]{3,2,1,0:T(8,128)(2,1)} %collective-permute-done.6.refs_12_), channel_id=1, source_target_pairs={{0,1},{1,2},{2,3},{3,4},{4,5},{5,6},{6,7},{7,0},{8,9},{9,10},{10,1... | collective-permute-start | bytes 786440 | tf_op jit(solution)/shard_map/ppermute | solution.py:190
  73.1 0.0 collective-permute-done.13.refs_19_
  73.1 1.9 %collective-permute-start.15 = (bf16[4,2,64,256]{3,2,1,0:T(8,128)(2,1)}, bf16[4,2,64,256]{3,2,1,0:T(8,128)(2,1)}, u32[]{:S(2)}, u32[]{:S(2)}) collective-permute-start(bf16[4,2,64,256]{3,2,1,0:T(8,128)(2,1)} %collective-permute-done.13.refs_19_), channel_id=1, source_target_pairs={{0,7},{1,0},{2,1},{3,2},{4,3},{5,4},{6,5},{7,6},{8,15},{9,8},{10,9... | collective-permute-start | bytes 786440 | tf_op jit(solution)/shard_map/ppermute | solution.py:192
  75.0 2.1 %copy.13 = bf16[256,1024]{0,1:T(8,128)(2,1)} copy(bf16[256,1024]{1,0:T(8,128)(2,1)} %param.13) | data formatting | bytes 1048576 | tf_op args[4]
  77.1 1.3 %pad_maximum_fusion.refs_5_ = bf16[2,1024,256]{2,1,0:T(8,128)(2,1)S(1)} fusion(bf16[1,1024,256]{2,1,0:T(8,128)(2,1)} %bitcast.11, bf16[1,1024,256]{2,1,0:T(8,128)(2,1)} %bitcast.13), kind=kLoop, calls=%fused_computation | loop fusion | flops 524288 | bytes 2097152 | tf_op jit(solution)/shard_map/stack | solution.py:196
  78.4 0.0 collective-permute-done.12.refs_18_
  78.4 0.0 collective-permute-done.7.refs_13_
  78.4 0.0 collective-permute-done.14.refs_20_
  78.5 4.4 %collective-permute-done.15.refs_21_ = bf16[4,2,64,256]{3,2,1,0:T(8,128)(2,1)} collective-permute-done((bf16[4,2,64,256]{3,2,1,0:T(8,128)(2,1)}, bf16[4,2,64,256]{3,2,1,0:T(8,128)(2,1)}, u32[]{:S(2)}, u32[]{:S(2)}) %collective-permute-start.15) | collective-permute-done | bytes 262176 | tf_op jit(solution)/shard_map/ppermute | solution.py:192
  82.9 0.0 all-gather.2.cloned.1.call-done.refs_3_
  82.9 0.0 copy-start
  82.9 0.7 copy-done
  83.6 0.0 copy-start.1
  83.6 0.7 copy-done.1
  84.3 0.0 copy-start.2
  84.3 0.7 copy-done.2
  85.0 13.3 %shard_map.91 = f32[4,2,14]{2,1,0:T(2,128)} custom-call(s32[4,14]{1,0:T(4,128)S(1)} %copy-done.1, s32[2048]{0:T(1024)S(1)} %copy-done, f32[2,4]{1,0:T(2,128)S(1)} %bitcast.10, bf16[3584,1024]{1,0:T(8,128)(2,1)} %all-gather.2.cloned.1.call-done.refs_3_, bf16[1000,1024]{1,0:T(8,128)(2,1)} %bitcast.12, bf16[2,1024,256]{2,1,0:T(8,128)(2,1)S(1)} %pad_maximum_fusion.refs_5_, ...), custom_call_target="tpu_custom_call" | custom-call | tf_op jit(solution)/shard_map/pallas_call | solution.py:200
  (1 shorter events, 0.0 us)
Async XLA Ops:
  6.5 76.4 %all-gather.2.cloned.1.call-start = ((), (), s32[]{:S(2)}) async-start(), calls=%async_computation | async-start | bytes 7798784 | tf_op jit(solution)/shard_map/all_gather | solution.py:177
  8.6 15.0 %collective-permute-start.1 = (bf16[4,2,64,256]{3,2,1,0:T(8,128)(2,1)S(1)}, bf16[4,2,64,256]{3,2,1,0:T(8,128)(2,1)S(1)}, u32[]{:S(2)}, u32[]{:S(2)}) collective-permute-start(bf16[4,2,64,256]{3,2,1,0:T(8,128)(2,1)S(1)} %pad_maximum_fusion.2.refs_6_), channel_id=1, source_target_pairs={{0,1},{1,2},{2,3},{3,4},{4,5},{5,6},{6,7},{7,0},{8,9},{9,10},{10,1... | collective-permute-start | bytes 786440 | tf_op jit(solution)/shard_map/ppermute | solution.py:175
  15.7 7.9 %collective-permute-start = (bf16[112,1024]{1,0:T(8,128)(2,1)S(1)}, bf16[112,1024]{1,0:T(8,128)(2,1)S(1)}, u32[]{:S(2)}, u32[]{:S(2)}) collective-permute-start(bf16[112,1024]{1,0:T(8,128)(2,1)S(1)} %reshape.3), channel_id=1, source_target_pairs={{0,256},{256,0},{1,257},{257,1},{2,258},{258,2},{3,259},{259,3},{4... | collective-permute-start | bytes 688136 | tf_op jit(solution)/shard_map/ppermute | solution.py:174
  24.5 9.8 %collective-permute-start.2 = (bf16[4,2,64,256]{3,2,1,0:T(8,128)(2,1)S(1)}, bf16[4,2,64,256]{3,2,1,0:T(8,128)(2,1)S(1)}, u32[]{:S(2)}, u32[]{:S(2)}) collective-permute-start(bf16[4,2,64,256]{3,2,1,0:T(8,128)(2,1)S(1)} %pad_maximum_fusion.2.refs_6_), channel_id=1, source_target_pairs={{0,8},{8,0},{1,9},{9,1},{2,10},{10,2},{3,11},{11,3},{4,12},{12,4},... | collective-permute-start | bytes 786440 | tf_op jit(solution)/shard_map/ppermute | solution.py:181
  34.2 12.9 %collective-permute-start.9 = (bf16[4,2,64,256]{3,2,1,0:T(8,128)(2,1)S(1)}, bf16[4,2,64,256]{3,2,1,0:T(8,128)(2,1)S(1)}, u32[]{:S(2)}, u32[]{:S(2)}) collective-permute-start(bf16[4,2,64,256]{3,2,1,0:T(8,128)(2,1)S(1)} %collective-permute-done.2.refs_7_), channel_id=1, source_target_pairs={{0,7},{1,0},{2,1},{3,2},{4,3},{5,4},{6,5},{7,6},{8,15},{9,8},{10,9... | collective-permute-start | bytes 786440 | tf_op jit(solution)/shard_map/ppermute | solution.py:185
  36.2 12.9 %collective-permute-start.8 = (bf16[4,2,64,256]{3,2,1,0:T(8,128)(2,1)S(1)}, bf16[4,2,64,256]{3,2,1,0:T(8,128)(2,1)S(1)}, u32[]{:S(2)}, u32[]{:S(2)}) collective-permute-start(bf16[4,2,64,256]{3,2,1,0:T(8,128)(2,1)S(1)} %pad_maximum_fusion.2.refs_6_), channel_id=1, source_target_pairs={{0,7},{1,0},{2,1},{3,2},{4,3},{5,4},{6,5},{7,6},{8,15},{9,8},{10,9... | collective-permute-start | bytes 786440 | tf_op jit(solution)/shard_map/ppermute | solution.py:185
  38.1 13.0 %collective-permute-start.3 = (bf16[4,2,64,256]{3,2,1,0:T(8,128)(2,1)S(1)}, bf16[4,2,64,256]{3,2,1,0:T(8,128)(2,1)S(1)}, u32[]{:S(2)}, u32[]{:S(2)}) collective-permute-start(bf16[4,2,64,256]{3,2,1,0:T(8,128)(2,1)S(1)} %collective-permute-done.2.refs_7_), channel_id=1, source_target_pairs={{0,1},{1,2},{2,3},{3,4},{4,5},{5,6},{6,7},{7,0},{8,9},{9,10},{10,1... | collective-permute-start | bytes 786440 | tf_op jit(solution)/shard_map/ppermute | solution.py:184
  43.2 13.0 %collective-permute-start.4 = (bf16[4,2,64,256]{3,2,1,0:T(8,128)(2,1)S(1)}, bf16[4,2,64,256]{3,2,1,0:T(8,128)(2,1)S(1)}, u32[]{:S(2)}, u32[]{:S(2)}) collective-permute-start(bf16[4,2,64,256]{3,2,1,0:T(8,128)(2,1)S(1)} %collective-permute-done.1.refs_8_), channel_id=1, source_target_pairs={{0,1},{1,2},{2,3},{3,4},{4,5},{5,6},{6,7},{7,0},{8,9},{9,10},{10,1... | collective-permute-start | bytes 786440 | tf_op jit(solution)/shard_map/ppermute | solution.py:187
  47.2 13.0 %collective-permute-start.11 = (bf16[4,2,64,256]{3,2,1,0:T(8,128)(2,1)S(1)}, bf16[4,2,64,256]{3,2,1,0:T(8,128)(2,1)S(1)}, u32[]{:S(2)}, u32[]{:S(2)}) collective-permute-start(bf16[4,2,64,256]{3,2,1,0:T(8,128)(2,1)S(1)} %collective-permute-done.9.refs_15_), channel_id=1, source_target_pairs={{0,7},{1,0},{2,1},{3,2},{4,3},{5,4},{6,5},{7,6},{8,15},{9,8},{10,9... | collective-permute-start | bytes 786440 | tf_op jit(solution)/shard_map/ppermute | solution.py:188
  49.1 13.0 %collective-permute-start.10 = (bf16[4,2,64,256]{3,2,1,0:T(8,128)(2,1)S(1)}, bf16[4,2,64,256]{3,2,1,0:T(8,128)(2,1)S(1)}, u32[]{:S(2)}, u32[]{:S(2)}) collective-permute-start(bf16[4,2,64,256]{3,2,1,0:T(8,128)(2,1)S(1)} %collective-permute-done.8.refs_14_), channel_id=1, source_target_pairs={{0,7},{1,0},{2,1},{3,2},{4,3},{5,4},{6,5},{7,6},{8,15},{9,8},{10,9... | collective-permute-start | bytes 786440 | tf_op jit(solution)/shard_map/ppermute | solution.py:188
  51.0 13.0 %collective-permute-start.5 = (bf16[4,2,64,256]{3,2,1,0:T(8,128)(2,1)S(1)}, bf16[4,2,64,256]{3,2,1,0:T(8,128)(2,1)}, u32[]{:S(2)}, u32[]{:S(2)}) collective-permute-start(bf16[4,2,64,256]{3,2,1,0:T(8,128)(2,1)S(1)} %collective-permute-done.3.refs_9_), channel_id=1, source_target_pairs={{0,1},{1,2},{2,3},{3,4},{4,5},{5,6},{6,7},{7,0},{8,9},{9,10},{10,1... | collective-permute-start | bytes 786440 | tf_op jit(solution)/shard_map/ppermute | solution.py:187
  56.2 13.0 %collective-permute-start.6 = (bf16[4,2,64,256]{3,2,1,0:T(8,128)(2,1)S(1)}, bf16[4,2,64,256]{3,2,1,0:T(8,128)(2,1)}, u32[]{:S(2)}, u32[]{:S(2)}) collective-permute-start(bf16[4,2,64,256]{3,2,1,0:T(8,128)(2,1)S(1)} %collective-permute-done.4.refs_10_), channel_id=1, source_target_pairs={{0,1},{1,2},{2,3},{3,4},{4,5},{5,6},{6,7},{7,0},{8,9},{9,10},{10,1... | collective-permute-start | bytes 786440 | tf_op jit(solution)/shard_map/ppermute | solution.py:187
  60.1 13.0 %collective-permute-start.13 = (bf16[4,2,64,256]{3,2,1,0:T(8,128)(2,1)S(1)}, bf16[4,2,64,256]{3,2,1,0:T(8,128)(2,1)}, u32[]{:S(2)}, u32[]{:S(2)}) collective-permute-start(bf16[4,2,64,256]{3,2,1,0:T(8,128)(2,1)S(1)} %collective-permute-done.11.refs_17_), channel_id=1, source_target_pairs={{0,7},{1,0},{2,1},{3,2},{4,3},{5,4},{6,5},{7,6},{8,15},{9,8},{10,9... | collective-permute-start | bytes 786440 | tf_op jit(solution)/shard_map/ppermute | solution.py:188
  62.1 16.4 %collective-permute-start.12 = (bf16[4,2,64,256]{3,2,1,0:T(8,128)(2,1)S(1)}, bf16[4,2,64,256]{3,2,1,0:T(8,128)(2,1)}, u32[]{:S(2)}, u32[]{:S(2)}) collective-permute-start(bf16[4,2,64,256]{3,2,1,0:T(8,128)(2,1)S(1)} %collective-permute-done.10.refs_16_), channel_id=1, source_target_pairs={{0,7},{1,0},{2,1},{3,2},{4,3},{5,4},{6,5},{7,6},{8,15},{9,8},{10,9... | collective-permute-start | bytes 786440 | tf_op jit(solution)/shard_map/ppermute | solution.py:188
  64.0 14.4 %collective-permute-start.7 = (bf16[4,2,64,256]{3,2,1,0:T(8,128)(2,1)}, bf16[4,2,64,256]{3,2,1,0:T(8,128)(2,1)}, u32[]{:S(2)}, u32[]{:S(2)}) collective-permute-start(bf16[4,2,64,256]{3,2,1,0:T(8,128)(2,1)} %collective-permute-done.5.refs_11_), channel_id=1, source_target_pairs={{0,1},{1,2},{2,3},{3,4},{4,5},{5,6},{6,7},{7,0},{8,9},{9,10},{10,1... | collective-permute-start | bytes 786440 | tf_op jit(solution)/shard_map/ppermute | solution.py:187
  69.2 9.3 %collective-permute-start.14 = (bf16[4,2,64,256]{3,2,1,0:T(8,128)(2,1)}, bf16[4,2,64,256]{3,2,1,0:T(8,128)(2,1)}, u32[]{:S(2)}, u32[]{:S(2)}) collective-permute-start(bf16[4,2,64,256]{3,2,1,0:T(8,128)(2,1)} %collective-permute-done.6.refs_12_), channel_id=1, source_target_pairs={{0,1},{1,2},{2,3},{3,4},{4,5},{5,6},{6,7},{7,0},{8,9},{9,10},{10,1... | collective-permute-start | bytes 786440 | tf_op jit(solution)/shard_map/ppermute | solution.py:190
  73.1 9.8 %collective-permute-start.15 = (bf16[4,2,64,256]{3,2,1,0:T(8,128)(2,1)}, bf16[4,2,64,256]{3,2,1,0:T(8,128)(2,1)}, u32[]{:S(2)}, u32[]{:S(2)}) collective-permute-start(bf16[4,2,64,256]{3,2,1,0:T(8,128)(2,1)} %collective-permute-done.13.refs_19_), channel_id=1, source_target_pairs={{0,7},{1,0},{2,1},{3,2},{4,3},{5,4},{6,5},{7,6},{8,15},{9,8},{10,9... | collective-permute-start | bytes 786440 | tf_op jit(solution)/shard_map/ppermute | solution.py:192
  82.9 0.7 copy-start
  83.6 0.7 copy-start.1
  84.3 0.7 copy-start.2
Sparse Core Ops, SparseCore 0:
  24.6 54.9 all-gather.1

commit v4 on v3

--- a/solution.py
+++ b/solution.py
@@ -29,35 +29,35 @@
 
 
 def score(*refs):
-    wanted_ref, class_ref, strength_ref, images_ref, readout_hbm_ref = refs[:5]
-    base_ref = refs[5]
-    pieces = refs[6 : 6 + N_TEST]
-    out_ref = refs[6 + N_TEST]
-    x_ref, pooled_ref, keep_ref, label_ref, readout_ref = refs[7 + N_TEST : 12 + N_TEST]
-    first_refs = refs[12 + N_TEST : 14 + N_TEST]
-    last_refs = refs[14 + N_TEST : 16 + N_TEST]
-    image_sem, readout_sem = refs[16 + N_TEST :]
-    my_xl = lax.axis_index("xl")
+    plan_ref, strength_ref, images_ref, readout_hbm_ref, base_ref = refs[:5]
+    piece_hbm_refs = refs[5 : 5 + N_TEST]
+    out_ref = refs[5 + N_TEST]
+    x_ref, pooled_ref, keep_ref, label_ref, readout_ref = refs[6 + N_TEST : 11 + N_TEST]
+    first_refs = refs[11 + N_TEST : 13 + N_TEST]
+    last_refs = refs[13 + N_TEST : 15 + N_TEST]
+    piece_refs = refs[15 + N_TEST : 15 + 2 * N_TEST]
+    image_sem, readout_sem, piece_sem = refs[15 + 2 * N_TEST :]
     my_xh = lax.axis_index("xh")
     my_y = lax.axis_index("y")
-    shard = my_xh * N_Y + my_y
-
-    for variant in range(MUT_DEV):
+
+    def fetch(variant):
         for entry in range(SURV):
-            wanted = wanted_ref[variant, entry]
-            holder = wanted // IMG_DEV
-            within = wanted % IMG_DEV
-            slot = jnp.where(holder // 16 != my_xl, 1, 0)
-            start = (
-                ((holder % 16) * 2 + slot) * (IMG_DEV * PIX)
-                + (within // 2) * (2 * PIX)
-                + (within % 2) * 24
-            )
+            start = pl.multiple_of(plan_ref[0, variant * SURV + entry], 8)
             pltpu.make_async_copy(
-                images_ref.at[pl.ds(pl.multiple_of(start, 8), SLOT)],
+                images_ref.at[pl.ds(start, SLOT)],
                 x_ref.at[variant, pl.ds(entry * SLOT, SLOT)],
                 image_sem.at[variant],
             ).start()
+
+    piece_copies = []
+    for number in range(N_TEST):
+        copy = pltpu.make_async_copy(
+            piece_hbm_refs[number], piece_refs[number], piece_sem.at[number]
+        )
+        copy.start()
+        piece_copies.append(copy)
+    for variant in range(MUT_DEV):
+        fetch(variant)
     pltpu.make_async_copy(readout_hbm_ref, readout_ref, readout_sem).start()
 
     rows_of = []
@@ -69,11 +69,13 @@
     def build(member):
         for number in range(N_TEST):
             row = rows_of[number]
+            if member == 0:
+                piece_copies[number].wait()
             for kind in range(2):
                 base = base_ref[kind, pl.ds(row, CHUNK), :].astype(jnp.float32)
-                change = pieces[number][member, kind].astype(jnp.float32)
+                change = piece_refs[number][member, kind].astype(jnp.float32)
                 for step in range(STEPS):
-                    value = (base + strength_ref[step, member] * change).astype(jnp.bfloat16)
+                    value = (base + strength_ref[0, step * MUT_DEV + member] * change).astype(jnp.bfloat16)
                     if kind == 0:
                         first_refs[member % 2][pl.ds(row, CHUNK), step * B : (step + 1) * B] = value
                     else:
@@ -85,12 +87,10 @@
     sublane = lax.broadcasted_iota(jnp.int32, (8, B), 0)
     for variant in range(MUT_DEV):
         for entry in range(SURV):
-            wanted = wanted_ref[variant, entry]
-            within = wanted % IMG_DEV
-            odd = within % 2
+            odd = plan_ref[1, variant * SURV + entry]
             keep_ref[variant, 0, entry] = jnp.where(sublane >= odd * 4, 1.0, 0.0)
             keep_ref[variant, 1, entry] = jnp.where(sublane < 4 + odd * 4, 1.0, 0.0)
-            label = class_ref[((wanted // IMG_DEV) * N_TEST + shard) * IMG_DEV + within]
+            label = plan_ref[2, variant * SURV + entry]
             for step in range(STEPS):
                 row = (variant * STEPS + step) * 16 + entry
                 label_ref[row : row + 1, :] = jnp.full((1, 128), label, jnp.int32)
@@ -170,36 +170,60 @@
     message = jnp.stack(
         [narrowing_perturbation, jnp.transpose(widening_perturbation, (0, 2, 1))], axis=1
     )
-    own_rows, message = lax.optimization_barrier((own_rows, message))
     partner_rows = lax.ppermute(own_rows, "xl", swap)
-    first_up = lax.ppermute(message, "y", up)
-    partner_rows, first_up = lax.optimization_barrier((partner_rows, first_up))
     images = lax.all_gather(
         jnp.concatenate([own_rows, partner_rows]), ("z", "core"), axis=0, tiled=True
     )
 
     other = lax.ppermute(message, "xh", swap)
-    flows = []
-    for number, seed in enumerate((message, other)):
-        rising = [first_up if number == 0 else lax.ppermute(seed, "y", up)]
-        falling = [lax.ppermute(seed, "y", down)]
-        for _ in range(2):
-            rising.append(lax.ppermute(rising[-1], "y", up))
-            falling.append(lax.ppermute(falling[-1], "y", down))
-        if number == 0:
-            farthest = lax.ppermute(rising[-1], "y", up)
-        else:
-            farthest = lax.ppermute(falling[-1], "y", down)
-        flows.append([seed] + rising + falling + [farthest])
-    pieces = [flows[number % 2][number // 2] for number in range(N_TEST)]
-
+
+    wanted = remaining_pictures.reshape(1, -1)
+    holder = wanted // IMG_DEV
+    within = wanted % IMG_DEV
+    slot = (holder // 16 != lax.axis_index("xl")).astype(jnp.int32)
+    start = (
+        ((holder % 16) * 2 + slot) * (IMG_DEV * PIX) + (within // 2) * (2 * PIX) + (within % 2) * 24
+    )
+    shard = lax.axis_index("xh") * N_Y + lax.axis_index("y")
+    label = jnp.take(ground_truth_class, (holder * N_TEST + shard) * IMG_DEV + within)
+    plan = jnp.concatenate([start, within % 2, label])
+    strength = jnp.pad(perturbation_strength.T.reshape(1, -1), ((0, 0), (0, 120)))
     bases = jnp.stack([learned_narrowing_kernel, learned_widening_kernel.T])
+    other, plan, strength, bases = lax.optimization_barrier((other, plan, strength, bases))
+
+    up_1 = lax.ppermute(message, "y", up)
+    down_1 = lax.ppermute(message, "y", down)
+    up_2 = lax.ppermute(up_1, "y", up)
+    down_2 = lax.ppermute(down_1, "y", down)
+    up_3 = lax.ppermute(up_2, "y", up)
+    down_3 = lax.ppermute(down_2, "y", down)
+    up_4 = lax.ppermute(up_3, "y", up)
+    other_up_1 = lax.ppermute(up_1, "xh", swap)
+    other_down_1 = lax.ppermute(down_1, "xh", swap)
+    other_up_2 = lax.ppermute(up_2, "xh", swap)
+    other_down_2 = lax.ppermute(down_2, "xh", swap)
+    other_up_3 = lax.ppermute(other_up_2, "y", up)
+    other_down_3 = lax.ppermute(other_down_2, "y", down)
+    other_4 = lax.ppermute(other_down_3, "y", down)
+    near = [message, up_1, up_2, up_3, down_1, down_2, down_3, up_4]
+    far = [
+        other,
+        other_up_1,
+        other_up_2,
+        other_up_3,
+        other_down_1,
+        other_down_2,
+        other_down_3,
+        other_4,
+    ]
+    pieces = [(near, far)[number % 2][number // 2] for number in range(N_TEST)]
+
     smem = pl.BlockSpec(memory_space=pltpu.SMEM)
     vmem = pl.BlockSpec(memory_space=pltpu.VMEM)
     hbm = pl.BlockSpec(memory_space=pl.ANY)
     return pl.pallas_call(
         score,
-        in_specs=[smem, smem, smem, hbm, hbm, vmem] + [vmem] * N_TEST,
+        in_specs=[smem, smem, hbm, hbm, vmem] + [hbm] * N_TEST,
         out_specs=vmem,
         out_shape=jax.ShapeDtypeStruct((MUT_DEV, STEPS, SURV), jnp.float32),
         scratch_shapes=[
@@ -212,18 +236,21 @@
             pltpu.VMEM((C, STEPS * B), jnp.bfloat16),
             pltpu.VMEM((STEPS, C, B), jnp.bfloat16),
             pltpu.VMEM((STEPS, C, B), jnp.bfloat16),
+        ]
+        + [pltpu.VMEM((MUT_DEV, 2, CHUNK, B), jnp.bfloat16)] * N_TEST
+        + [
             pltpu.SemaphoreType.DMA((MUT_DEV,)),
             pltpu.SemaphoreType.DMA,
+            pltpu.SemaphoreType.DMA((N_TEST,)),
         ],
-        compiler_params=pltpu.CompilerParams(vmem_limit_bytes=24 * 2**20),
+        compiler_params=pltpu.CompilerParams(vmem_limit_bytes=30 * 2**20),
     )(
-        remaining_pictures,
-        ground_truth_class,
-        perturbation_strength.T,
+        plan,
+        strength,
         in_hbm(images),
         in_hbm(readout_matrix.T),
         in_vmem(bases),
-        *[in_vmem(value) for value in pieces],
+        *[in_hbm(value) for value in pieces],
     )
 
 

time: 106 us -> 107 us (level)
  starting transfers between devices: 51.5 us -> 56.4 us
  waiting for transfers between devices: 18.3 us -> 13.5 us
    ppermute x1, waiting for transfers between devices: 7.84 us -> 0.01 us  [on_device(): other = lax.ppermute(message, 'xh', swap)]
    ppermute x14, waiting for transfers between devices: 4.48 us -> 7.64 us  [the longest x1 2.62 us: on_device(): down_1 = lax.ppermute(message, 'y', down)]
    ppermute x14, starting transfers between devices: 47.7 us -> 50.6 us  [the longest x1 5.13 us: on_device(): other_up_3 = lax.ppermute(other_up_2, 'y', up)]
    unnamed x8 -> x20, local copies, waits for them, and re-layouts: 5.12 us -> 2.3 us
    reshape x0 -> x3, local copies, waits for them, and re-layouts: none -> 2.31 us  [the longest x2 1.55 us: on_device(): wanted = remaining_pictures.reshape(1, -1)]
    ppermute x1, starting transfers between devices: 1.92 us -> 3.4 us  [on_device(): partner_rows = lax.ppermute(own_rows, 'xl', swap)]
  transfers between devices with their start and end apart: 17 -> 17, of which waited for: 3 -> 4; matrix products, arithmetic and copies ran while one was open for 3% -> 6% of each run, Pallas kernels for 0% -> 0%
where the time goes in v4:
time: 107 us; the launch traced here: 106 us
  starting transfers between devices  56.4 us (53%)
  between operations  13.8 us (13%)
  Pallas kernels  13.7 us (13%)
  waiting for transfers between devices  13.5 us (13%)
  local copies, waits for them, and re-layouts  5.44 us (5%)
  other arithmetic  3.01 us (3%)
    pallas_call x1, Pallas kernels, on_device(): pl.pallas_call(score, in_specs=[smem, smem, hbm, hbm, vmem] + [hbm] * N_T...  13.7 us
    ppermute x1, waiting for transfers between devices, on_device(): partner_rows = lax.ppermute(own_rows, 'xl', swap)  5.83 us
    ppermute x1, starting transfers between devices, on_device(): other_up_3 = lax.ppermute(other_up_2, 'y', up)  5.13 us
    ppermute x1, starting transfers between devices, on_device(): up_2 = lax.ppermute(up_1, 'y', up)  5.01 us
    ppermute x1, starting transfers between devices, on_device(): other_down_1 = lax.ppermute(down_1, 'xh', swap)  4.92 us
    ppermute x1, starting transfers between devices, on_device(): other_up_1 = lax.ppermute(up_1, 'xh', swap)  4.92 us
    ppermute x1, starting transfers between devices, on_device(): other_down_2 = lax.ppermute(down_2, 'xh', swap)  4.92 us
    ppermute x1, starting transfers between devices, on_device(): up_1 = lax.ppermute(message, 'y', up)  4.39 us
  transfers between devices with their start and end apart: 17, of which 4 were waited for; matrix products, arithmetic and copies ran while one was open for 6% of the time, Pallas kernels for 0%

profile of v4, /device:TPU:56, one launch (start us, length us, event | category | flops | bytes accessed | tf_op | source)
XLA Modules:
  0.0 105.9 jit_solution(4396358421200520895)
XLA Ops:
  6.5 0.0 copy-start
  6.5 0.0 all-gather.2.cloned.1.call-start
  6.5 1.0 copy.13
  7.6 3.4 %collective-permute-start.1 = (bf16[112,1024]{1,0:T(8,128)(2,1)S(1)}, bf16[112,1024]{1,0:T(8,128)(2,1)S(1)}, u32[]{:S(2)}, u32[]{:S(2)}) collective-permute-start(bf16[112,1024]{1,0:T(8,128)(2,1)S(1)} %reshape.632), channel_id=1, source_target_pairs={{0,256},{256,0},{1,257},{257,1},{2,258},{258,2},{3,259},{259,3},{4... | collective-permute-start | bytes 688136 | tf_op jit(solution)/shard_map/ppermute | solution.py:173
  11.0 5.8 %collective-permute-done.1 = bf16[112,1024]{1,0:T(8,128)(2,1)S(1)} collective-permute-done((bf16[112,1024]{1,0:T(8,128)(2,1)S(1)}, bf16[112,1024]{1,0:T(8,128)(2,1)S(1)}, u32[]{:S(2)}, u32[]{:S(2)}) %collective-permute-start.1) | collective-permute-done | bytes 229408 | tf_op jit(solution)/shard_map/ppermute | solution.py:173
  16.9 0.8 pad_maximum_fusion.1
  17.7 0.0 all-gather.2.cloned.1.call-update
  17.7 1.0 pad_maximum_fusion.2.refs_5_
  18.7 0.0 copy-start.1
  18.7 3.3 %collective-permute-start.8 = (bf16[4,2,64,256]{3,2,1,0:T(8,128)(2,1)S(1)}, bf16[4,2,64,256]{3,2,1,0:T(8,128)(2,1)S(1)}, u32[]{:S(2)}, u32[]{:S(2)}) collective-permute-start(bf16[4,2,64,256]{3,2,1,0:T(8,128)(2,1)S(1)} %pad_maximum_fusion.2.refs_5_), channel_id=1, source_target_pairs={{0,7},{1,0},{2,1},{3,2},{4,3},{5,4},{6,5},{7,6},{8,15},{9,8},{10,9... | collective-permute-start | bytes 786440 | tf_op jit(solution)/shard_map/ppermute | solution.py:195
  22.0 4.4 %collective-permute-start.2 = (bf16[4,2,64,256]{3,2,1,0:T(8,128)(2,1)S(1)}, bf16[4,2,64,256]{3,2,1,0:T(8,128)(2,1)S(1)}, u32[]{:S(2)}, u32[]{:S(2)}) collective-permute-start(bf16[4,2,64,256]{3,2,1,0:T(8,128)(2,1)S(1)} %pad_maximum_fusion.2.refs_5_), channel_id=1, source_target_pairs={{0,1},{1,2},{2,3},{3,4},{4,5},{5,6},{6,7},{7,0},{8,9},{9,10},{10,1... | collective-permute-start | bytes 786440 | tf_op jit(solution)/shard_map/ppermute | solution.py:194
  26.4 2.6 %collective-permute-done.8.refs_13_ = bf16[4,2,64,256]{3,2,1,0:T(8,128)(2,1)S(1)} collective-permute-done((bf16[4,2,64,256]{3,2,1,0:T(8,128)(2,1)S(1)}, bf16[4,2,64,256]{3,2,1,0:T(8,128)(2,1)S(1)}, u32[]{:S(2)}, u32[]{:S(2)}) %collective-permute-start.8) | collective-permute-done | bytes 262176 | tf_op jit(solution)/shard_map/ppermute | solution.py:195
  29.0 0.0 copy-start.2
  29.0 2.0 %collective-permute-start.10 = (bf16[4,2,64,256]{3,2,1,0:T(8,128)(2,1)S(1)}, bf16[4,2,64,256]{3,2,1,0:T(8,128)(2,1)S(1)}, u32[]{:S(2)}, u32[]{:S(2)}) collective-permute-start(bf16[4,2,64,256]{3,2,1,0:T(8,128)(2,1)S(1)} %collective-permute-done.8.refs_13_), channel_id=1, source_target_pairs={{0,7},{1,0},{2,1},{3,2},{4,3},{5,4},{6,5},{7,6},{8,15},{9,8},{10,9... | collective-permute-start | bytes 786440 | tf_op jit(solution)/shard_map/ppermute | solution.py:197
  31.0 0.0 collective-permute-done.2.refs_7_
  31.0 0.0 copy-start.3
  31.0 5.0 %collective-permute-start.4 = (bf16[4,2,64,256]{3,2,1,0:T(8,128)(2,1)S(1)}, bf16[4,2,64,256]{3,2,1,0:T(8,128)(2,1)S(1)}, u32[]{:S(2)}, u32[]{:S(2)}) collective-permute-start(bf16[4,2,64,256]{3,2,1,0:T(8,128)(2,1)S(1)} %collective-permute-done.2.refs_7_), channel_id=1, source_target_pairs={{0,1},{1,2},{2,3},{3,4},{4,5},{5,6},{6,7},{7,0},{8,9},{9,10},{10,1... | collective-permute-start | bytes 786440 | tf_op jit(solution)/shard_map/ppermute | solution.py:196
  36.1 2.4 %collective-permute-done.10.refs_15_ = bf16[4,2,64,256]{3,2,1,0:T(8,128)(2,1)S(1)} collective-permute-done((bf16[4,2,64,256]{3,2,1,0:T(8,128)(2,1)S(1)}, bf16[4,2,64,256]{3,2,1,0:T(8,128)(2,1)S(1)}, u32[]{:S(2)}, u32[]{:S(2)}) %collective-permute-start.10) | collective-permute-done | bytes 262176 | tf_op jit(solution)/shard_map/ppermute | solution.py:197
  38.4 0.0 copy-start.4
  38.4 4.9 %collective-permute-start.11 = (bf16[4,2,64,256]{3,2,1,0:T(8,128)(2,1)S(1)}, bf16[4,2,64,256]{3,2,1,0:T(8,128)(2,1)S(1)}, u32[]{:S(2)}, u32[]{:S(2)}) collective-permute-start(bf16[4,2,64,256]{3,2,1,0:T(8,128)(2,1)S(1)} %collective-permute-done.10.refs_15_), channel_id=1, source_target_pairs={{0,8},{8,0},{1,9},{9,1},{2,10},{10,2},{3,11},{11,3},{4,12},{12,4},... | collective-permute-start | bytes 786440 | tf_op jit(solution)/shard_map/ppermute | solution.py:204
  43.4 2.4 %collective-permute-start = (bf16[4,2,64,256]{3,2,1,0:T(8,128)(2,1)S(1)}, bf16[4,2,64,256]{3,2,1,0:T(8,128)(2,1)S(1)}, u32[]{:S(2)}, u32[]{:S(2)}) collective-permute-start(bf16[4,2,64,256]{3,2,1,0:T(8,128)(2,1)S(1)} %pad_maximum_fusion.2.refs_5_), channel_id=1, source_target_pairs={{0,8},{8,0},{1,9},{9,1},{2,10},{10,2},{3,11},{11,3},{4,12},{12,4},... | collective-permute-start | bytes 786440 | tf_op jit(solution)/shard_map/ppermute | solution.py:178
  45.8 0.8 reshape.630
  46.6 4.9 %collective-permute-start.3 = (bf16[4,2,64,256]{3,2,1,0:T(8,128)(2,1)S(1)}, bf16[4,2,64,256]{3,2,1,0:T(8,128)(2,1)S(1)}, u32[]{:S(2)}, u32[]{:S(2)}) collective-permute-start(bf16[4,2,64,256]{3,2,1,0:T(8,128)(2,1)S(1)} %collective-permute-done.2.refs_7_), channel_id=1, source_target_pairs={{0,8},{8,0},{1,9},{9,1},{2,10},{10,2},{3,11},{11,3},{4,12},{12,4},... | collective-permute-start | bytes 786440 | tf_op jit(solution)/shard_map/ppermute | solution.py:201
  51.5 0.0 collective-permute-done.4.refs_9_
  51.5 0.0 copy-start.5
  51.6 2.4 %collective-permute-start.5 = (bf16[4,2,64,256]{3,2,1,0:T(8,128)(2,1)S(1)}, bf16[4,2,64,256]{3,2,1,0:T(8,128)(2,1)}, u32[]{:S(2)}, u32[]{:S(2)}) collective-permute-start(bf16[4,2,64,256]{3,2,1,0:T(8,128)(2,1)S(1)} %collective-permute-done.4.refs_9_), channel_id=1, source_target_pairs={{0,8},{8,0},{1,9},{9,1},{2,10},{10,2},{3,11},{11,3},{4,12},{12,4},... | collective-permute-start | bytes 786440 | tf_op jit(solution)/shard_map/ppermute | solution.py:203
  54.0 2.9 %collective-permute-start.6 = (bf16[4,2,64,256]{3,2,1,0:T(8,128)(2,1)S(1)}, bf16[4,2,64,256]{3,2,1,0:T(8,128)(2,1)}, u32[]{:S(2)}, u32[]{:S(2)}) collective-permute-start(bf16[4,2,64,256]{3,2,1,0:T(8,128)(2,1)S(1)} %collective-permute-done.4.refs_9_), channel_id=1, source_target_pairs={{0,1},{1,2},{2,3},{3,4},{4,5},{5,6},{6,7},{7,0},{8,9},{9,10},{10,1... | collective-permute-start | bytes 786440 | tf_op jit(solution)/shard_map/ppermute | solution.py:198
  56.9 0.0 collective-permute-done.11.refs_16_
  56.9 0.0 copy-start.6
  56.9 2.9 %collective-permute-start.13 = (bf16[4,2,64,256]{3,2,1,0:T(8,128)(2,1)S(1)}, bf16[4,2,64,256]{3,2,1,0:T(8,128)(2,1)}, u32[]{:S(2)}, u32[]{:S(2)}) collective-permute-start(bf16[4,2,64,256]{3,2,1,0:T(8,128)(2,1)S(1)} %collective-permute-done.11.refs_16_), channel_id=1, source_target_pairs={{0,7},{1,0},{2,1},{3,2},{4,3},{5,4},{6,5},{7,6},{8,15},{9,8},{10,9... | collective-permute-start | bytes 786440 | tf_op jit(solution)/shard_map/ppermute | solution.py:206
  59.9 0.8 reshape.629
  60.6 0.0 copy-done
  60.7 0.8 gather_fusion
  61.5 0.0 collective-permute-done.refs_6_
  61.5 0.0 copy-start.7
  61.5 4.9 %collective-permute-start.9 = (bf16[4,2,64,256]{3,2,1,0:T(8,128)(2,1)S(1)}, bf16[4,2,64,256]{3,2,1,0:T(8,128)(2,1)}, u32[]{:S(2)}, u32[]{:S(2)}) collective-permute-start(bf16[4,2,64,256]{3,2,1,0:T(8,128)(2,1)S(1)} %collective-permute-done.8.refs_13_), channel_id=1, source_target_pairs={{0,8},{8,0},{1,9},{9,1},{2,10},{10,2},{3,11},{11,3},{4,12},{12,4},... | collective-permute-start | bytes 786440 | tf_op jit(solution)/shard_map/ppermute | solution.py:202
  66.4 0.0 collective-permute-done.3.refs_8_
  66.4 0.0 copy-start.8
  66.4 1.9 %collective-permute-start.12 = (bf16[4,2,64,256]{3,2,1,0:T(8,128)(2,1)S(1)}, bf16[4,2,64,256]{3,2,1,0:T(8,128)(2,1)}, u32[]{:S(2)}, u32[]{:S(2)}) collective-permute-start(bf16[4,2,64,256]{3,2,1,0:T(8,128)(2,1)S(1)} %collective-permute-done.10.refs_15_), channel_id=1, source_target_pairs={{0,7},{1,0},{2,1},{3,2},{4,3},{5,4},{6,5},{7,6},{8,15},{9,8},{10,9... | collective-permute-start | bytes 786440 | tf_op jit(solution)/shard_map/ppermute | solution.py:199
  68.4 0.0 collective-permute-done.5.refs_10_
  68.4 5.1 %collective-permute-start.7 = (bf16[4,2,64,256]{3,2,1,0:T(8,128)(2,1)}, bf16[4,2,64,256]{3,2,1,0:T(8,128)(2,1)}, u32[]{:S(2)}, u32[]{:S(2)}) collective-permute-start(bf16[4,2,64,256]{3,2,1,0:T(8,128)(2,1)} %collective-permute-done.5.refs_10_), channel_id=1, source_target_pairs={{0,1},{1,2},{2,3},{3,4},{4,5},{5,6},{6,7},{7,0},{8,9},{9,10},{10,1... | collective-permute-start | bytes 786440 | tf_op jit(solution)/shard_map/ppermute | solution.py:205
  73.5 0.0 collective-permute-done.6.refs_11_
  73.5 1.9 %collective-permute-start.14 = (bf16[4,2,64,256]{3,2,1,0:T(8,128)(2,1)}, bf16[4,2,64,256]{3,2,1,0:T(8,128)(2,1)}, u32[]{:S(2)}, u32[]{:S(2)}) collective-permute-start(bf16[4,2,64,256]{3,2,1,0:T(8,128)(2,1)} %collective-permute-done.6.refs_11_), channel_id=1, source_target_pairs={{0,1},{1,2},{2,3},{3,4},{4,5},{5,6},{6,7},{7,0},{8,9},{9,10},{10,1... | collective-permute-start | bytes 786440 | tf_op jit(solution)/shard_map/ppermute | solution.py:200
  75.4 0.0 collective-permute-done.13.refs_18_
  75.5 3.9 %collective-permute-start.15 = (bf16[4,2,64,256]{3,2,1,0:T(8,128)(2,1)}, bf16[4,2,64,256]{3,2,1,0:T(8,128)(2,1)}, u32[]{:S(2)}, u32[]{:S(2)}) collective-permute-start(bf16[4,2,64,256]{3,2,1,0:T(8,128)(2,1)} %collective-permute-done.13.refs_18_), channel_id=1, source_target_pairs={{0,7},{1,0},{2,1},{3,2},{4,3},{5,4},{6,5},{7,6},{8,15},{9,8},{10,9... | collective-permute-start | bytes 786440 | tf_op jit(solution)/shard_map/ppermute | solution.py:207
  79.4 0.8 reshape.631
  80.2 1.2 %copy.12 = bf16[256,1024]{0,1:T(8,128)(2,1)S(1)} copy(bf16[256,1024]{1,0:T(8,128)(2,1)} %param.13) | data formatting | bytes 1048576 | tf_op args[4]
  81.4 0.0 copy-done.8
  81.5 1.1 %pad_maximum_fusion.refs_4_ = bf16[2,1024,256]{2,1,0:T(8,128)(2,1)S(1)} fusion(bf16[1,1024,256]{2,1,0:T(8,128)(2,1)S(1)} %bitcast.14, bf16[1,1024,256]{2,1,0:T(8,128)(2,1)} %bitcast.16), kind=kLoop, calls=%fused_computation.1 | loop fusion | flops 524288 | bytes 2097152 | tf_op jit(solution)/shard_map/stack | solution.py:191
  82.6 0.0 collective-permute-done.9.refs_14_
  82.6 0.0 collective-permute-done.12.refs_17_
  82.6 0.0 collective-permute-done.7.refs_12_
  82.6 0.0 collective-permute-done.14.refs_19_
  82.6 2.6 %collective-permute-done.15.refs_20_ = bf16[4,2,64,256]{3,2,1,0:T(8,128)(2,1)} collective-permute-done((bf16[4,2,64,256]{3,2,1,0:T(8,128)(2,1)}, bf16[4,2,64,256]{3,2,1,0:T(8,128)(2,1)}, u32[]{:S(2)}, u32[]{:S(2)}) %collective-permute-start.15) | collective-permute-done | bytes 262176 | tf_op jit(solution)/shard_map/ppermute | solution.py:207
  85.2 0.0 all-gather.2.cloned.1.call-done.refs_2_
  85.3 0.0 copy-done.1
  85.3 0.0 copy-done.2
  85.3 0.0 copy-done.3
  85.3 0.0 copy-done.4
  85.3 0.0 copy-done.5
  85.3 0.0 copy-done.6
  85.3 0.0 copy-done.7
  85.3 13.7 %shard_map.91 = f32[4,2,14]{2,1,0:T(2,128)} custom-call(s32[3,56]{1,0:T(4,128)S(1)} %pad_add_fusion.refs_0_, f32[1,128]{1,0:T(1,128)S(1)} %pad.4.refs_1_, bf16[3584,1024]{1,0:T(8,128)(2,1)} %all-gather.2.cloned.1.call-done.refs_2_, bf16[1000,1024]{1,0:T(8,128)(2,1)} %bitcast.15, bf16[2,1024,256]{2,1,0:T(8,128)(2,1)S(1)} %pad_maximum_fusion.refs_4_, ...), custom_call_target="tpu_custom_call" | custom-call | tf_op jit(solution)/shard_map/pallas_call | solution.py:224
  (7 shorter events, 0.1 us)
Async XLA Ops:
  6.5 54.1 %copy-start = (s32[2048]{0:T(1024)S(1)}, s32[2048]{0:T(1024)}, u32[]{:S(2)}) copy-start(s32[2048]{0:T(1024)} %param.10) | copy-start | bytes 24580
  6.5 78.7 %all-gather.2.cloned.1.call-start = ((), (), s32[]{:S(2)}) async-start(), calls=%async_computation | async-start | bytes 7798784 | tf_op jit(solution)/shard_map/all_gather | solution.py:174
  7.6 9.2 %collective-permute-start.1 = (bf16[112,1024]{1,0:T(8,128)(2,1)S(1)}, bf16[112,1024]{1,0:T(8,128)(2,1)S(1)}, u32[]{:S(2)}, u32[]{:S(2)}) collective-permute-start(bf16[112,1024]{1,0:T(8,128)(2,1)S(1)} %reshape.632), channel_id=1, source_target_pairs={{0,256},{256,0},{1,257},{257,1},{2,258},{258,2},{3,259},{259,3},{4... | collective-permute-start | bytes 688136 | tf_op jit(solution)/shard_map/ppermute | solution.py:173
  18.7 66.6 %copy-start.1 = (bf16[4,2,64,256]{3,2,1,0:T(8,128)(2,1)}, bf16[4,2,64,256]{3,2,1,0:T(8,128)(2,1)S(1)}, u32[]{:S(2)}) copy-start(bf16[4,2,64,256]{3,2,1,0:T(8,128)(2,1)S(1)} %pad_maximum_fusion.2.refs_5_) | copy-start | bytes 786436
  18.7 10.3 %collective-permute-start.8 = (bf16[4,2,64,256]{3,2,1,0:T(8,128)(2,1)S(1)}, bf16[4,2,64,256]{3,2,1,0:T(8,128)(2,1)S(1)}, u32[]{:S(2)}, u32[]{:S(2)}) collective-permute-start(bf16[4,2,64,256]{3,2,1,0:T(8,128)(2,1)S(1)} %pad_maximum_fusion.2.refs_5_), channel_id=1, source_target_pairs={{0,7},{1,0},{2,1},{3,2},{4,3},{5,4},{6,5},{7,6},{8,15},{9,8},{10,9... | collective-permute-start | bytes 786440 | tf_op jit(solution)/shard_map/ppermute | solution.py:195
  22.0 9.1 %collective-permute-start.2 = (bf16[4,2,64,256]{3,2,1,0:T(8,128)(2,1)S(1)}, bf16[4,2,64,256]{3,2,1,0:T(8,128)(2,1)S(1)}, u32[]{:S(2)}, u32[]{:S(2)}) collective-permute-start(bf16[4,2,64,256]{3,2,1,0:T(8,128)(2,1)S(1)} %pad_maximum_fusion.2.refs_5_), channel_id=1, source_target_pairs={{0,1},{1,2},{2,3},{3,4},{4,5},{5,6},{6,7},{7,0},{8,9},{9,10},{10,1... | collective-permute-start | bytes 786440 | tf_op jit(solution)/shard_map/ppermute | solution.py:194
  29.0 56.3 %copy-start.2 = (bf16[4,2,64,256]{3,2,1,0:T(8,128)(2,1)}, bf16[4,2,64,256]{3,2,1,0:T(8,128)(2,1)S(1)}, u32[]{:S(2)}) copy-start(bf16[4,2,64,256]{3,2,1,0:T(8,128)(2,1)S(1)} %collective-permute-done.8.refs_13_) | copy-start | bytes 786436
  29.0 9.5 %collective-permute-start.10 = (bf16[4,2,64,256]{3,2,1,0:T(8,128)(2,1)S(1)}, bf16[4,2,64,256]{3,2,1,0:T(8,128)(2,1)S(1)}, u32[]{:S(2)}, u32[]{:S(2)}) collective-permute-start(bf16[4,2,64,256]{3,2,1,0:T(8,128)(2,1)S(1)} %collective-permute-done.8.refs_13_), channel_id=1, source_target_pairs={{0,7},{1,0},{2,1},{3,2},{4,3},{5,4},{6,5},{7,6},{8,15},{9,8},{10,9... | collective-permute-start | bytes 786440 | tf_op jit(solution)/shard_map/ppermute | solution.py:197
  31.0 54.2 %copy-start.3 = (bf16[4,2,64,256]{3,2,1,0:T(8,128)(2,1)}, bf16[4,2,64,256]{3,2,1,0:T(8,128)(2,1)S(1)}, u32[]{:S(2)}) copy-start(bf16[4,2,64,256]{3,2,1,0:T(8,128)(2,1)S(1)} %collective-permute-done.2.refs_7_) | copy-start | bytes 786436
  31.0 20.5 %collective-permute-start.4 = (bf16[4,2,64,256]{3,2,1,0:T(8,128)(2,1)S(1)}, bf16[4,2,64,256]{3,2,1,0:T(8,128)(2,1)S(1)}, u32[]{:S(2)}, u32[]{:S(2)}) collective-permute-start(bf16[4,2,64,256]{3,2,1,0:T(8,128)(2,1)S(1)} %collective-permute-done.2.refs_7_), channel_id=1, source_target_pairs={{0,1},{1,2},{2,3},{3,4},{4,5},{5,6},{6,7},{7,0},{8,9},{9,10},{10,1... | collective-permute-start | bytes 786440 | tf_op jit(solution)/shard_map/ppermute | solution.py:196
  38.4 46.8 %copy-start.4 = (bf16[4,2,64,256]{3,2,1,0:T(8,128)(2,1)}, bf16[4,2,64,256]{3,2,1,0:T(8,128)(2,1)S(1)}, u32[]{:S(2)}) copy-start(bf16[4,2,64,256]{3,2,1,0:T(8,128)(2,1)S(1)} %collective-permute-done.10.refs_15_) | copy-start | bytes 786436
  38.4 18.5 %collective-permute-start.11 = (bf16[4,2,64,256]{3,2,1,0:T(8,128)(2,1)S(1)}, bf16[4,2,64,256]{3,2,1,0:T(8,128)(2,1)S(1)}, u32[]{:S(2)}, u32[]{:S(2)}) collective-permute-start(bf16[4,2,64,256]{3,2,1,0:T(8,128)(2,1)S(1)} %collective-permute-done.10.refs_15_), channel_id=1, source_target_pairs={{0,8},{8,0},{1,9},{9,1},{2,10},{10,2},{3,11},{11,3},{4,12},{12,4},... | collective-permute-start | bytes 786440 | tf_op jit(solution)/shard_map/ppermute | solution.py:204
  43.4 18.1 %collective-permute-start = (bf16[4,2,64,256]{3,2,1,0:T(8,128)(2,1)S(1)}, bf16[4,2,64,256]{3,2,1,0:T(8,128)(2,1)S(1)}, u32[]{:S(2)}, u32[]{:S(2)}) collective-permute-start(bf16[4,2,64,256]{3,2,1,0:T(8,128)(2,1)S(1)} %pad_maximum_fusion.2.refs_5_), channel_id=1, source_target_pairs={{0,8},{8,0},{1,9},{9,1},{2,10},{10,2},{3,11},{11,3},{4,12},{12,4},... | collective-permute-start | bytes 786440 | tf_op jit(solution)/shard_map/ppermute | solution.py:178
  46.6 19.8 %collective-permute-start.3 = (bf16[4,2,64,256]{3,2,1,0:T(8,128)(2,1)S(1)}, bf16[4,2,64,256]{3,2,1,0:T(8,128)(2,1)S(1)}, u32[]{:S(2)}, u32[]{:S(2)}) collective-permute-start(bf16[4,2,64,256]{3,2,1,0:T(8,128)(2,1)S(1)} %collective-permute-done.2.refs_7_), channel_id=1, source_target_pairs={{0,8},{8,0},{1,9},{9,1},{2,10},{10,2},{3,11},{11,3},{4,12},{12,4},... | collective-permute-start | bytes 786440 | tf_op jit(solution)/shard_map/ppermute | solution.py:201
  51.5 33.7 %copy-start.5 = (bf16[4,2,64,256]{3,2,1,0:T(8,128)(2,1)}, bf16[4,2,64,256]{3,2,1,0:T(8,128)(2,1)S(1)}, u32[]{:S(2)}) copy-start(bf16[4,2,64,256]{3,2,1,0:T(8,128)(2,1)S(1)} %collective-permute-done.4.refs_9_) | copy-start | bytes 786436
  51.6 16.8 %collective-permute-start.5 = (bf16[4,2,64,256]{3,2,1,0:T(8,128)(2,1)S(1)}, bf16[4,2,64,256]{3,2,1,0:T(8,128)(2,1)}, u32[]{:S(2)}, u32[]{:S(2)}) collective-permute-start(bf16[4,2,64,256]{3,2,1,0:T(8,128)(2,1)S(1)} %collective-permute-done.4.refs_9_), channel_id=1, source_target_pairs={{0,8},{8,0},{1,9},{9,1},{2,10},{10,2},{3,11},{11,3},{4,12},{12,4},... | collective-permute-start | bytes 786440 | tf_op jit(solution)/shard_map/ppermute | solution.py:203
  54.0 19.5 %collective-permute-start.6 = (bf16[4,2,64,256]{3,2,1,0:T(8,128)(2,1)S(1)}, bf16[4,2,64,256]{3,2,1,0:T(8,128)(2,1)}, u32[]{:S(2)}, u32[]{:S(2)}) collective-permute-start(bf16[4,2,64,256]{3,2,1,0:T(8,128)(2,1)S(1)} %collective-permute-done.4.refs_9_), channel_id=1, source_target_pairs={{0,1},{1,2},{2,3},{3,4},{4,5},{5,6},{6,7},{7,0},{8,9},{9,10},{10,1... | collective-permute-start | bytes 786440 | tf_op jit(solution)/shard_map/ppermute | solution.py:198
  56.9 28.4 %copy-start.6 = (bf16[4,2,64,256]{3,2,1,0:T(8,128)(2,1)}, bf16[4,2,64,256]{3,2,1,0:T(8,128)(2,1)S(1)}, u32[]{:S(2)}) copy-start(bf16[4,2,64,256]{3,2,1,0:T(8,128)(2,1)S(1)} %collective-permute-done.11.refs_16_) | copy-start | bytes 786436
  56.9 18.5 %collective-permute-start.13 = (bf16[4,2,64,256]{3,2,1,0:T(8,128)(2,1)S(1)}, bf16[4,2,64,256]{3,2,1,0:T(8,128)(2,1)}, u32[]{:S(2)}, u32[]{:S(2)}) collective-permute-start(bf16[4,2,64,256]{3,2,1,0:T(8,128)(2,1)S(1)} %collective-permute-done.11.refs_16_), channel_id=1, source_target_pairs={{0,7},{1,0},{2,1},{3,2},{4,3},{5,4},{6,5},{7,6},{8,15},{9,8},{10,9... | collective-permute-start | bytes 786440 | tf_op jit(solution)/shard_map/ppermute | solution.py:206
  61.5 23.8 %copy-start.7 = (bf16[4,2,64,256]{3,2,1,0:T(8,128)(2,1)}, bf16[4,2,64,256]{3,2,1,0:T(8,128)(2,1)S(1)}, u32[]{:S(2)}) copy-start(bf16[4,2,64,256]{3,2,1,0:T(8,128)(2,1)S(1)} %collective-permute-done.refs_6_) | copy-start | bytes 786436
  61.5 21.1 %collective-permute-start.9 = (bf16[4,2,64,256]{3,2,1,0:T(8,128)(2,1)S(1)}, bf16[4,2,64,256]{3,2,1,0:T(8,128)(2,1)}, u32[]{:S(2)}, u32[]{:S(2)}) collective-permute-start(bf16[4,2,64,256]{3,2,1,0:T(8,128)(2,1)S(1)} %collective-permute-done.8.refs_13_), channel_id=1, source_target_pairs={{0,8},{8,0},{1,9},{9,1},{2,10},{10,2},{3,11},{11,3},{4,12},{12,4},... | collective-permute-start | bytes 786440 | tf_op jit(solution)/shard_map/ppermute | solution.py:202
  66.4 15.0 %copy-start.8 = (bf16[4,2,64,256]{3,2,1,0:T(8,128)(2,1)}, bf16[4,2,64,256]{3,2,1,0:T(8,128)(2,1)S(1)}, u32[]{:S(2)}) copy-start(bf16[4,2,64,256]{3,2,1,0:T(8,128)(2,1)S(1)} %collective-permute-done.3.refs_8_) | copy-start | bytes 786436
  66.4 16.2 %collective-permute-start.12 = (bf16[4,2,64,256]{3,2,1,0:T(8,128)(2,1)S(1)}, bf16[4,2,64,256]{3,2,1,0:T(8,128)(2,1)}, u32[]{:S(2)}, u32[]{:S(2)}) collective-permute-start(bf16[4,2,64,256]{3,2,1,0:T(8,128)(2,1)S(1)} %collective-permute-done.10.refs_15_), channel_id=1, source_target_pairs={{0,7},{1,0},{2,1},{3,2},{4,3},{5,4},{6,5},{7,6},{8,15},{9,8},{10,9... | collective-permute-start | bytes 786440 | tf_op jit(solution)/shard_map/ppermute | solution.py:199
  68.4 14.3 %collective-permute-start.7 = (bf16[4,2,64,256]{3,2,1,0:T(8,128)(2,1)}, bf16[4,2,64,256]{3,2,1,0:T(8,128)(2,1)}, u32[]{:S(2)}, u32[]{:S(2)}) collective-permute-start(bf16[4,2,64,256]{3,2,1,0:T(8,128)(2,1)} %collective-permute-done.5.refs_10_), channel_id=1, source_target_pairs={{0,1},{1,2},{2,3},{3,4},{4,5},{5,6},{6,7},{7,0},{8,9},{9,10},{10,1... | collective-permute-start | bytes 786440 | tf_op jit(solution)/shard_map/ppermute | solution.py:205
  73.5 9.1 %collective-permute-start.14 = (bf16[4,2,64,256]{3,2,1,0:T(8,128)(2,1)}, bf16[4,2,64,256]{3,2,1,0:T(8,128)(2,1)}, u32[]{:S(2)}, u32[]{:S(2)}) collective-permute-start(bf16[4,2,64,256]{3,2,1,0:T(8,128)(2,1)} %collective-permute-done.6.refs_11_), channel_id=1, source_target_pairs={{0,1},{1,2},{2,3},{3,4},{4,5},{5,6},{6,7},{7,0},{8,9},{9,10},{10,1... | collective-permute-start | bytes 786440 | tf_op jit(solution)/shard_map/ppermute | solution.py:200
  75.5 9.8 %collective-permute-start.15 = (bf16[4,2,64,256]{3,2,1,0:T(8,128)(2,1)}, bf16[4,2,64,256]{3,2,1,0:T(8,128)(2,1)}, u32[]{:S(2)}, u32[]{:S(2)}) collective-permute-start(bf16[4,2,64,256]{3,2,1,0:T(8,128)(2,1)} %collective-permute-done.13.refs_18_), channel_id=1, source_target_pairs={{0,7},{1,0},{2,1},{3,2},{4,3},{5,4},{6,5},{7,6},{8,15},{9,8},{10,9... | collective-permute-start | bytes 786440 | tf_op jit(solution)/shard_map/ppermute | solution.py:207
Sparse Core Ops, SparseCore 0:
  17.8 58.4 all-gather.1

commit v5 on v4

--- a/solution.py
+++ b/solution.py
@@ -49,14 +49,16 @@
                 image_sem.at[variant],
             ).start()
 
-    piece_copies = []
-    for number in range(N_TEST):
-        copy = pltpu.make_async_copy(
-            piece_hbm_refs[number], piece_refs[number], piece_sem.at[number]
-        )
-        copy.start()
-        piece_copies.append(copy)
+    piece_copies = {}
     for variant in range(MUT_DEV):
+        for number in range(N_TEST):
+            copy = pltpu.make_async_copy(
+                piece_hbm_refs[number].at[variant],
+                piece_refs[number].at[variant],
+                piece_sem.at[variant, number],
+            )
+            copy.start()
+            piece_copies[variant, number] = copy
         fetch(variant)
     pltpu.make_async_copy(readout_hbm_ref, readout_ref, readout_sem).start()
 
@@ -69,8 +71,7 @@
     def build(member):
         for number in range(N_TEST):
             row = rows_of[number]
-            if member == 0:
-                piece_copies[number].wait()
+            piece_copies[member, number].wait()
             for kind in range(2):
                 base = base_ref[kind, pl.ds(row, CHUNK), :].astype(jnp.float32)
                 change = piece_refs[number][member, kind].astype(jnp.float32)
@@ -101,15 +102,12 @@
         ).wait()
         if member + 1 < MUT_DEV:
             build(member + 1)
+        both = jnp.maximum(
+            jnp.dot(x_ref[member], first_refs[member % 2][...], preferred_element_type=jnp.float32),
+            0.0,
+        ).astype(jnp.bfloat16)
         for step in range(STEPS):
-            hidden = jnp.maximum(
-                jnp.dot(
-                    x_ref[member],
-                    first_refs[member % 2][:, step * B : (step + 1) * B],
-                    preferred_element_type=jnp.float32,
-                ),
-                0.0,
-            ).astype(jnp.bfloat16)
+            hidden = both[:, step * B : (step + 1) * B]
             for part in range(C // B):
                 columns = slice(part * B, (part + 1) * B)
                 expanded = lax.dot_general(
@@ -151,6 +149,43 @@
         out_ref[variant] = lined[variant * STEPS : (variant + 1) * STEPS, :SURV]
 
 
+def run_score(plan, strength, images, readout, bases, pieces):
+    smem = pl.BlockSpec(memory_space=pltpu.SMEM)
+    vmem = pl.BlockSpec(memory_space=pltpu.VMEM)
+    hbm = pl.BlockSpec(memory_space=pl.ANY)
+    return pl.pallas_call(
+        score,
+        in_specs=[smem, smem, hbm, hbm, vmem] + [hbm] * N_TEST,
+        out_specs=vmem,
+        out_shape=jax.ShapeDtypeStruct((MUT_DEV, STEPS, SURV), jnp.float32),
+        scratch_shapes=[
+            pltpu.VMEM((MUT_DEV, ROWS, C), jnp.bfloat16),
+            pltpu.VMEM((MUT_DEV * STEPS, 16, C), jnp.bfloat16),
+            pltpu.VMEM((MUT_DEV, 2, SURV, 8, B), jnp.float32),
+            pltpu.VMEM((MUT_DEV * STEPS * 16, 128), jnp.int32),
+            pltpu.VMEM((readout.shape[0], C), jnp.bfloat16),
+            pltpu.VMEM((C, STEPS * B), jnp.bfloat16),
+            pltpu.VMEM((C, STEPS * B), jnp.bfloat16),
+            pltpu.VMEM((STEPS, C, B), jnp.bfloat16),
+            pltpu.VMEM((STEPS, C, B), jnp.bfloat16),
+        ]
+        + [pltpu.VMEM((MUT_DEV, 2, CHUNK, B), jnp.bfloat16)] * N_TEST
+        + [
+            pltpu.SemaphoreType.DMA((MUT_DEV,)),
+            pltpu.SemaphoreType.DMA,
+            pltpu.SemaphoreType.DMA((MUT_DEV, N_TEST)),
+        ],
+        compiler_params=pltpu.CompilerParams(vmem_limit_bytes=30 * 2**20),
+    )(
+        plan,
+        strength,
+        in_hbm(images),
+        in_hbm(readout),
+        in_vmem(bases),
+        *[in_hbm(value) for value in pieces],
+    )
+
+
 def on_device(
     input_activation,
     ground_truth_class,
@@ -171,6 +206,7 @@
         [narrowing_perturbation, jnp.transpose(widening_perturbation, (0, 2, 1))], axis=1
     )
     partner_rows = lax.ppermute(own_rows, "xl", swap)
+    first_up = lax.ppermute(message, "y", up)
     images = lax.all_gather(
         jnp.concatenate([own_rows, partner_rows]), ("z", "core"), axis=0, tiled=True
     )
@@ -191,67 +227,21 @@
     bases = jnp.stack([learned_narrowing_kernel, learned_widening_kernel.T])
     other, plan, strength, bases = lax.optimization_barrier((other, plan, strength, bases))
 
-    up_1 = lax.ppermute(message, "y", up)
-    down_1 = lax.ppermute(message, "y", down)
-    up_2 = lax.ppermute(up_1, "y", up)
-    down_2 = lax.ppermute(down_1, "y", down)
-    up_3 = lax.ppermute(up_2, "y", up)
-    down_3 = lax.ppermute(down_2, "y", down)
-    up_4 = lax.ppermute(up_3, "y", up)
-    other_up_1 = lax.ppermute(up_1, "xh", swap)
-    other_down_1 = lax.ppermute(down_1, "xh", swap)
-    other_up_2 = lax.ppermute(up_2, "xh", swap)
-    other_down_2 = lax.ppermute(down_2, "xh", swap)
-    other_up_3 = lax.ppermute(other_up_2, "y", up)
-    other_down_3 = lax.ppermute(other_down_2, "y", down)
-    other_4 = lax.ppermute(other_down_3, "y", down)
-    near = [message, up_1, up_2, up_3, down_1, down_2, down_3, up_4]
-    far = [
-        other,
-        other_up_1,
-        other_up_2,
-        other_up_3,
-        other_down_1,
-        other_down_2,
-        other_down_3,
-        other_4,
-    ]
-    pieces = [(near, far)[number % 2][number // 2] for number in range(N_TEST)]
-
-    smem = pl.BlockSpec(memory_space=pltpu.SMEM)
-    vmem = pl.BlockSpec(memory_space=pltpu.VMEM)
-    hbm = pl.BlockSpec(memory_space=pl.ANY)
-    return pl.pallas_call(
-        score,
-        in_specs=[smem, smem, hbm, hbm, vmem] + [hbm] * N_TEST,
-        out_specs=vmem,
-        out_shape=jax.ShapeDtypeStruct((MUT_DEV, STEPS, SURV), jnp.float32),
-        scratch_shapes=[
-            pltpu.VMEM((MUT_DEV, ROWS, C), jnp.bfloat16),
-            pltpu.VMEM((MUT_DEV * STEPS, 16, C), jnp.bfloat16),
-            pltpu.VMEM((MUT_DEV, 2, SURV, 8, B), jnp.float32),
-            pltpu.VMEM((MUT_DEV * STEPS * 16, 128), jnp.int32),
-            pltpu.VMEM((readout_matrix.shape[1], C), jnp.bfloat16),
-            pltpu.VMEM((C, STEPS * B), jnp.bfloat16),
-            pltpu.VMEM((C, STEPS * B), jnp.bfloat16),
-            pltpu.VMEM((STEPS, C, B), jnp.bfloat16),
-            pltpu.VMEM((STEPS, C, B), jnp.bfloat16),
-        ]
-        + [pltpu.VMEM((MUT_DEV, 2, CHUNK, B), jnp.bfloat16)] * N_TEST
-        + [
-            pltpu.SemaphoreType.DMA((MUT_DEV,)),
-            pltpu.SemaphoreType.DMA,
-            pltpu.SemaphoreType.DMA((N_TEST,)),
-        ],
-        compiler_params=pltpu.CompilerParams(vmem_limit_bytes=30 * 2**20),
-    )(
-        plan,
-        strength,
-        in_hbm(images),
-        in_hbm(readout_matrix.T),
-        in_vmem(bases),
-        *[in_hbm(value) for value in pieces],
-    )
+    flows = []
+    for number, seed in enumerate((message, other)):
+        rising = [first_up if number == 0 else lax.ppermute(seed, "y", up)]
+        falling = [lax.ppermute(seed, "y", down)]
+        for _ in range(2):
+            rising.append(lax.ppermute(rising[-1], "y", up))
+            falling.append(lax.ppermute(falling[-1], "y", down))
+        if number == 0:
+            farthest = lax.ppermute(rising[-1], "y", up)
+        else:
+            farthest = lax.ppermute(falling[-1], "y", down)
+        flows.append([seed] + rising + falling + [farthest])
+    pieces = [flows[number % 2][number // 2] for number in range(N_TEST)]
+
+    return run_score(plan, strength, images, readout_matrix.T, bases, pieces)
 
 
 def solution(mesh):

time: 107 us -> 103 us (0.963)
  starting transfers between devices: 56.4 us -> 51.6 us
  Pallas kernels: 13.7 us -> 12 us
  waiting for transfers between devices: 13.5 us -> 15 us
    ppermute x14, starting transfers between devices: 50.6 us -> 46.3 us  [the longest x4 17.8 us: on_device(): rising.append(lax.ppermute(rising[-1], 'y', up))]
    ppermute x1, waiting for transfers between devices: 0.01 us -> 2.27 us  [on_device(): other = lax.ppermute(message, 'xh', swap)]
    pallas_call x1, Pallas kernels: 13.7 us -> 12 us  [run_score(): pl.pallas_call(score, in_specs=[smem, smem, hbm, hbm, vmem] + [hbm] * N_T...]
    unnamed x20 -> x34, local copies, waits for them, and re-layouts: 2.3 us -> 3.03 us
where the time goes in v5:
time: 103 us; the launch traced here: 102 us
  starting transfers between devices  51.6 us (50%)
  waiting for transfers between devices  15 us (15%)
  between operations  13.9 us (13%)
  Pallas kernels  12 us (12%)
  local copies, waits for them, and re-layouts  6.15 us (6%)
  other arithmetic  3.03 us (3%)
    ppermute x4, starting transfers between devices, on_device(): rising.append(lax.ppermute(rising[-1], 'y', up))  17.8 us
    pallas_call x1, Pallas kernels, run_score(): pl.pallas_call(score, in_specs=[smem, smem, hbm, hbm, vmem] + [hbm] * N_T...  12 us
    ppermute x4, starting transfers between devices, on_device(): falling.append(lax.ppermute(falling[-1], 'y', down))  7.68 us
    ppermute x1, waiting for transfers between devices, on_device(): partner_rows = lax.ppermute(own_rows, 'xl', swap)  5.83 us
    ppermute x1, starting transfers between devices, on_device(): first_up = lax.ppermute(message, 'y', up)  5.73 us
    ppermute x1, starting transfers between devices, on_device(): farthest = lax.ppermute(rising[-1], 'y', up)  5.13 us
    ppermute x1, waiting for transfers between devices, on_device(): farthest = lax.ppermute(falling[-1], 'y', down)  4.54 us
    ppermute x2, starting transfers between devices, on_device(): falling = [lax.ppermute(seed, 'y', down)]  4.13 us
  transfers between devices with their start and end apart: 17, of which 4 were waited for; matrix products, arithmetic and copies ran while one was open for 6% of the time, Pallas kernels for 0%

profile of v5, /device:TPU:56, one launch (start us, length us, event | category | flops | bytes accessed | tf_op | source)
XLA Modules:
  0.0 101.7 jit_solution(14016250950034235170)
XLA Ops:
  6.5 0.0 copy-start
  6.5 0.0 all-gather.2.cloned.1.call-start
  6.5 1.0 %copy.13 = bf16[4,28,1024]{2,1,0:T(8,128)(2,1)S(1)} copy(bf16[4,28,1024]{2,0,1:T(4,128)(2,1)} %param.9) | data formatting | bytes 458752 | tf_op args[0]
  7.6 3.4 %collective-permute-start.1 = (bf16[112,1024]{1,0:T(8,128)(2,1)S(1)}, bf16[112,1024]{1,0:T(8,128)(2,1)S(1)}, u32[]{:S(2)}, u32[]{:S(2)}) collective-permute-start(bf16[112,1024]{1,0:T(8,128)(2,1)S(1)} %reshape.632), channel_id=1, source_target_pairs={{0,256},{256,0},{1,257},{257,1},{2,258},{258,2},{3,259},{259,3},{4... | collective-permute-start | bytes 688136 | tf_op jit(solution)/shard_map/ppermute | solution.py:208
  11.0 5.8 %collective-permute-done.1 = bf16[112,1024]{1,0:T(8,128)(2,1)S(1)} collective-permute-done((bf16[112,1024]{1,0:T(8,128)(2,1)S(1)}, bf16[112,1024]{1,0:T(8,128)(2,1)S(1)}, u32[]{:S(2)}, u32[]{:S(2)}) %collective-permute-start.1) | collective-permute-done | bytes 229408 | tf_op jit(solution)/shard_map/ppermute | solution.py:208
  16.9 0.8 pad_maximum_fusion.1
  17.7 0.0 all-gather.2.cloned.1.call-update
  17.7 1.0 pad_maximum_fusion.2.refs_5_
  18.7 0.0 copy-start.1
  18.7 5.7 %collective-permute-start.2 = (bf16[4,2,64,256]{3,2,1,0:T(8,128)(2,1)S(1)}, bf16[4,2,64,256]{3,2,1,0:T(8,128)(2,1)S(1)}, u32[]{:S(2)}, u32[]{:S(2)}) collective-permute-start(bf16[4,2,64,256]{3,2,1,0:T(8,128)(2,1)S(1)} %pad_maximum_fusion.2.refs_5_), channel_id=1, source_target_pairs={{0,1},{1,2},{2,3},{3,4},{4,5},{5,6},{6,7},{7,0},{8,9},{9,10},{10,1... | collective-permute-start | bytes 786440 | tf_op jit(solution)/shard_map/ppermute | solution.py:209
  24.5 1.9 %collective-permute-start = (bf16[4,2,64,256]{3,2,1,0:T(8,128)(2,1)S(1)}, bf16[4,2,64,256]{3,2,1,0:T(8,128)(2,1)S(1)}, u32[]{:S(2)}, u32[]{:S(2)}) collective-permute-start(bf16[4,2,64,256]{3,2,1,0:T(8,128)(2,1)S(1)} %pad_maximum_fusion.2.refs_5_), channel_id=1, source_target_pairs={{0,8},{8,0},{1,9},{9,1},{2,10},{10,2},{3,11},{11,3},{4,12},{12,4},... | collective-permute-start | bytes 786440 | tf_op jit(solution)/shard_map/ppermute | solution.py:214
  26.4 0.8 reshape.630
  27.2 0.8 reshape.629
  27.9 0.0 copy-done
  28.0 0.8 gather_fusion
  28.8 0.8 reshape.631
  29.5 1.2 %copy.12 = bf16[256,1024]{0,1:T(8,128)(2,1)S(1)} copy(bf16[256,1024]{1,0:T(8,128)(2,1)} %param.13) | data formatting | bytes 1048576 | tf_op args[4]
  30.8 1.1 %pad_maximum_fusion.refs_4_ = bf16[2,1024,256]{2,1,0:T(8,128)(2,1)S(1)} fusion(bf16[1,1024,256]{2,1,0:T(8,128)(2,1)S(1)} %bitcast.14, bf16[1,1024,256]{2,1,0:T(8,128)(2,1)} %bitcast.16), kind=kLoop, calls=%fused_computation.1 | loop fusion | flops 524288 | bytes 2097152 | tf_op jit(solution)/shard_map/stack | solution.py:227
  32.0 2.3 %collective-permute-done.refs_6_ = bf16[4,2,64,256]{3,2,1,0:T(8,128)(2,1)S(1)} collective-permute-done((bf16[4,2,64,256]{3,2,1,0:T(8,128)(2,1)S(1)}, bf16[4,2,64,256]{3,2,1,0:T(8,128)(2,1)S(1)}, u32[]{:S(2)}, u32[]{:S(2)}) %collective-permute-start) | collective-permute-done | bytes 262176 | tf_op jit(solution)/shard_map/ppermute | solution.py:214
  34.2 1.9 %collective-permute-start.9 = (bf16[4,2,64,256]{3,2,1,0:T(8,128)(2,1)S(1)}, bf16[4,2,64,256]{3,2,1,0:T(8,128)(2,1)S(1)}, u32[]{:S(2)}, u32[]{:S(2)}) collective-permute-start(bf16[4,2,64,256]{3,2,1,0:T(8,128)(2,1)S(1)} %collective-permute-done.refs_6_), channel_id=1, source_target_pairs={{0,7},{1,0},{2,1},{3,2},{4,3},{5,4},{6,5},{7,6},{8,15},{9,8},{10,9... | collective-permute-start | bytes 786440 | tf_op jit(solution)/shard_map/ppermute | solution.py:233
  36.1 2.2 %collective-permute-start.8 = (bf16[4,2,64,256]{3,2,1,0:T(8,128)(2,1)S(1)}, bf16[4,2,64,256]{3,2,1,0:T(8,128)(2,1)S(1)}, u32[]{:S(2)}, u32[]{:S(2)}) collective-permute-start(bf16[4,2,64,256]{3,2,1,0:T(8,128)(2,1)S(1)} %pad_maximum_fusion.2.refs_5_), channel_id=1, source_target_pairs={{0,7},{1,0},{2,1},{3,2},{4,3},{5,4},{6,5},{7,6},{8,15},{9,8},{10,9... | collective-permute-start | bytes 786440 | tf_op jit(solution)/shard_map/ppermute | solution.py:233
  38.4 0.0 collective-permute-done.2.refs_7_
  38.4 0.0 copy-start.2
  38.4 4.8 %collective-permute-start.4 = (bf16[4,2,64,256]{3,2,1,0:T(8,128)(2,1)S(1)}, bf16[4,2,64,256]{3,2,1,0:T(8,128)(2,1)S(1)}, u32[]{:S(2)}, u32[]{:S(2)}) collective-permute-start(bf16[4,2,64,256]{3,2,1,0:T(8,128)(2,1)S(1)} %collective-permute-done.2.refs_7_), channel_id=1, source_target_pairs={{0,1},{1,2},{2,3},{3,4},{4,5},{5,6},{6,7},{7,0},{8,9},{9,10},{10,1... | collective-permute-start | bytes 786440 | tf_op jit(solution)/shard_map/ppermute | solution.py:235
  43.2 3.9 %collective-permute-start.3 = (bf16[4,2,64,256]{3,2,1,0:T(8,128)(2,1)S(1)}, bf16[4,2,64,256]{3,2,1,0:T(8,128)(2,1)S(1)}, u32[]{:S(2)}, u32[]{:S(2)}) collective-permute-start(bf16[4,2,64,256]{3,2,1,0:T(8,128)(2,1)S(1)} %collective-permute-done.refs_6_), channel_id=1, source_target_pairs={{0,1},{1,2},{2,3},{3,4},{4,5},{5,6},{6,7},{7,0},{8,9},{9,10},{10,1... | collective-permute-start | bytes 786440 | tf_op jit(solution)/shard_map/ppermute | solution.py:232
  47.2 0.0 collective-permute-done.9.refs_14_
  47.2 0.0 copy-start.4
  47.2 1.9 %collective-permute-start.11 = (bf16[4,2,64,256]{3,2,1,0:T(8,128)(2,1)S(1)}, bf16[4,2,64,256]{3,2,1,0:T(8,128)(2,1)S(1)}, u32[]{:S(2)}, u32[]{:S(2)}) collective-permute-start(bf16[4,2,64,256]{3,2,1,0:T(8,128)(2,1)S(1)} %collective-permute-done.9.refs_14_), channel_id=1, source_target_pairs={{0,7},{1,0},{2,1},{3,2},{4,3},{5,4},{6,5},{7,6},{8,15},{9,8},{10,9... | collective-permute-start | bytes 786440 | tf_op jit(solution)/shard_map/ppermute | solution.py:236
  49.1 0.0 collective-permute-done.8.refs_13_
  49.1 0.0 copy-start.5
  49.1 1.9 %collective-permute-start.10 = (bf16[4,2,64,256]{3,2,1,0:T(8,128)(2,1)S(1)}, bf16[4,2,64,256]{3,2,1,0:T(8,128)(2,1)S(1)}, u32[]{:S(2)}, u32[]{:S(2)}) collective-permute-start(bf16[4,2,64,256]{3,2,1,0:T(8,128)(2,1)S(1)} %collective-permute-done.8.refs_13_), channel_id=1, source_target_pairs={{0,7},{1,0},{2,1},{3,2},{4,3},{5,4},{6,5},{7,6},{8,15},{9,8},{10,9... | collective-permute-start | bytes 786440 | tf_op jit(solution)/shard_map/ppermute | solution.py:236
  51.1 0.0 collective-permute-done.4.refs_9_
  51.1 0.0 copy-start.6
  51.1 5.1 %collective-permute-start.6 = (bf16[4,2,64,256]{3,2,1,0:T(8,128)(2,1)S(1)}, bf16[4,2,64,256]{3,2,1,0:T(8,128)(2,1)S(1)}, u32[]{:S(2)}, u32[]{:S(2)}) collective-permute-start(bf16[4,2,64,256]{3,2,1,0:T(8,128)(2,1)S(1)} %collective-permute-done.4.refs_9_), channel_id=1, source_target_pairs={{0,1},{1,2},{2,3},{3,4},{4,5},{5,6},{6,7},{7,0},{8,9},{9,10},{10,1... | collective-permute-start | bytes 786440 | tf_op jit(solution)/shard_map/ppermute | solution.py:235
  56.2 0.0 collective-permute-done.3.refs_8_
  56.2 0.0 copy-start.7
  56.2 3.9 %collective-permute-start.5 = (bf16[4,2,64,256]{3,2,1,0:T(8,128)(2,1)S(1)}, bf16[4,2,64,256]{3,2,1,0:T(8,128)(2,1)S(1)}, u32[]{:S(2)}, u32[]{:S(2)}) collective-permute-start(bf16[4,2,64,256]{3,2,1,0:T(8,128)(2,1)S(1)} %collective-permute-done.3.refs_8_), channel_id=1, source_target_pairs={{0,1},{1,2},{2,3},{3,4},{4,5},{5,6},{6,7},{7,0},{8,9},{9,10},{10,1... | collective-permute-start | bytes 786440 | tf_op jit(solution)/shard_map/ppermute | solution.py:235
  60.2 0.0 collective-permute-done.11.refs_16_
  60.2 0.0 copy-start.8
  60.2 1.9 %collective-permute-start.13 = (bf16[4,2,64,256]{3,2,1,0:T(8,128)(2,1)S(1)}, bf16[4,2,64,256]{3,2,1,0:T(8,128)(2,1)S(1)}, u32[]{:S(2)}, u32[]{:S(2)}) collective-permute-start(bf16[4,2,64,256]{3,2,1,0:T(8,128)(2,1)S(1)} %collective-permute-done.11.refs_16_), channel_id=1, source_target_pairs={{0,7},{1,0},{2,1},{3,2},{4,3},{5,4},{6,5},{7,6},{8,15},{9,8},{10,9... | collective-permute-start | bytes 786440 | tf_op jit(solution)/shard_map/ppermute | solution.py:236
  62.1 0.0 collective-permute-done.10.refs_15_
  62.1 0.0 copy-start.9
  62.1 1.9 %collective-permute-start.12 = (bf16[4,2,64,256]{3,2,1,0:T(8,128)(2,1)S(1)}, bf16[4,2,64,256]{3,2,1,0:T(8,128)(2,1)S(1)}, u32[]{:S(2)}, u32[]{:S(2)}) collective-permute-start(bf16[4,2,64,256]{3,2,1,0:T(8,128)(2,1)S(1)} %collective-permute-done.10.refs_15_), channel_id=1, source_target_pairs={{0,7},{1,0},{2,1},{3,2},{4,3},{5,4},{6,5},{7,6},{8,15},{9,8},{10,9... | collective-permute-start | bytes 786440 | tf_op jit(solution)/shard_map/ppermute | solution.py:236
  64.1 0.0 collective-permute-done.6.refs_11_
  64.1 0.0 copy-start.10
  64.1 5.1 %collective-permute-start.14 = (bf16[4,2,64,256]{3,2,1,0:T(8,128)(2,1)S(1)}, bf16[4,2,64,256]{3,2,1,0:T(8,128)(2,1)S(1)}, u32[]{:S(2)}, u32[]{:S(2)}) collective-permute-start(bf16[4,2,64,256]{3,2,1,0:T(8,128)(2,1)S(1)} %collective-permute-done.6.refs_11_), channel_id=1, source_target_pairs={{0,1},{1,2},{2,3},{3,4},{4,5},{5,6},{6,7},{7,0},{8,9},{9,10},{10,1... | collective-permute-start | bytes 786440 | tf_op jit(solution)/shard_map/ppermute | solution.py:238
  69.2 0.0 collective-permute-done.5.refs_10_
  69.2 0.0 copy-start.11
  69.3 3.9 %collective-permute-start.7 = (bf16[4,2,64,256]{3,2,1,0:T(8,128)(2,1)S(1)}, bf16[4,2,64,256]{3,2,1,0:T(8,128)(2,1)S(1)}, u32[]{:S(2)}, u32[]{:S(2)}) collective-permute-start(bf16[4,2,64,256]{3,2,1,0:T(8,128)(2,1)S(1)} %collective-permute-done.5.refs_10_), channel_id=1, source_target_pairs={{0,1},{1,2},{2,3},{3,4},{4,5},{5,6},{6,7},{7,0},{8,9},{9,10},{10,1... | collective-permute-start | bytes 786440 | tf_op jit(solution)/shard_map/ppermute | solution.py:235
  73.2 0.0 collective-permute-done.13.refs_18_
  73.2 0.0 copy-start.12
  73.2 1.9 %collective-permute-start.15 = (bf16[4,2,64,256]{3,2,1,0:T(8,128)(2,1)S(1)}, bf16[4,2,64,256]{3,2,1,0:T(8,128)(2,1)}, u32[]{:S(2)}, u32[]{:S(2)}) collective-permute-start(bf16[4,2,64,256]{3,2,1,0:T(8,128)(2,1)S(1)} %collective-permute-done.13.refs_18_), channel_id=1, source_target_pairs={{0,7},{1,0},{2,1},{3,2},{4,3},{5,4},{6,5},{7,6},{8,15},{9,8},{10,9... | collective-permute-start | bytes 786440 | tf_op jit(solution)/shard_map/ppermute | solution.py:240
  75.1 0.0 collective-permute-done.12.refs_17_
  75.1 0.0 copy-done.10
  75.2 0.0 copy-start.13
  75.2 0.0 collective-permute-done.14.refs_19_
  75.2 0.0 copy-done.11
  75.2 0.0 copy-start.14
  75.2 2.3 %collective-permute-done.7.refs_12_ = bf16[4,2,64,256]{3,2,1,0:T(8,128)(2,1)S(1)} collective-permute-done((bf16[4,2,64,256]{3,2,1,0:T(8,128)(2,1)S(1)}, bf16[4,2,64,256]{3,2,1,0:T(8,128)(2,1)S(1)}, u32[]{:S(2)}, u32[]{:S(2)}) %collective-permute-start.7) | collective-permute-done | bytes 262176 | tf_op jit(solution)/shard_map/ppermute | solution.py:235
  77.5 0.0 copy-done.12
  77.5 0.0 copy-done.13
  77.5 0.7 copy-done.15
  78.2 4.5 %collective-permute-done.15.refs_20_ = bf16[4,2,64,256]{3,2,1,0:T(8,128)(2,1)} collective-permute-done((bf16[4,2,64,256]{3,2,1,0:T(8,128)(2,1)S(1)}, bf16[4,2,64,256]{3,2,1,0:T(8,128)(2,1)}, u32[]{:S(2)}, u32[]{:S(2)}) %collective-permute-start.15) | collective-permute-done | bytes 262176 | tf_op jit(solution)/shard_map/ppermute | solution.py:240
  82.9 12.0 %shard_map.91 = f32[4,2,14]{2,1,0:T(2,128)} custom-call(s32[3,56]{1,0:T(4,128)S(1)} %pad_add_fusion.refs_0_, f32[1,128]{1,0:T(1,128)S(1)} %pad.4.refs_1_, bf16[3584,1024]{1,0:T(8,128)(2,1)} %all-gather.2.cloned.1.call-done.refs_2_, bf16[1000,1024]{1,0:T(8,128)(2,1)} %bitcast.15, bf16[2,1024,256]{2,1,0:T(8,128)(2,1)S(1)} %pad_maximum_fusion.refs_4_, ...), custom_call_target="tpu_custom_call" | custom-call | tf_op jit(solution)/shard_map/pallas_call | solution.py:156
  (20 shorter events, 0.2 us)
Async XLA Ops:
  6.5 21.4 %copy-start = (s32[2048]{0:T(1024)S(1)}, s32[2048]{0:T(1024)}, u32[]{:S(2)}) copy-start(s32[2048]{0:T(1024)} %param.10) | copy-start | bytes 24580
  6.5 76.3 %all-gather.2.cloned.1.call-start = ((), (), s32[]{:S(2)}) async-start(), calls=%async_computation | async-start | bytes 7798784 | tf_op jit(solution)/shard_map/all_gather | solution.py:210
  7.6 9.2 %collective-permute-start.1 = (bf16[112,1024]{1,0:T(8,128)(2,1)S(1)}, bf16[112,1024]{1,0:T(8,128)(2,1)S(1)}, u32[]{:S(2)}, u32[]{:S(2)}) collective-permute-start(bf16[112,1024]{1,0:T(8,128)(2,1)S(1)} %reshape.632), channel_id=1, source_target_pairs={{0,256},{256,0},{1,257},{257,1},{2,258},{258,2},{3,259},{259,3},{4... | collective-permute-start | bytes 688136 | tf_op jit(solution)/shard_map/ppermute | solution.py:208
  18.7 64.1 %copy-start.1 = (bf16[4,2,64,256]{3,2,1,0:T(8,128)(2,1)}, bf16[4,2,64,256]{3,2,1,0:T(8,128)(2,1)S(1)}, u32[]{:S(2)}) copy-start(bf16[4,2,64,256]{3,2,1,0:T(8,128)(2,1)S(1)} %pad_maximum_fusion.2.refs_5_) | copy-start | bytes 786436
  18.7 19.7 %collective-permute-start.2 = (bf16[4,2,64,256]{3,2,1,0:T(8,128)(2,1)S(1)}, bf16[4,2,64,256]{3,2,1,0:T(8,128)(2,1)S(1)}, u32[]{:S(2)}, u32[]{:S(2)}) collective-permute-start(bf16[4,2,64,256]{3,2,1,0:T(8,128)(2,1)S(1)} %pad_maximum_fusion.2.refs_5_), channel_id=1, source_target_pairs={{0,1},{1,2},{2,3},{3,4},{4,5},{5,6},{6,7},{7,0},{8,9},{9,10},{10,1... | collective-permute-start | bytes 786440 | tf_op jit(solution)/shard_map/ppermute | solution.py:209
  24.5 9.8 %collective-permute-start = (bf16[4,2,64,256]{3,2,1,0:T(8,128)(2,1)S(1)}, bf16[4,2,64,256]{3,2,1,0:T(8,128)(2,1)S(1)}, u32[]{:S(2)}, u32[]{:S(2)}) collective-permute-start(bf16[4,2,64,256]{3,2,1,0:T(8,128)(2,1)S(1)} %pad_maximum_fusion.2.refs_5_), channel_id=1, source_target_pairs={{0,8},{8,0},{1,9},{9,1},{2,10},{10,2},{3,11},{11,3},{4,12},{12,4},... | collective-permute-start | bytes 786440 | tf_op jit(solution)/shard_map/ppermute | solution.py:214
  34.2 48.6 %copy-start.3 = (bf16[4,2,64,256]{3,2,1,0:T(8,128)(2,1)}, bf16[4,2,64,256]{3,2,1,0:T(8,128)(2,1)S(1)}, u32[]{:S(2)}) copy-start(bf16[4,2,64,256]{3,2,1,0:T(8,128)(2,1)S(1)} %collective-permute-done.refs_6_) | copy-start | bytes 786436
  34.2 12.9 %collective-permute-start.9 = (bf16[4,2,64,256]{3,2,1,0:T(8,128)(2,1)S(1)}, bf16[4,2,64,256]{3,2,1,0:T(8,128)(2,1)S(1)}, u32[]{:S(2)}, u32[]{:S(2)}) collective-permute-start(bf16[4,2,64,256]{3,2,1,0:T(8,128)(2,1)S(1)} %collective-permute-done.refs_6_), channel_id=1, source_target_pairs={{0,7},{1,0},{2,1},{3,2},{4,3},{5,4},{6,5},{7,6},{8,15},{9,8},{10,9... | collective-permute-start | bytes 786440 | tf_op jit(solution)/shard_map/ppermute | solution.py:233
  36.1 13.0 %collective-permute-start.8 = (bf16[4,2,64,256]{3,2,1,0:T(8,128)(2,1)S(1)}, bf16[4,2,64,256]{3,2,1,0:T(8,128)(2,1)S(1)}, u32[]{:S(2)}, u32[]{:S(2)}) collective-permute-start(bf16[4,2,64,256]{3,2,1,0:T(8,128)(2,1)S(1)} %pad_maximum_fusion.2.refs_5_), channel_id=1, source_target_pairs={{0,7},{1,0},{2,1},{3,2},{4,3},{5,4},{6,5},{7,6},{8,15},{9,8},{10,9... | collective-permute-start | bytes 786440 | tf_op jit(solution)/shard_map/ppermute | solution.py:233
  38.4 44.4 %copy-start.2 = (bf16[4,2,64,256]{3,2,1,0:T(8,128)(2,1)}, bf16[4,2,64,256]{3,2,1,0:T(8,128)(2,1)S(1)}, u32[]{:S(2)}) copy-start(bf16[4,2,64,256]{3,2,1,0:T(8,128)(2,1)S(1)} %collective-permute-done.2.refs_7_) | copy-start | bytes 786436
  38.4 12.7 %collective-permute-start.4 = (bf16[4,2,64,256]{3,2,1,0:T(8,128)(2,1)S(1)}, bf16[4,2,64,256]{3,2,1,0:T(8,128)(2,1)S(1)}, u32[]{:S(2)}, u32[]{:S(2)}) collective-permute-start(bf16[4,2,64,256]{3,2,1,0:T(8,128)(2,1)S(1)} %collective-permute-done.2.refs_7_), channel_id=1, source_target_pairs={{0,1},{1,2},{2,3},{3,4},{4,5},{5,6},{6,7},{7,0},{8,9},{9,10},{10,1... | collective-permute-start | bytes 786440 | tf_op jit(solution)/shard_map/ppermute | solution.py:235
  43.2 13.0 %collective-permute-start.3 = (bf16[4,2,64,256]{3,2,1,0:T(8,128)(2,1)S(1)}, bf16[4,2,64,256]{3,2,1,0:T(8,128)(2,1)S(1)}, u32[]{:S(2)}, u32[]{:S(2)}) collective-permute-start(bf16[4,2,64,256]{3,2,1,0:T(8,128)(2,1)S(1)} %collective-permute-done.refs_6_), channel_id=1, source_target_pairs={{0,1},{1,2},{2,3},{3,4},{4,5},{5,6},{6,7},{7,0},{8,9},{9,10},{10,1... | collective-permute-start | bytes 786440 | tf_op jit(solution)/shard_map/ppermute | solution.py:232
  47.2 35.6 %copy-start.4 = (bf16[4,2,64,256]{3,2,1,0:T(8,128)(2,1)}, bf16[4,2,64,256]{3,2,1,0:T(8,128)(2,1)S(1)}, u32[]{:S(2)}) copy-start(bf16[4,2,64,256]{3,2,1,0:T(8,128)(2,1)S(1)} %collective-permute-done.9.refs_14_) | copy-start | bytes 786436
  47.2 13.0 %collective-permute-start.11 = (bf16[4,2,64,256]{3,2,1,0:T(8,128)(2,1)S(1)}, bf16[4,2,64,256]{3,2,1,0:T(8,128)(2,1)S(1)}, u32[]{:S(2)}, u32[]{:S(2)}) collective-permute-start(bf16[4,2,64,256]{3,2,1,0:T(8,128)(2,1)S(1)} %collective-permute-done.9.refs_14_), channel_id=1, source_target_pairs={{0,7},{1,0},{2,1},{3,2},{4,3},{5,4},{6,5},{7,6},{8,15},{9,8},{10,9... | collective-permute-start | bytes 786440 | tf_op jit(solution)/shard_map/ppermute | solution.py:236
  49.1 33.7 %copy-start.5 = (bf16[4,2,64,256]{3,2,1,0:T(8,128)(2,1)}, bf16[4,2,64,256]{3,2,1,0:T(8,128)(2,1)S(1)}, u32[]{:S(2)}) copy-start(bf16[4,2,64,256]{3,2,1,0:T(8,128)(2,1)S(1)} %collective-permute-done.8.refs_13_) | copy-start | bytes 786436
  49.1 13.0 %collective-permute-start.10 = (bf16[4,2,64,256]{3,2,1,0:T(8,128)(2,1)S(1)}, bf16[4,2,64,256]{3,2,1,0:T(8,128)(2,1)S(1)}, u32[]{:S(2)}, u32[]{:S(2)}) collective-permute-start(bf16[4,2,64,256]{3,2,1,0:T(8,128)(2,1)S(1)} %collective-permute-done.8.refs_13_), channel_id=1, source_target_pairs={{0,7},{1,0},{2,1},{3,2},{4,3},{5,4},{6,5},{7,6},{8,15},{9,8},{10,9... | collective-permute-start | bytes 786440 | tf_op jit(solution)/shard_map/ppermute | solution.py:236
  51.1 31.7 %copy-start.6 = (bf16[4,2,64,256]{3,2,1,0:T(8,128)(2,1)}, bf16[4,2,64,256]{3,2,1,0:T(8,128)(2,1)S(1)}, u32[]{:S(2)}) copy-start(bf16[4,2,64,256]{3,2,1,0:T(8,128)(2,1)S(1)} %collective-permute-done.4.refs_9_) | copy-start | bytes 786436
  51.1 13.0 %collective-permute-start.6 = (bf16[4,2,64,256]{3,2,1,0:T(8,128)(2,1)S(1)}, bf16[4,2,64,256]{3,2,1,0:T(8,128)(2,1)S(1)}, u32[]{:S(2)}, u32[]{:S(2)}) collective-permute-start(bf16[4,2,64,256]{3,2,1,0:T(8,128)(2,1)S(1)} %collective-permute-done.4.refs_9_), channel_id=1, source_target_pairs={{0,1},{1,2},{2,3},{3,4},{4,5},{5,6},{6,7},{7,0},{8,9},{9,10},{10,1... | collective-permute-start | bytes 786440 | tf_op jit(solution)/shard_map/ppermute | solution.py:235
  56.2 26.6 %copy-start.7 = (bf16[4,2,64,256]{3,2,1,0:T(8,128)(2,1)}, bf16[4,2,64,256]{3,2,1,0:T(8,128)(2,1)S(1)}, u32[]{:S(2)}) copy-start(bf16[4,2,64,256]{3,2,1,0:T(8,128)(2,1)S(1)} %collective-permute-done.3.refs_8_) | copy-start | bytes 786436
  56.2 13.0 %collective-permute-start.5 = (bf16[4,2,64,256]{3,2,1,0:T(8,128)(2,1)S(1)}, bf16[4,2,64,256]{3,2,1,0:T(8,128)(2,1)S(1)}, u32[]{:S(2)}, u32[]{:S(2)}) collective-permute-start(bf16[4,2,64,256]{3,2,1,0:T(8,128)(2,1)S(1)} %collective-permute-done.3.refs_8_), channel_id=1, source_target_pairs={{0,1},{1,2},{2,3},{3,4},{4,5},{5,6},{6,7},{7,0},{8,9},{9,10},{10,1... | collective-permute-start | bytes 786440 | tf_op jit(solution)/shard_map/ppermute | solution.py:235
  60.2 22.7 %copy-start.8 = (bf16[4,2,64,256]{3,2,1,0:T(8,128)(2,1)}, bf16[4,2,64,256]{3,2,1,0:T(8,128)(2,1)S(1)}, u32[]{:S(2)}) copy-start(bf16[4,2,64,256]{3,2,1,0:T(8,128)(2,1)S(1)} %collective-permute-done.11.refs_16_) | copy-start | bytes 786436
  60.2 13.0 %collective-permute-start.13 = (bf16[4,2,64,256]{3,2,1,0:T(8,128)(2,1)S(1)}, bf16[4,2,64,256]{3,2,1,0:T(8,128)(2,1)S(1)}, u32[]{:S(2)}, u32[]{:S(2)}) collective-permute-start(bf16[4,2,64,256]{3,2,1,0:T(8,128)(2,1)S(1)} %collective-permute-done.11.refs_16_), channel_id=1, source_target_pairs={{0,7},{1,0},{2,1},{3,2},{4,3},{5,4},{6,5},{7,6},{8,15},{9,8},{10,9... | collective-permute-start | bytes 786440 | tf_op jit(solution)/shard_map/ppermute | solution.py:236
  62.1 20.7 %copy-start.9 = (bf16[4,2,64,256]{3,2,1,0:T(8,128)(2,1)}, bf16[4,2,64,256]{3,2,1,0:T(8,128)(2,1)S(1)}, u32[]{:S(2)}) copy-start(bf16[4,2,64,256]{3,2,1,0:T(8,128)(2,1)S(1)} %collective-permute-done.10.refs_15_) | copy-start | bytes 786436
  62.1 13.0 %collective-permute-start.12 = (bf16[4,2,64,256]{3,2,1,0:T(8,128)(2,1)S(1)}, bf16[4,2,64,256]{3,2,1,0:T(8,128)(2,1)S(1)}, u32[]{:S(2)}, u32[]{:S(2)}) collective-permute-start(bf16[4,2,64,256]{3,2,1,0:T(8,128)(2,1)S(1)} %collective-permute-done.10.refs_15_), channel_id=1, source_target_pairs={{0,7},{1,0},{2,1},{3,2},{4,3},{5,4},{6,5},{7,6},{8,15},{9,8},{10,9... | collective-permute-start | bytes 786440 | tf_op jit(solution)/shard_map/ppermute | solution.py:236
  64.1 11.1 %copy-start.10 = (bf16[4,2,64,256]{3,2,1,0:T(8,128)(2,1)}, bf16[4,2,64,256]{3,2,1,0:T(8,128)(2,1)S(1)}, u32[]{:S(2)}) copy-start(bf16[4,2,64,256]{3,2,1,0:T(8,128)(2,1)S(1)} %collective-permute-done.6.refs_11_) | copy-start | bytes 786436
  64.1 11.1 %collective-permute-start.14 = (bf16[4,2,64,256]{3,2,1,0:T(8,128)(2,1)S(1)}, bf16[4,2,64,256]{3,2,1,0:T(8,128)(2,1)S(1)}, u32[]{:S(2)}, u32[]{:S(2)}) collective-permute-start(bf16[4,2,64,256]{3,2,1,0:T(8,128)(2,1)S(1)} %collective-permute-done.6.refs_11_), channel_id=1, source_target_pairs={{0,1},{1,2},{2,3},{3,4},{4,5},{5,6},{6,7},{7,0},{8,9},{9,10},{10,1... | collective-permute-start | bytes 786440 | tf_op jit(solution)/shard_map/ppermute | solution.py:238
  69.2 5.9 %copy-start.11 = (bf16[4,2,64,256]{3,2,1,0:T(8,128)(2,1)}, bf16[4,2,64,256]{3,2,1,0:T(8,128)(2,1)S(1)}, u32[]{:S(2)}) copy-start(bf16[4,2,64,256]{3,2,1,0:T(8,128)(2,1)S(1)} %collective-permute-done.5.refs_10_) | copy-start | bytes 786436
  69.3 8.3 %collective-permute-start.7 = (bf16[4,2,64,256]{3,2,1,0:T(8,128)(2,1)S(1)}, bf16[4,2,64,256]{3,2,1,0:T(8,128)(2,1)S(1)}, u32[]{:S(2)}, u32[]{:S(2)}) collective-permute-start(bf16[4,2,64,256]{3,2,1,0:T(8,128)(2,1)S(1)} %collective-permute-done.5.refs_10_), channel_id=1, source_target_pairs={{0,1},{1,2},{2,3},{3,4},{4,5},{5,6},{6,7},{7,0},{8,9},{9,10},{10,1... | collective-permute-start | bytes 786440 | tf_op jit(solution)/shard_map/ppermute | solution.py:235
  73.2 4.3 %copy-start.12 = (bf16[4,2,64,256]{3,2,1,0:T(8,128)(2,1)}, bf16[4,2,64,256]{3,2,1,0:T(8,128)(2,1)S(1)}, u32[]{:S(2)}) copy-start(bf16[4,2,64,256]{3,2,1,0:T(8,128)(2,1)S(1)} %collective-permute-done.13.refs_18_) | copy-start | bytes 786436
  73.2 9.6 %collective-permute-start.15 = (bf16[4,2,64,256]{3,2,1,0:T(8,128)(2,1)S(1)}, bf16[4,2,64,256]{3,2,1,0:T(8,128)(2,1)}, u32[]{:S(2)}, u32[]{:S(2)}) collective-permute-start(bf16[4,2,64,256]{3,2,1,0:T(8,128)(2,1)S(1)} %collective-permute-done.13.refs_18_), channel_id=1, source_target_pairs={{0,7},{1,0},{2,1},{3,2},{4,3},{5,4},{6,5},{7,6},{8,15},{9,8},{10,9... | collective-permute-start | bytes 786440 | tf_op jit(solution)/shard_map/ppermute | solution.py:240
  75.2 2.4 %copy-start.13 = (bf16[4,2,64,256]{3,2,1,0:T(8,128)(2,1)}, bf16[4,2,64,256]{3,2,1,0:T(8,128)(2,1)S(1)}, u32[]{:S(2)}) copy-start(bf16[4,2,64,256]{3,2,1,0:T(8,128)(2,1)S(1)} %collective-permute-done.12.refs_17_) | copy-start | bytes 786436
  75.2 2.3 %copy-start.14 = (bf16[4,2,64,256]{3,2,1,0:T(8,128)(2,1)}, bf16[4,2,64,256]{3,2,1,0:T(8,128)(2,1)S(1)}, u32[]{:S(2)}) copy-start(bf16[4,2,64,256]{3,2,1,0:T(8,128)(2,1)S(1)} %collective-permute-done.14.refs_19_) | copy-start | bytes 786436
  77.5 0.7 copy-start.15
Sparse Core Ops, SparseCore 0:
  17.8 58.4 all-gather.1

commit v6 on v5

--- a/solution.py
+++ b/solution.py
@@ -206,13 +206,6 @@
         [narrowing_perturbation, jnp.transpose(widening_perturbation, (0, 2, 1))], axis=1
     )
     partner_rows = lax.ppermute(own_rows, "xl", swap)
-    first_up = lax.ppermute(message, "y", up)
-    images = lax.all_gather(
-        jnp.concatenate([own_rows, partner_rows]), ("z", "core"), axis=0, tiled=True
-    )
-
-    other = lax.ppermute(message, "xh", swap)
-
     wanted = remaining_pictures.reshape(1, -1)
     holder = wanted // IMG_DEV
     within = wanted % IMG_DEV
@@ -225,12 +218,21 @@
     plan = jnp.concatenate([start, within % 2, label])
     strength = jnp.pad(perturbation_strength.T.reshape(1, -1), ((0, 0), (0, 120)))
     bases = jnp.stack([learned_narrowing_kernel, learned_widening_kernel.T])
-    other, plan, strength, bases = lax.optimization_barrier((other, plan, strength, bases))
-
+    partner_rows, message, plan, strength, bases = lax.optimization_barrier(
+        (partner_rows, message, plan, strength, bases)
+    )
+    images = lax.all_gather(
+        jnp.concatenate([own_rows, partner_rows]), ("z", "core"), axis=0, tiled=True
+    )
+
+    other = lax.ppermute(message, "xh", swap)
+    first_up = lax.ppermute(message, "y", up)
+    first_down = lax.ppermute(message, "y", down)
+    other, first_down = lax.optimization_barrier((other, first_down))
     flows = []
     for number, seed in enumerate((message, other)):
         rising = [first_up if number == 0 else lax.ppermute(seed, "y", up)]
-        falling = [lax.ppermute(seed, "y", down)]
+        falling = [first_down if number == 0 else lax.ppermute(seed, "y", down)]
         for _ in range(2):
             rising.append(lax.ppermute(rising[-1], "y", up))
             falling.append(lax.ppermute(falling[-1], "y", down))

time: 103 us -> 98.7 us (0.958)
  waiting for transfers between devices: 15 us -> 7.41 us
  starting transfers between devices: 51.6 us -> 54.6 us
    ppermute x1, waiting for transfers between devices: 5.83 us -> 0.01 us  [on_device(): partner_rows = lax.ppermute(own_rows, 'xl', swap)]
    ppermute x4, starting transfers between devices: 17.8 us -> 13.7 us  [on_device(): rising.append(lax.ppermute(rising[-1], 'y', up))]
    ppermute x4, starting transfers between devices: 7.68 us -> 11.6 us  [on_device(): falling.append(lax.ppermute(falling[-1], 'y', down))]
    ppermute x1, starting transfers between devices: 1.92 us -> 4.64 us  [on_device(): other = lax.ppermute(message, 'xh', swap)]
    ppermute x2, starting transfers between devices: 4.13 us -> 6.5 us  [the longest x1 3.26 us: on_device(): first_down = lax.ppermute(message, 'y', down)]
    ppermute x1, waiting for transfers between devices: 4.54 us -> 2.42 us  [on_device(): farthest = lax.ppermute(falling[-1], 'y', down)]
    ppermute x1, starting transfers between devices: 3.92 us -> 1.92 us  [on_device(): rising = [first_up if number == 0 else lax.ppermute(seed, 'y', up)]]
    ppermute x1, starting transfers between devices: 5.73 us -> 3.8 us  [on_device(): first_up = lax.ppermute(message, 'y', up)]
  transfers between devices with their start and end apart: 17 -> 17, of which waited for: 4 -> 3; matrix products, arithmetic and copies ran while one was open for 6% -> 7% of each run, Pallas kernels for 0% -> 0%
where the time goes in v6:
time: 98.7 us; the launch traced here: 97.6 us
  starting transfers between devices  54.6 us (55%)
  between operations  13.9 us (14%)
  Pallas kernels  12.5 us (13%)
  waiting for transfers between devices  7.41 us (8%)
  local copies, waits for them, and re-layouts  6.15 us (6%)
  other arithmetic  3.09 us (3%)
    ppermute x4, starting transfers between devices, on_device(): rising.append(lax.ppermute(rising[-1], 'y', up))  13.7 us
    pallas_call x1, Pallas kernels, run_score(): pl.pallas_call(score, in_specs=[smem, smem, hbm, hbm, vmem] + [hbm] * N_T...  12.5 us
    ppermute x4, starting transfers between devices, on_device(): falling.append(lax.ppermute(falling[-1], 'y', down))  11.6 us
    ppermute x1, starting transfers between devices, on_device(): farthest = lax.ppermute(rising[-1], 'y', up)  5.13 us
    ppermute x1, starting transfers between devices, on_device(): other = lax.ppermute(message, 'xh', swap)  4.64 us
    ppermute x1, starting transfers between devices, on_device(): farthest = lax.ppermute(falling[-1], 'y', down)  3.85 us
    ppermute x1, starting transfers between devices, on_device(): first_up = lax.ppermute(message, 'y', up)  3.8 us
    ppermute x1, starting transfers between devices, on_device(): partner_rows = lax.ppermute(own_rows, 'xl', swap)  3.4 us
  transfers between devices with their start and end apart: 17, of which 3 were waited for; matrix products, arithmetic and copies ran while one was open for 7% of the time, Pallas kernels for 0%

profile of v6, /device:TPU:56, one launch (start us, length us, event | category | flops | bytes accessed | tf_op | source)
XLA Modules:
  0.0 97.6 jit_solution(7908024481083639102)
XLA Ops:
  6.5 0.0 copy-start
  6.5 0.0 all-gather.2.cloned.1.call-start
  6.5 1.0 %copy.12 = bf16[4,28,1024]{2,1,0:T(8,128)(2,1)S(1)} copy(bf16[4,28,1024]{2,0,1:T(4,128)(2,1)} %param.9) | data formatting | bytes 458752 | tf_op args[0]
  7.6 3.4 %collective-permute-start = (bf16[112,1024]{1,0:T(8,128)(2,1)S(1)}, bf16[112,1024]{1,0:T(8,128)(2,1)S(1)}, u32[]{:S(2)}, u32[]{:S(2)}) collective-permute-start(bf16[112,1024]{1,0:T(8,128)(2,1)S(1)} %reshape.629), channel_id=1, source_target_pairs={{0,256},{256,0},{1,257},{257,1},{2,258},{258,2},{3,259},{259,3},{4... | collective-permute-start | bytes 688136 | tf_op jit(solution)/shard_map/ppermute | solution.py:208
  11.0 0.8 reshape.631
  11.8 0.8 reshape.630
  12.6 0.8 reshape.632
  13.4 1.2 %copy.13 = bf16[256,1024]{0,1:T(8,128)(2,1)S(1)} copy(bf16[256,1024]{1,0:T(8,128)(2,1)} %param.13) | data formatting | bytes 1048576 | tf_op args[4]
  14.6 0.0 copy-done
  14.7 0.8 gather_fusion
  15.4 1.0 %pad_maximum_fusion.2.refs_5_ = bf16[4,2,64,256]{3,2,1,0:T(8,128)(2,1)S(1)} fusion(bf16[4,1,64,256]{3,2,1,0:T(8,128)(2,1)} %bitcast.17, bf16[4,1,64,256]{3,2,1,0:T(8,128)(2,1)} %bitcast.18), kind=kLoop, calls=%fused_computation.3 | loop fusion | flops 131072 | bytes 524288 | tf_op jit(solution)/shard_map/stack | solution.py:205
  16.4 0.0 copy-start.1
  16.5 1.2 %pad_maximum_fusion.refs_4_ = bf16[2,1024,256]{2,1,0:T(8,128)(2,1)S(1)} fusion(bf16[1,1024,256]{2,1,0:T(8,128)(2,1)S(1)} %bitcast.14, bf16[1,1024,256]{2,1,0:T(8,128)(2,1)} %bitcast.16), kind=kLoop, calls=%fused_computation.1 | loop fusion | flops 524288 | bytes 2097152 | tf_op jit(solution)/shard_map/stack | solution.py:220
  17.7 0.0 collective-permute-done
  17.7 0.8 pad_maximum_fusion.1
  18.5 0.0 all-gather.2.cloned.1.call-update
  18.5 3.3 %collective-permute-start.2 = (bf16[4,2,64,256]{3,2,1,0:T(8,128)(2,1)S(1)}, bf16[4,2,64,256]{3,2,1,0:T(8,128)(2,1)S(1)}, u32[]{:S(2)}, u32[]{:S(2)}) collective-permute-start(bf16[4,2,64,256]{3,2,1,0:T(8,128)(2,1)S(1)} %pad_maximum_fusion.2.refs_5_), channel_id=1, source_target_pairs={{0,7},{1,0},{2,1},{3,2},{4,3},{5,4},{6,5},{7,6},{8,15},{9,8},{10,9... | collective-permute-start | bytes 786440 | tf_op jit(solution)/shard_map/ppermute | solution.py:230
  21.8 4.6 %collective-permute-start.1 = (bf16[4,2,64,256]{3,2,1,0:T(8,128)(2,1)S(1)}, bf16[4,2,64,256]{3,2,1,0:T(8,128)(2,1)S(1)}, u32[]{:S(2)}, u32[]{:S(2)}) collective-permute-start(bf16[4,2,64,256]{3,2,1,0:T(8,128)(2,1)S(1)} %pad_maximum_fusion.2.refs_5_), channel_id=1, source_target_pairs={{0,8},{8,0},{1,9},{9,1},{2,10},{10,2},{3,11},{11,3},{4,12},{12,4},... | collective-permute-start | bytes 786440 | tf_op jit(solution)/shard_map/ppermute | solution.py:228
  26.5 3.8 %collective-permute-start.3 = (bf16[4,2,64,256]{3,2,1,0:T(8,128)(2,1)S(1)}, bf16[4,2,64,256]{3,2,1,0:T(8,128)(2,1)S(1)}, u32[]{:S(2)}, u32[]{:S(2)}) collective-permute-start(bf16[4,2,64,256]{3,2,1,0:T(8,128)(2,1)S(1)} %pad_maximum_fusion.2.refs_5_), channel_id=1, source_target_pairs={{0,1},{1,2},{2,3},{3,4},{4,5},{5,6},{6,7},{7,0},{8,9},{9,10},{10,1... | collective-permute-start | bytes 786440 | tf_op jit(solution)/shard_map/ppermute | solution.py:229
  30.3 0.0 collective-permute-done.2.refs_13_
  30.3 0.0 copy-start.2
  30.3 2.4 %collective-permute-done.1.refs_6_ = bf16[4,2,64,256]{3,2,1,0:T(8,128)(2,1)S(1)} collective-permute-done((bf16[4,2,64,256]{3,2,1,0:T(8,128)(2,1)S(1)}, bf16[4,2,64,256]{3,2,1,0:T(8,128)(2,1)S(1)}, u32[]{:S(2)}, u32[]{:S(2)}) %collective-permute-start.1) | collective-permute-done | bytes 262176 | tf_op jit(solution)/shard_map/ppermute | solution.py:228
  32.7 3.2 %collective-permute-start.9 = (bf16[4,2,64,256]{3,2,1,0:T(8,128)(2,1)S(1)}, bf16[4,2,64,256]{3,2,1,0:T(8,128)(2,1)S(1)}, u32[]{:S(2)}, u32[]{:S(2)}) collective-permute-start(bf16[4,2,64,256]{3,2,1,0:T(8,128)(2,1)S(1)} %collective-permute-done.1.refs_6_), channel_id=1, source_target_pairs={{0,7},{1,0},{2,1},{3,2},{4,3},{5,4},{6,5},{7,6},{8,15},{9,8},{10,9... | collective-permute-start | bytes 786440 | tf_op jit(solution)/shard_map/ppermute | solution.py:235
  35.9 0.0 collective-permute-done.3.refs_7_
  36.0 0.0 copy-start.4
  36.0 4.6 %collective-permute-start.5 = (bf16[4,2,64,256]{3,2,1,0:T(8,128)(2,1)S(1)}, bf16[4,2,64,256]{3,2,1,0:T(8,128)(2,1)S(1)}, u32[]{:S(2)}, u32[]{:S(2)}) collective-permute-start(bf16[4,2,64,256]{3,2,1,0:T(8,128)(2,1)S(1)} %collective-permute-done.3.refs_7_), channel_id=1, source_target_pairs={{0,1},{1,2},{2,3},{3,4},{4,5},{5,6},{6,7},{7,0},{8,9},{9,10},{10,1... | collective-permute-start | bytes 786440 | tf_op jit(solution)/shard_map/ppermute | solution.py:237
  40.6 1.9 %collective-permute-start.4 = (bf16[4,2,64,256]{3,2,1,0:T(8,128)(2,1)S(1)}, bf16[4,2,64,256]{3,2,1,0:T(8,128)(2,1)S(1)}, u32[]{:S(2)}, u32[]{:S(2)}) collective-permute-start(bf16[4,2,64,256]{3,2,1,0:T(8,128)(2,1)S(1)} %collective-permute-done.1.refs_6_), channel_id=1, source_target_pairs={{0,1},{1,2},{2,3},{3,4},{4,5},{5,6},{6,7},{7,0},{8,9},{9,10},{10,1... | collective-permute-start | bytes 786440 | tf_op jit(solution)/shard_map/ppermute | solution.py:234
  42.5 0.0 collective-permute-done.9.refs_14_
  42.5 0.0 copy-start.5
  42.5 3.9 %collective-permute-start.11 = (bf16[4,2,64,256]{3,2,1,0:T(8,128)(2,1)S(1)}, bf16[4,2,64,256]{3,2,1,0:T(8,128)(2,1)S(1)}, u32[]{:S(2)}, u32[]{:S(2)}) collective-permute-start(bf16[4,2,64,256]{3,2,1,0:T(8,128)(2,1)S(1)} %collective-permute-done.9.refs_14_), channel_id=1, source_target_pairs={{0,7},{1,0},{2,1},{3,2},{4,3},{5,4},{6,5},{7,6},{8,15},{9,8},{10,9... | collective-permute-start | bytes 786440 | tf_op jit(solution)/shard_map/ppermute | solution.py:238
  46.4 1.9 %collective-permute-start.10 = (bf16[4,2,64,256]{3,2,1,0:T(8,128)(2,1)S(1)}, bf16[4,2,64,256]{3,2,1,0:T(8,128)(2,1)S(1)}, u32[]{:S(2)}, u32[]{:S(2)}) collective-permute-start(bf16[4,2,64,256]{3,2,1,0:T(8,128)(2,1)S(1)} %collective-permute-done.2.refs_13_), channel_id=1, source_target_pairs={{0,7},{1,0},{2,1},{3,2},{4,3},{5,4},{6,5},{7,6},{8,15},{9,8},{10,9... | collective-permute-start | bytes 786440 | tf_op jit(solution)/shard_map/ppermute | solution.py:238
  48.4 0.0 collective-permute-done.5.refs_9_
  48.4 0.0 copy-start.6
  48.4 5.1 %collective-permute-start.7 = (bf16[4,2,64,256]{3,2,1,0:T(8,128)(2,1)S(1)}, bf16[4,2,64,256]{3,2,1,0:T(8,128)(2,1)S(1)}, u32[]{:S(2)}, u32[]{:S(2)}) collective-permute-start(bf16[4,2,64,256]{3,2,1,0:T(8,128)(2,1)S(1)} %collective-permute-done.5.refs_9_), channel_id=1, source_target_pairs={{0,1},{1,2},{2,3},{3,4},{4,5},{5,6},{6,7},{7,0},{8,9},{9,10},{10,1... | collective-permute-start | bytes 786440 | tf_op jit(solution)/shard_map/ppermute | solution.py:237
  53.5 0.0 collective-permute-done.4.refs_8_
  53.5 0.0 copy-start.7
  53.5 2.0 %collective-permute-start.6 = (bf16[4,2,64,256]{3,2,1,0:T(8,128)(2,1)S(1)}, bf16[4,2,64,256]{3,2,1,0:T(8,128)(2,1)S(1)}, u32[]{:S(2)}, u32[]{:S(2)}) collective-permute-start(bf16[4,2,64,256]{3,2,1,0:T(8,128)(2,1)S(1)} %collective-permute-done.4.refs_8_), channel_id=1, source_target_pairs={{0,1},{1,2},{2,3},{3,4},{4,5},{5,6},{6,7},{7,0},{8,9},{9,10},{10,1... | collective-permute-start | bytes 786440 | tf_op jit(solution)/shard_map/ppermute | solution.py:237
  55.5 0.0 collective-permute-done.11.refs_16_
  55.6 0.0 copy-start.8
  55.6 3.8 %collective-permute-start.13 = (bf16[4,2,64,256]{3,2,1,0:T(8,128)(2,1)S(1)}, bf16[4,2,64,256]{3,2,1,0:T(8,128)(2,1)S(1)}, u32[]{:S(2)}, u32[]{:S(2)}) collective-permute-start(bf16[4,2,64,256]{3,2,1,0:T(8,128)(2,1)S(1)} %collective-permute-done.11.refs_16_), channel_id=1, source_target_pairs={{0,7},{1,0},{2,1},{3,2},{4,3},{5,4},{6,5},{7,6},{8,15},{9,8},{10,9... | collective-permute-start | bytes 786440 | tf_op jit(solution)/shard_map/ppermute | solution.py:238
  59.4 0.0 collective-permute-done.10.refs_15_
  59.4 0.0 copy-start.9
  59.4 1.9 %collective-permute-start.12 = (bf16[4,2,64,256]{3,2,1,0:T(8,128)(2,1)S(1)}, bf16[4,2,64,256]{3,2,1,0:T(8,128)(2,1)S(1)}, u32[]{:S(2)}, u32[]{:S(2)}) collective-permute-start(bf16[4,2,64,256]{3,2,1,0:T(8,128)(2,1)S(1)} %collective-permute-done.10.refs_15_), channel_id=1, source_target_pairs={{0,7},{1,0},{2,1},{3,2},{4,3},{5,4},{6,5},{7,6},{8,15},{9,8},{10,9... | collective-permute-start | bytes 786440 | tf_op jit(solution)/shard_map/ppermute | solution.py:238
  61.4 0.0 collective-permute-done.7.refs_11_
  61.4 5.1 %collective-permute-start.14 = (bf16[4,2,64,256]{3,2,1,0:T(8,128)(2,1)S(1)}, bf16[4,2,64,256]{3,2,1,0:T(8,128)(2,1)S(1)}, u32[]{:S(2)}, u32[]{:S(2)}) collective-permute-start(bf16[4,2,64,256]{3,2,1,0:T(8,128)(2,1)S(1)} %collective-permute-done.7.refs_11_), channel_id=1, source_target_pairs={{0,1},{1,2},{2,3},{3,4},{4,5},{5,6},{6,7},{7,0},{8,9},{9,10},{10,1... | collective-permute-start | bytes 786440 | tf_op jit(solution)/shard_map/ppermute | solution.py:240
  66.5 0.0 collective-permute-done.6.refs_10_
  66.6 2.0 %collective-permute-start.8 = (bf16[4,2,64,256]{3,2,1,0:T(8,128)(2,1)S(1)}, bf16[4,2,64,256]{3,2,1,0:T(8,128)(2,1)S(1)}, u32[]{:S(2)}, u32[]{:S(2)}) collective-permute-start(bf16[4,2,64,256]{3,2,1,0:T(8,128)(2,1)S(1)} %collective-permute-done.6.refs_10_), channel_id=1, source_target_pairs={{0,1},{1,2},{2,3},{3,4},{4,5},{5,6},{6,7},{7,0},{8,9},{9,10},{10,1... | collective-permute-start | bytes 786440 | tf_op jit(solution)/shard_map/ppermute | solution.py:237
  68.6 0.0 collective-permute-done.13.refs_18_
  68.6 0.0 copy-start.12
  68.6 3.8 %collective-permute-start.15 = (bf16[4,2,64,256]{3,2,1,0:T(8,128)(2,1)S(1)}, bf16[4,2,64,256]{3,2,1,0:T(8,128)(2,1)}, u32[]{:S(2)}, u32[]{:S(2)}) collective-permute-start(bf16[4,2,64,256]{3,2,1,0:T(8,128)(2,1)S(1)} %collective-permute-done.13.refs_18_), channel_id=1, source_target_pairs={{0,7},{1,0},{2,1},{3,2},{4,3},{5,4},{6,5},{7,6},{8,15},{9,8},{10,9... | collective-permute-start | bytes 786440 | tf_op jit(solution)/shard_map/ppermute | solution.py:242
  72.4 0.0 collective-permute-done.12.refs_17_
  72.5 0.0 collective-permute-done.14.refs_19_
  72.5 0.0 copy-done.11
  72.5 0.0 copy-start.14
  72.5 2.5 %collective-permute-done.8.refs_12_ = bf16[4,2,64,256]{3,2,1,0:T(8,128)(2,1)S(1)} collective-permute-done((bf16[4,2,64,256]{3,2,1,0:T(8,128)(2,1)S(1)}, bf16[4,2,64,256]{3,2,1,0:T(8,128)(2,1)S(1)}, u32[]{:S(2)}, u32[]{:S(2)}) %collective-permute-start.8) | collective-permute-done | bytes 262176 | tf_op jit(solution)/shard_map/ppermute | solution.py:237
  75.0 0.7 copy-done.15
  75.7 2.4 %collective-permute-done.15.refs_20_ = bf16[4,2,64,256]{3,2,1,0:T(8,128)(2,1)} collective-permute-done((bf16[4,2,64,256]{3,2,1,0:T(8,128)(2,1)S(1)}, bf16[4,2,64,256]{3,2,1,0:T(8,128)(2,1)}, u32[]{:S(2)}, u32[]{:S(2)}) %collective-permute-start.15) | collective-permute-done | bytes 262176 | tf_op jit(solution)/shard_map/ppermute | solution.py:242
  78.2 0.0 copy-done.4
  78.2 0.0 copy-done.5
  78.2 0.0 copy-done.6
  78.2 0.0 copy-done.7
  78.2 0.0 copy-done.8
  78.2 0.0 copy-done.9
  78.2 12.5 %shard_map.91 = f32[4,2,14]{2,1,0:T(2,128)} custom-call(s32[3,56]{1,0:T(4,128)S(1)} %pad_add_fusion.refs_0_, f32[1,128]{1,0:T(1,128)S(1)} %pad.4.refs_1_, bf16[3584,1024]{1,0:T(8,128)(2,1)} %all-gather.2.cloned.1.call-done.refs_2_, bf16[1000,1024]{1,0:T(8,128)(2,1)} %bitcast.15, bf16[2,1024,256]{2,1,0:T(8,128)(2,1)S(1)} %pad_maximum_fusion.refs_4_, ...), custom_call_target="tpu_custom_call" | custom-call | tf_op jit(solution)/shard_map/pallas_call | solution.py:156
  (20 shorter events, 0.2 us)
Async XLA Ops:
  6.5 8.1 %copy-start = (s32[2048]{0:T(1024)S(1)}, s32[2048]{0:T(1024)}, u32[]{:S(2)}) copy-start(s32[2048]{0:T(1024)} %param.10) | copy-start | bytes 24580
  6.5 71.6 %all-gather.2.cloned.1.call-start = ((), (), s32[]{:S(2)}) async-start(), calls=%async_computation | async-start | bytes 7798784 | tf_op jit(solution)/shard_map/all_gather | solution.py:224
  7.6 10.1 %collective-permute-start = (bf16[112,1024]{1,0:T(8,128)(2,1)S(1)}, bf16[112,1024]{1,0:T(8,128)(2,1)S(1)}, u32[]{:S(2)}, u32[]{:S(2)}) collective-permute-start(bf16[112,1024]{1,0:T(8,128)(2,1)S(1)} %reshape.629), channel_id=1, source_target_pairs={{0,256},{256,0},{1,257},{257,1},{2,258},{258,2},{3,259},{259,3},{4... | collective-permute-start | bytes 688136 | tf_op jit(solution)/shard_map/ppermute | solution.py:208
  16.4 61.7 %copy-start.1 = (bf16[4,2,64,256]{3,2,1,0:T(8,128)(2,1)}, bf16[4,2,64,256]{3,2,1,0:T(8,128)(2,1)S(1)}, u32[]{:S(2)}) copy-start(bf16[4,2,64,256]{3,2,1,0:T(8,128)(2,1)S(1)} %pad_maximum_fusion.2.refs_5_) | copy-start | bytes 786436
  18.5 11.7 %collective-permute-start.2 = (bf16[4,2,64,256]{3,2,1,0:T(8,128)(2,1)S(1)}, bf16[4,2,64,256]{3,2,1,0:T(8,128)(2,1)S(1)}, u32[]{:S(2)}, u32[]{:S(2)}) collective-permute-start(bf16[4,2,64,256]{3,2,1,0:T(8,128)(2,1)S(1)} %pad_maximum_fusion.2.refs_5_), channel_id=1, source_target_pairs={{0,7},{1,0},{2,1},{3,2},{4,3},{5,4},{6,5},{7,6},{8,15},{9,8},{10,9... | collective-permute-start | bytes 786440 | tf_op jit(solution)/shard_map/ppermute | solution.py:230
  21.8 10.9 %collective-permute-start.1 = (bf16[4,2,64,256]{3,2,1,0:T(8,128)(2,1)S(1)}, bf16[4,2,64,256]{3,2,1,0:T(8,128)(2,1)S(1)}, u32[]{:S(2)}, u32[]{:S(2)}) collective-permute-start(bf16[4,2,64,256]{3,2,1,0:T(8,128)(2,1)S(1)} %pad_maximum_fusion.2.refs_5_), channel_id=1, source_target_pairs={{0,8},{8,0},{1,9},{9,1},{2,10},{10,2},{3,11},{11,3},{4,12},{12,4},... | collective-permute-start | bytes 786440 | tf_op jit(solution)/shard_map/ppermute | solution.py:228
  26.5 9.5 %collective-permute-start.3 = (bf16[4,2,64,256]{3,2,1,0:T(8,128)(2,1)S(1)}, bf16[4,2,64,256]{3,2,1,0:T(8,128)(2,1)S(1)}, u32[]{:S(2)}, u32[]{:S(2)}) collective-permute-start(bf16[4,2,64,256]{3,2,1,0:T(8,128)(2,1)S(1)} %pad_maximum_fusion.2.refs_5_), channel_id=1, source_target_pairs={{0,1},{1,2},{2,3},{3,4},{4,5},{5,6},{6,7},{7,0},{8,9},{9,10},{10,1... | collective-permute-start | bytes 786440 | tf_op jit(solution)/shard_map/ppermute | solution.py:229
  30.3 47.9 %copy-start.2 = (bf16[4,2,64,256]{3,2,1,0:T(8,128)(2,1)}, bf16[4,2,64,256]{3,2,1,0:T(8,128)(2,1)S(1)}, u32[]{:S(2)}) copy-start(bf16[4,2,64,256]{3,2,1,0:T(8,128)(2,1)S(1)} %collective-permute-done.2.refs_13_) | copy-start | bytes 786436
  32.7 45.5 %copy-start.3 = (bf16[4,2,64,256]{3,2,1,0:T(8,128)(2,1)}, bf16[4,2,64,256]{3,2,1,0:T(8,128)(2,1)S(1)}, u32[]{:S(2)}) copy-start(bf16[4,2,64,256]{3,2,1,0:T(8,128)(2,1)S(1)} %collective-permute-done.1.refs_6_) | copy-start | bytes 786436
  32.7 9.8 %collective-permute-start.9 = (bf16[4,2,64,256]{3,2,1,0:T(8,128)(2,1)S(1)}, bf16[4,2,64,256]{3,2,1,0:T(8,128)(2,1)S(1)}, u32[]{:S(2)}, u32[]{:S(2)}) collective-permute-start(bf16[4,2,64,256]{3,2,1,0:T(8,128)(2,1)S(1)} %collective-permute-done.1.refs_6_), channel_id=1, source_target_pairs={{0,7},{1,0},{2,1},{3,2},{4,3},{5,4},{6,5},{7,6},{8,15},{9,8},{10,9... | collective-permute-start | bytes 786440 | tf_op jit(solution)/shard_map/ppermute | solution.py:235
  36.0 42.2 %copy-start.4 = (bf16[4,2,64,256]{3,2,1,0:T(8,128)(2,1)}, bf16[4,2,64,256]{3,2,1,0:T(8,128)(2,1)S(1)}, u32[]{:S(2)}) copy-start(bf16[4,2,64,256]{3,2,1,0:T(8,128)(2,1)S(1)} %collective-permute-done.3.refs_7_) | copy-start | bytes 786436
  36.0 12.4 %collective-permute-start.5 = (bf16[4,2,64,256]{3,2,1,0:T(8,128)(2,1)S(1)}, bf16[4,2,64,256]{3,2,1,0:T(8,128)(2,1)S(1)}, u32[]{:S(2)}, u32[]{:S(2)}) collective-permute-start(bf16[4,2,64,256]{3,2,1,0:T(8,128)(2,1)S(1)} %collective-permute-done.3.refs_7_), channel_id=1, source_target_pairs={{0,1},{1,2},{2,3},{3,4},{4,5},{5,6},{6,7},{7,0},{8,9},{9,10},{10,1... | collective-permute-start | bytes 786440 | tf_op jit(solution)/shard_map/ppermute | solution.py:237
  40.6 13.0 %collective-permute-start.4 = (bf16[4,2,64,256]{3,2,1,0:T(8,128)(2,1)S(1)}, bf16[4,2,64,256]{3,2,1,0:T(8,128)(2,1)S(1)}, u32[]{:S(2)}, u32[]{:S(2)}) collective-permute-start(bf16[4,2,64,256]{3,2,1,0:T(8,128)(2,1)S(1)} %collective-permute-done.1.refs_6_), channel_id=1, source_target_pairs={{0,1},{1,2},{2,3},{3,4},{4,5},{5,6},{6,7},{7,0},{8,9},{9,10},{10,1... | collective-permute-start | bytes 786440 | tf_op jit(solution)/shard_map/ppermute | solution.py:234
  42.5 35.7 %copy-start.5 = (bf16[4,2,64,256]{3,2,1,0:T(8,128)(2,1)}, bf16[4,2,64,256]{3,2,1,0:T(8,128)(2,1)S(1)}, u32[]{:S(2)}) copy-start(bf16[4,2,64,256]{3,2,1,0:T(8,128)(2,1)S(1)} %collective-permute-done.9.refs_14_) | copy-start | bytes 786436
  42.5 13.0 %collective-permute-start.11 = (bf16[4,2,64,256]{3,2,1,0:T(8,128)(2,1)S(1)}, bf16[4,2,64,256]{3,2,1,0:T(8,128)(2,1)S(1)}, u32[]{:S(2)}, u32[]{:S(2)}) collective-permute-start(bf16[4,2,64,256]{3,2,1,0:T(8,128)(2,1)S(1)} %collective-permute-done.9.refs_14_), channel_id=1, source_target_pairs={{0,7},{1,0},{2,1},{3,2},{4,3},{5,4},{6,5},{7,6},{8,15},{9,8},{10,9... | collective-permute-start | bytes 786440 | tf_op jit(solution)/shard_map/ppermute | solution.py:238
  46.4 13.0 %collective-permute-start.10 = (bf16[4,2,64,256]{3,2,1,0:T(8,128)(2,1)S(1)}, bf16[4,2,64,256]{3,2,1,0:T(8,128)(2,1)S(1)}, u32[]{:S(2)}, u32[]{:S(2)}) collective-permute-start(bf16[4,2,64,256]{3,2,1,0:T(8,128)(2,1)S(1)} %collective-permute-done.2.refs_13_), channel_id=1, source_target_pairs={{0,7},{1,0},{2,1},{3,2},{4,3},{5,4},{6,5},{7,6},{8,15},{9,8},{10,9... | collective-permute-start | bytes 786440 | tf_op jit(solution)/shard_map/ppermute | solution.py:238
  48.4 29.8 %copy-start.6 = (bf16[4,2,64,256]{3,2,1,0:T(8,128)(2,1)}, bf16[4,2,64,256]{3,2,1,0:T(8,128)(2,1)S(1)}, u32[]{:S(2)}) copy-start(bf16[4,2,64,256]{3,2,1,0:T(8,128)(2,1)S(1)} %collective-permute-done.5.refs_9_) | copy-start | bytes 786436
  48.4 13.0 %collective-permute-start.7 = (bf16[4,2,64,256]{3,2,1,0:T(8,128)(2,1)S(1)}, bf16[4,2,64,256]{3,2,1,0:T(8,128)(2,1)S(1)}, u32[]{:S(2)}, u32[]{:S(2)}) collective-permute-start(bf16[4,2,64,256]{3,2,1,0:T(8,128)(2,1)S(1)} %collective-permute-done.5.refs_9_), channel_id=1, source_target_pairs={{0,1},{1,2},{2,3},{3,4},{4,5},{5,6},{6,7},{7,0},{8,9},{9,10},{10,1... | collective-permute-start | bytes 786440 | tf_op jit(solution)/shard_map/ppermute | solution.py:237
  53.5 24.7 %copy-start.7 = (bf16[4,2,64,256]{3,2,1,0:T(8,128)(2,1)}, bf16[4,2,64,256]{3,2,1,0:T(8,128)(2,1)S(1)}, u32[]{:S(2)}) copy-start(bf16[4,2,64,256]{3,2,1,0:T(8,128)(2,1)S(1)} %collective-permute-done.4.refs_8_) | copy-start | bytes 786436
  53.5 13.0 %collective-permute-start.6 = (bf16[4,2,64,256]{3,2,1,0:T(8,128)(2,1)S(1)}, bf16[4,2,64,256]{3,2,1,0:T(8,128)(2,1)S(1)}, u32[]{:S(2)}, u32[]{:S(2)}) collective-permute-start(bf16[4,2,64,256]{3,2,1,0:T(8,128)(2,1)S(1)} %collective-permute-done.4.refs_8_), channel_id=1, source_target_pairs={{0,1},{1,2},{2,3},{3,4},{4,5},{5,6},{6,7},{7,0},{8,9},{9,10},{10,1... | collective-permute-start | bytes 786440 | tf_op jit(solution)/shard_map/ppermute | solution.py:237
  55.6 22.7 %copy-start.8 = (bf16[4,2,64,256]{3,2,1,0:T(8,128)(2,1)}, bf16[4,2,64,256]{3,2,1,0:T(8,128)(2,1)S(1)}, u32[]{:S(2)}) copy-start(bf16[4,2,64,256]{3,2,1,0:T(8,128)(2,1)S(1)} %collective-permute-done.11.refs_16_) | copy-start | bytes 786436
  55.6 13.0 %collective-permute-start.13 = (bf16[4,2,64,256]{3,2,1,0:T(8,128)(2,1)S(1)}, bf16[4,2,64,256]{3,2,1,0:T(8,128)(2,1)S(1)}, u32[]{:S(2)}, u32[]{:S(2)}) collective-permute-start(bf16[4,2,64,256]{3,2,1,0:T(8,128)(2,1)S(1)} %collective-permute-done.11.refs_16_), channel_id=1, source_target_pairs={{0,7},{1,0},{2,1},{3,2},{4,3},{5,4},{6,5},{7,6},{8,15},{9,8},{10,9... | collective-permute-start | bytes 786440 | tf_op jit(solution)/shard_map/ppermute | solution.py:238
  59.4 18.8 %copy-start.9 = (bf16[4,2,64,256]{3,2,1,0:T(8,128)(2,1)}, bf16[4,2,64,256]{3,2,1,0:T(8,128)(2,1)S(1)}, u32[]{:S(2)}) copy-start(bf16[4,2,64,256]{3,2,1,0:T(8,128)(2,1)S(1)} %collective-permute-done.10.refs_15_) | copy-start | bytes 786436
  59.4 13.0 %collective-permute-start.12 = (bf16[4,2,64,256]{3,2,1,0:T(8,128)(2,1)S(1)}, bf16[4,2,64,256]{3,2,1,0:T(8,128)(2,1)S(1)}, u32[]{:S(2)}, u32[]{:S(2)}) collective-permute-start(bf16[4,2,64,256]{3,2,1,0:T(8,128)(2,1)S(1)} %collective-permute-done.10.refs_15_), channel_id=1, source_target_pairs={{0,7},{1,0},{2,1},{3,2},{4,3},{5,4},{6,5},{7,6},{8,15},{9,8},{10,9... | collective-permute-start | bytes 786440 | tf_op jit(solution)/shard_map/ppermute | solution.py:238
  61.4 11.1 %copy-start.10 = (bf16[4,2,64,256]{3,2,1,0:T(8,128)(2,1)}, bf16[4,2,64,256]{3,2,1,0:T(8,128)(2,1)S(1)}, u32[]{:S(2)}) copy-start(bf16[4,2,64,256]{3,2,1,0:T(8,128)(2,1)S(1)} %collective-permute-done.7.refs_11_) | copy-start | bytes 786436
  61.4 11.1 %collective-permute-start.14 = (bf16[4,2,64,256]{3,2,1,0:T(8,128)(2,1)S(1)}, bf16[4,2,64,256]{3,2,1,0:T(8,128)(2,1)S(1)}, u32[]{:S(2)}, u32[]{:S(2)}) collective-permute-start(bf16[4,2,64,256]{3,2,1,0:T(8,128)(2,1)S(1)} %collective-permute-done.7.refs_11_), channel_id=1, source_target_pairs={{0,1},{1,2},{2,3},{3,4},{4,5},{5,6},{6,7},{7,0},{8,9},{9,10},{10,1... | collective-permute-start | bytes 786440 | tf_op jit(solution)/shard_map/ppermute | solution.py:240
  66.5 5.9 %copy-start.11 = (bf16[4,2,64,256]{3,2,1,0:T(8,128)(2,1)}, bf16[4,2,64,256]{3,2,1,0:T(8,128)(2,1)S(1)}, u32[]{:S(2)}) copy-start(bf16[4,2,64,256]{3,2,1,0:T(8,128)(2,1)S(1)} %collective-permute-done.6.refs_10_) | copy-start | bytes 786436
  66.6 8.5 %collective-permute-start.8 = (bf16[4,2,64,256]{3,2,1,0:T(8,128)(2,1)S(1)}, bf16[4,2,64,256]{3,2,1,0:T(8,128)(2,1)S(1)}, u32[]{:S(2)}, u32[]{:S(2)}) collective-permute-start(bf16[4,2,64,256]{3,2,1,0:T(8,128)(2,1)S(1)} %collective-permute-done.6.refs_10_), channel_id=1, source_target_pairs={{0,1},{1,2},{2,3},{3,4},{4,5},{5,6},{6,7},{7,0},{8,9},{9,10},{10,1... | collective-permute-start | bytes 786440 | tf_op jit(solution)/shard_map/ppermute | solution.py:237
  68.6 6.5 %copy-start.12 = (bf16[4,2,64,256]{3,2,1,0:T(8,128)(2,1)}, bf16[4,2,64,256]{3,2,1,0:T(8,128)(2,1)S(1)}, u32[]{:S(2)}) copy-start(bf16[4,2,64,256]{3,2,1,0:T(8,128)(2,1)S(1)} %collective-permute-done.13.refs_18_) | copy-start | bytes 786436
  68.6 9.6 %collective-permute-start.15 = (bf16[4,2,64,256]{3,2,1,0:T(8,128)(2,1)S(1)}, bf16[4,2,64,256]{3,2,1,0:T(8,128)(2,1)}, u32[]{:S(2)}, u32[]{:S(2)}) collective-permute-start(bf16[4,2,64,256]{3,2,1,0:T(8,128)(2,1)S(1)} %collective-permute-done.13.refs_18_), channel_id=1, source_target_pairs={{0,7},{1,0},{2,1},{3,2},{4,3},{5,4},{6,5},{7,6},{8,15},{9,8},{10,9... | collective-permute-start | bytes 786440 | tf_op jit(solution)/shard_map/ppermute | solution.py:242
  72.5 2.6 %copy-start.13 = (bf16[4,2,64,256]{3,2,1,0:T(8,128)(2,1)}, bf16[4,2,64,256]{3,2,1,0:T(8,128)(2,1)S(1)}, u32[]{:S(2)}) copy-start(bf16[4,2,64,256]{3,2,1,0:T(8,128)(2,1)S(1)} %collective-permute-done.12.refs_17_) | copy-start | bytes 786436
  72.5 2.5 %copy-start.14 = (bf16[4,2,64,256]{3,2,1,0:T(8,128)(2,1)}, bf16[4,2,64,256]{3,2,1,0:T(8,128)(2,1)S(1)}, u32[]{:S(2)}) copy-start(bf16[4,2,64,256]{3,2,1,0:T(8,128)(2,1)S(1)} %collective-permute-done.14.refs_19_) | copy-start | bytes 786436
  75.0 0.7 copy-start.15
Sparse Core Ops, SparseCore 0:
  18.7 58.1 all-gather.1

commit v7 on v6

--- a/solution.py
+++ b/solution.py
@@ -17,6 +17,7 @@
 B = 256
 CHUNK = C // N_TEST
 ROWS = SURV * SLOT
+LATE = (7, 12, 14, 15)
 OFFSETS = (0, -1, -2, -3, 1, 2, 3, 4)
 
 
@@ -182,7 +183,7 @@
         in_hbm(images),
         in_hbm(readout),
         in_vmem(bases),
-        *[in_hbm(value) for value in pieces],
+        *[value if number in LATE else in_hbm(value) for number, value in enumerate(pieces)],
     )
 
 

time: 98.7 us -> 99.2 us (level)
    unnamed x34 -> x28, local copies, waits for them, and re-layouts: 3.03 us -> 2.32 us
where the time goes in v7:
time: 99.2 us; the launch traced here: 97.8 us
  starting transfers between devices  54.6 us (55%)
  between operations  13.8 us (14%)
  Pallas kernels  12.8 us (13%)
  waiting for transfers between devices  8.04 us (8%)
  local copies, waits for them, and re-layouts  5.44 us (5%)
  other arithmetic  3.09 us (3%)
    ppermute x4, starting transfers between devices, on_device(): rising.append(lax.ppermute(rising[-1], 'y', up))  13.7 us
    pallas_call x1, Pallas kernels, run_score(): pl.pallas_call(score, in_specs=[smem, smem, hbm, hbm, vmem] + [hbm] * N_T...  12.8 us
    ppermute x4, starting transfers between devices, on_device(): falling.append(lax.ppermute(falling[-1], 'y', down))  11.6 us
    ppermute x1, starting transfers between devices, on_device(): farthest = lax.ppermute(rising[-1], 'y', up)  5.13 us
    ppermute x1, starting transfers between devices, on_device(): other = lax.ppermute(message, 'xh', swap)  4.64 us
    ppermute x1, starting transfers between devices, on_device(): farthest = lax.ppermute(falling[-1], 'y', down)  3.85 us
    ppermute x1, starting transfers between devices, on_device(): first_up = lax.ppermute(message, 'y', up)  3.8 us
    ppermute x1, starting transfers between devices, on_device(): partner_rows = lax.ppermute(own_rows, 'xl', swap)  3.4 us
  transfers between devices with their start and end apart: 17, of which 3 were waited for; matrix products, arithmetic and copies ran while one was open for 7% of the time, Pallas kernels for 0%

profile of v7, /device:TPU:56, one launch (start us, length us, event | category | flops | bytes accessed | tf_op | source)
XLA Modules:
  0.0 97.8 jit_solution(17176093419419906610)
XLA Ops:
  6.5 0.0 copy-start
  6.5 0.0 all-gather.2.cloned.1.call-start
  6.5 1.0 %copy.12 = bf16[4,28,1024]{2,1,0:T(8,128)(2,1)S(1)} copy(bf16[4,28,1024]{2,0,1:T(4,128)(2,1)} %param.9) | data formatting | bytes 458752 | tf_op args[0]
  7.6 3.4 %collective-permute-start = (bf16[112,1024]{1,0:T(8,128)(2,1)S(1)}, bf16[112,1024]{1,0:T(8,128)(2,1)S(1)}, u32[]{:S(2)}, u32[]{:S(2)}) collective-permute-start(bf16[112,1024]{1,0:T(8,128)(2,1)S(1)} %reshape.629), channel_id=1, source_target_pairs={{0,256},{256,0},{1,257},{257,1},{2,258},{258,2},{3,259},{259,3},{4... | collective-permute-start | bytes 688136 | tf_op jit(solution)/shard_map/ppermute | solution.py:209
  11.0 0.8 reshape.631
  11.8 0.8 reshape.630
  12.6 0.8 reshape.632
  13.4 1.2 %copy.13 = bf16[256,1024]{0,1:T(8,128)(2,1)S(1)} copy(bf16[256,1024]{1,0:T(8,128)(2,1)} %param.13) | data formatting | bytes 1048576 | tf_op args[4]
  14.6 0.0 copy-done
  14.7 0.8 gather_fusion
  15.4 1.0 %pad_maximum_fusion.2.refs_5_ = bf16[4,2,64,256]{3,2,1,0:T(8,128)(2,1)S(1)} fusion(bf16[4,1,64,256]{3,2,1,0:T(8,128)(2,1)} %bitcast.17, bf16[4,1,64,256]{3,2,1,0:T(8,128)(2,1)} %bitcast.18), kind=kLoop, calls=%fused_computation.3 | loop fusion | flops 131072 | bytes 524288 | tf_op jit(solution)/shard_map/stack | solution.py:206
  16.4 0.0 copy-start.1
  16.5 1.2 %pad_maximum_fusion.refs_4_ = bf16[2,1024,256]{2,1,0:T(8,128)(2,1)S(1)} fusion(bf16[1,1024,256]{2,1,0:T(8,128)(2,1)S(1)} %bitcast.14, bf16[1,1024,256]{2,1,0:T(8,128)(2,1)} %bitcast.16), kind=kLoop, calls=%fused_computation.1 | loop fusion | flops 524288 | bytes 2097152 | tf_op jit(solution)/shard_map/stack | solution.py:221
  17.7 0.0 collective-permute-done
  17.7 0.8 pad_maximum_fusion.1
  18.5 0.0 all-gather.2.cloned.1.call-update
  18.5 3.3 %collective-permute-start.2 = (bf16[4,2,64,256]{3,2,1,0:T(8,128)(2,1)S(1)}, bf16[4,2,64,256]{3,2,1,0:T(8,128)(2,1)S(1)}, u32[]{:S(2)}, u32[]{:S(2)}) collective-permute-start(bf16[4,2,64,256]{3,2,1,0:T(8,128)(2,1)S(1)} %pad_maximum_fusion.2.refs_5_), channel_id=1, source_target_pairs={{0,7},{1,0},{2,1},{3,2},{4,3},{5,4},{6,5},{7,6},{8,15},{9,8},{10,9... | collective-permute-start | bytes 786440 | tf_op jit(solution)/shard_map/ppermute | solution.py:231
  21.8 4.6 %collective-permute-start.1 = (bf16[4,2,64,256]{3,2,1,0:T(8,128)(2,1)S(1)}, bf16[4,2,64,256]{3,2,1,0:T(8,128)(2,1)S(1)}, u32[]{:S(2)}, u32[]{:S(2)}) collective-permute-start(bf16[4,2,64,256]{3,2,1,0:T(8,128)(2,1)S(1)} %pad_maximum_fusion.2.refs_5_), channel_id=1, source_target_pairs={{0,8},{8,0},{1,9},{9,1},{2,10},{10,2},{3,11},{11,3},{4,12},{12,4},... | collective-permute-start | bytes 786440 | tf_op jit(solution)/shard_map/ppermute | solution.py:229
  26.4 3.8 %collective-permute-start.3 = (bf16[4,2,64,256]{3,2,1,0:T(8,128)(2,1)S(1)}, bf16[4,2,64,256]{3,2,1,0:T(8,128)(2,1)S(1)}, u32[]{:S(2)}, u32[]{:S(2)}) collective-permute-start(bf16[4,2,64,256]{3,2,1,0:T(8,128)(2,1)S(1)} %pad_maximum_fusion.2.refs_5_), channel_id=1, source_target_pairs={{0,1},{1,2},{2,3},{3,4},{4,5},{5,6},{6,7},{7,0},{8,9},{9,10},{10,1... | collective-permute-start | bytes 786440 | tf_op jit(solution)/shard_map/ppermute | solution.py:230
  30.3 0.0 collective-permute-done.2.refs_13_
  30.3 0.0 copy-start.2
  30.3 2.4 %collective-permute-done.1.refs_6_ = bf16[4,2,64,256]{3,2,1,0:T(8,128)(2,1)S(1)} collective-permute-done((bf16[4,2,64,256]{3,2,1,0:T(8,128)(2,1)S(1)}, bf16[4,2,64,256]{3,2,1,0:T(8,128)(2,1)S(1)}, u32[]{:S(2)}, u32[]{:S(2)}) %collective-permute-start.1) | collective-permute-done | bytes 262176 | tf_op jit(solution)/shard_map/ppermute | solution.py:229
  32.7 3.2 %collective-permute-start.9 = (bf16[4,2,64,256]{3,2,1,0:T(8,128)(2,1)S(1)}, bf16[4,2,64,256]{3,2,1,0:T(8,128)(2,1)S(1)}, u32[]{:S(2)}, u32[]{:S(2)}) collective-permute-start(bf16[4,2,64,256]{3,2,1,0:T(8,128)(2,1)S(1)} %collective-permute-done.1.refs_6_), channel_id=1, source_target_pairs={{0,7},{1,0},{2,1},{3,2},{4,3},{5,4},{6,5},{7,6},{8,15},{9,8},{10,9... | collective-permute-start | bytes 786440 | tf_op jit(solution)/shard_map/ppermute | solution.py:236
  35.9 0.0 collective-permute-done.3.refs_7_
  36.0 0.0 copy-start.4
  36.0 4.6 %collective-permute-start.5 = (bf16[4,2,64,256]{3,2,1,0:T(8,128)(2,1)S(1)}, bf16[4,2,64,256]{3,2,1,0:T(8,128)(2,1)S(1)}, u32[]{:S(2)}, u32[]{:S(2)}) collective-permute-start(bf16[4,2,64,256]{3,2,1,0:T(8,128)(2,1)S(1)} %collective-permute-done.3.refs_7_), channel_id=1, source_target_pairs={{0,1},{1,2},{2,3},{3,4},{4,5},{5,6},{6,7},{7,0},{8,9},{9,10},{10,1... | collective-permute-start | bytes 786440 | tf_op jit(solution)/shard_map/ppermute | solution.py:238
  40.6 1.9 %collective-permute-start.4 = (bf16[4,2,64,256]{3,2,1,0:T(8,128)(2,1)S(1)}, bf16[4,2,64,256]{3,2,1,0:T(8,128)(2,1)S(1)}, u32[]{:S(2)}, u32[]{:S(2)}) collective-permute-start(bf16[4,2,64,256]{3,2,1,0:T(8,128)(2,1)S(1)} %collective-permute-done.1.refs_6_), channel_id=1, source_target_pairs={{0,1},{1,2},{2,3},{3,4},{4,5},{5,6},{6,7},{7,0},{8,9},{9,10},{10,1... | collective-permute-start | bytes 786440 | tf_op jit(solution)/shard_map/ppermute | solution.py:235
  42.5 0.0 collective-permute-done.9.refs_14_
  42.5 0.0 copy-start.5
  42.5 3.9 %collective-permute-start.11 = (bf16[4,2,64,256]{3,2,1,0:T(8,128)(2,1)S(1)}, bf16[4,2,64,256]{3,2,1,0:T(8,128)(2,1)S(1)}, u32[]{:S(2)}, u32[]{:S(2)}) collective-permute-start(bf16[4,2,64,256]{3,2,1,0:T(8,128)(2,1)S(1)} %collective-permute-done.9.refs_14_), channel_id=1, source_target_pairs={{0,7},{1,0},{2,1},{3,2},{4,3},{5,4},{6,5},{7,6},{8,15},{9,8},{10,9... | collective-permute-start | bytes 786440 | tf_op jit(solution)/shard_map/ppermute | solution.py:239
  46.4 1.9 %collective-permute-start.10 = (bf16[4,2,64,256]{3,2,1,0:T(8,128)(2,1)S(1)}, bf16[4,2,64,256]{3,2,1,0:T(8,128)(2,1)S(1)}, u32[]{:S(2)}, u32[]{:S(2)}) collective-permute-start(bf16[4,2,64,256]{3,2,1,0:T(8,128)(2,1)S(1)} %collective-permute-done.2.refs_13_), channel_id=1, source_target_pairs={{0,7},{1,0},{2,1},{3,2},{4,3},{5,4},{6,5},{7,6},{8,15},{9,8},{10,9... | collective-permute-start | bytes 786440 | tf_op jit(solution)/shard_map/ppermute | solution.py:239
  48.4 0.0 collective-permute-done.5.refs_9_
  48.4 0.0 copy-start.6
  48.4 5.1 %collective-permute-start.7 = (bf16[4,2,64,256]{3,2,1,0:T(8,128)(2,1)S(1)}, bf16[4,2,64,256]{3,2,1,0:T(8,128)(2,1)S(1)}, u32[]{:S(2)}, u32[]{:S(2)}) collective-permute-start(bf16[4,2,64,256]{3,2,1,0:T(8,128)(2,1)S(1)} %collective-permute-done.5.refs_9_), channel_id=1, source_target_pairs={{0,1},{1,2},{2,3},{3,4},{4,5},{5,6},{6,7},{7,0},{8,9},{9,10},{10,1... | collective-permute-start | bytes 786440 | tf_op jit(solution)/shard_map/ppermute | solution.py:238
  53.5 0.0 collective-permute-done.4.refs_8_
  53.5 0.0 copy-start.7
  53.5 2.0 %collective-permute-start.6 = (bf16[4,2,64,256]{3,2,1,0:T(8,128)(2,1)S(1)}, bf16[4,2,64,256]{3,2,1,0:T(8,128)(2,1)S(1)}, u32[]{:S(2)}, u32[]{:S(2)}) collective-permute-start(bf16[4,2,64,256]{3,2,1,0:T(8,128)(2,1)S(1)} %collective-permute-done.4.refs_8_), channel_id=1, source_target_pairs={{0,1},{1,2},{2,3},{3,4},{4,5},{5,6},{6,7},{7,0},{8,9},{9,10},{10,1... | collective-permute-start | bytes 786440 | tf_op jit(solution)/shard_map/ppermute | solution.py:238
  55.5 0.0 collective-permute-done.11.refs_16_
  55.6 0.0 copy-start.8
  55.6 3.8 %collective-permute-start.13 = (bf16[4,2,64,256]{3,2,1,0:T(8,128)(2,1)S(1)}, bf16[4,2,64,256]{3,2,1,0:T(8,128)(2,1)S(1)}, u32[]{:S(2)}, u32[]{:S(2)}) collective-permute-start(bf16[4,2,64,256]{3,2,1,0:T(8,128)(2,1)S(1)} %collective-permute-done.11.refs_16_), channel_id=1, source_target_pairs={{0,7},{1,0},{2,1},{3,2},{4,3},{5,4},{6,5},{7,6},{8,15},{9,8},{10,9... | collective-permute-start | bytes 786440 | tf_op jit(solution)/shard_map/ppermute | solution.py:239
  59.4 0.0 collective-permute-done.10.refs_15_
  59.4 0.0 copy-start.9
  59.4 1.9 %collective-permute-start.12 = (bf16[4,2,64,256]{3,2,1,0:T(8,128)(2,1)S(1)}, bf16[4,2,64,256]{3,2,1,0:T(8,128)(2,1)S(1)}, u32[]{:S(2)}, u32[]{:S(2)}) collective-permute-start(bf16[4,2,64,256]{3,2,1,0:T(8,128)(2,1)S(1)} %collective-permute-done.10.refs_15_), channel_id=1, source_target_pairs={{0,7},{1,0},{2,1},{3,2},{4,3},{5,4},{6,5},{7,6},{8,15},{9,8},{10,9... | collective-permute-start | bytes 786440 | tf_op jit(solution)/shard_map/ppermute | solution.py:239
  61.4 0.0 copy-done.6
  61.4 0.0 collective-permute-done.7.refs_11_
  61.4 0.0 copy-start.10
  61.4 5.1 %collective-permute-start.14 = (bf16[4,2,64,256]{3,2,1,0:T(8,128)(2,1)S(1)}, bf16[4,2,64,256]{3,2,1,0:T(8,128)(2,1)S(1)}, u32[]{:S(2)}, u32[]{:S(2)}) collective-permute-start(bf16[4,2,64,256]{3,2,1,0:T(8,128)(2,1)S(1)} %collective-permute-done.7.refs_11_), channel_id=1, source_target_pairs={{0,1},{1,2},{2,3},{3,4},{4,5},{5,6},{6,7},{7,0},{8,9},{9,10},{10,1... | collective-permute-start | bytes 786440 | tf_op jit(solution)/shard_map/ppermute | solution.py:241
  66.5 0.0 copy-done.7
  66.5 0.0 collective-permute-done.6.refs_10_
  66.6 0.0 copy-start.11
  66.6 2.0 %collective-permute-start.8 = (bf16[4,2,64,256]{3,2,1,0:T(8,128)(2,1)S(1)}, bf16[4,2,64,256]{3,2,1,0:T(8,128)(2,1)S(1)}, u32[]{:S(2)}, u32[]{:S(2)}) collective-permute-start(bf16[4,2,64,256]{3,2,1,0:T(8,128)(2,1)S(1)} %collective-permute-done.6.refs_10_), channel_id=1, source_target_pairs={{0,1},{1,2},{2,3},{3,4},{4,5},{5,6},{6,7},{7,0},{8,9},{9,10},{10,1... | collective-permute-start | bytes 786440 | tf_op jit(solution)/shard_map/ppermute | solution.py:238
  68.6 0.0 copy-done.8
  68.6 0.0 collective-permute-done.13.refs_18_
  68.6 0.0 copy-start.12
  68.6 3.8 %collective-permute-start.15 = (bf16[4,2,64,256]{3,2,1,0:T(8,128)(2,1)S(1)}, bf16[4,2,64,256]{3,2,1,0:T(8,128)(2,1)S(1)}, u32[]{:S(2)}, u32[]{:S(2)}) collective-permute-start(bf16[4,2,64,256]{3,2,1,0:T(8,128)(2,1)S(1)} %collective-permute-done.13.refs_18_), channel_id=1, source_target_pairs={{0,7},{1,0},{2,1},{3,2},{4,3},{5,4},{6,5},{7,6},{8,15},{9,8},{10,9... | collective-permute-start | bytes 786440 | tf_op jit(solution)/shard_map/ppermute | solution.py:243
  72.5 0.0 collective-permute-done.12.refs_17_
  72.5 0.0 collective-permute-done.14.refs_19_
  72.5 2.6 %collective-permute-done.8.refs_12_ = bf16[4,2,64,256]{3,2,1,0:T(8,128)(2,1)S(1)} collective-permute-done((bf16[4,2,64,256]{3,2,1,0:T(8,128)(2,1)S(1)}, bf16[4,2,64,256]{3,2,1,0:T(8,128)(2,1)S(1)}, u32[]{:S(2)}, u32[]{:S(2)}) %collective-permute-start.8) | collective-permute-done | bytes 262176 | tf_op jit(solution)/shard_map/ppermute | solution.py:238
  75.0 0.0 copy-done.9
  75.1 3.0 %collective-permute-done.15.refs_20_ = bf16[4,2,64,256]{3,2,1,0:T(8,128)(2,1)S(1)} collective-permute-done((bf16[4,2,64,256]{3,2,1,0:T(8,128)(2,1)S(1)}, bf16[4,2,64,256]{3,2,1,0:T(8,128)(2,1)S(1)}, u32[]{:S(2)}, u32[]{:S(2)}) %collective-permute-start.15) | collective-permute-done | bytes 262176 | tf_op jit(solution)/shard_map/ppermute | solution.py:243
  78.1 0.0 copy-done.2
  78.1 0.0 copy-done.4
  78.1 0.0 copy-done.5
  78.1 12.8 %shard_map.91 = f32[4,2,14]{2,1,0:T(2,128)} custom-call(s32[3,56]{1,0:T(4,128)S(1)} %pad_add_fusion.refs_0_, f32[1,128]{1,0:T(1,128)S(1)} %pad.4.refs_1_, bf16[3584,1024]{1,0:T(8,128)(2,1)} %all-gather.2.cloned.1.call-done.refs_2_, bf16[1000,1024]{1,0:T(8,128)(2,1)} %bitcast.15, bf16[2,1024,256]{2,1,0:T(8,128)(2,1)S(1)} %pad_maximum_fusion.refs_4_, ...), custom_call_target="tpu_custom_call" | custom-call | tf_op jit(solution)/shard_map/pallas_call | solution.py:157
  (14 shorter events, 0.1 us)
Async XLA Ops:
  6.5 8.1 %copy-start = (s32[2048]{0:T(1024)S(1)}, s32[2048]{0:T(1024)}, u32[]{:S(2)}) copy-start(s32[2048]{0:T(1024)} %param.10) | copy-start | bytes 24580
  6.5 71.5 %all-gather.2.cloned.1.call-start = ((), (), s32[]{:S(2)}) async-start(), calls=%async_computation | async-start | bytes 7798784 | tf_op jit(solution)/shard_map/all_gather | solution.py:225
  7.6 10.1 %collective-permute-start = (bf16[112,1024]{1,0:T(8,128)(2,1)S(1)}, bf16[112,1024]{1,0:T(8,128)(2,1)S(1)}, u32[]{:S(2)}, u32[]{:S(2)}) collective-permute-start(bf16[112,1024]{1,0:T(8,128)(2,1)S(1)} %reshape.629), channel_id=1, source_target_pairs={{0,256},{256,0},{1,257},{257,1},{2,258},{258,2},{3,259},{259,3},{4... | collective-permute-start | bytes 688136 | tf_op jit(solution)/shard_map/ppermute | solution.py:209
  16.4 61.7 %copy-start.1 = (bf16[4,2,64,256]{3,2,1,0:T(8,128)(2,1)}, bf16[4,2,64,256]{3,2,1,0:T(8,128)(2,1)S(1)}, u32[]{:S(2)}) copy-start(bf16[4,2,64,256]{3,2,1,0:T(8,128)(2,1)S(1)} %pad_maximum_fusion.2.refs_5_) | copy-start | bytes 786436
  18.5 11.7 %collective-permute-start.2 = (bf16[4,2,64,256]{3,2,1,0:T(8,128)(2,1)S(1)}, bf16[4,2,64,256]{3,2,1,0:T(8,128)(2,1)S(1)}, u32[]{:S(2)}, u32[]{:S(2)}) collective-permute-start(bf16[4,2,64,256]{3,2,1,0:T(8,128)(2,1)S(1)} %pad_maximum_fusion.2.refs_5_), channel_id=1, source_target_pairs={{0,7},{1,0},{2,1},{3,2},{4,3},{5,4},{6,5},{7,6},{8,15},{9,8},{10,9... | collective-permute-start | bytes 786440 | tf_op jit(solution)/shard_map/ppermute | solution.py:231
  21.8 10.9 %collective-permute-start.1 = (bf16[4,2,64,256]{3,2,1,0:T(8,128)(2,1)S(1)}, bf16[4,2,64,256]{3,2,1,0:T(8,128)(2,1)S(1)}, u32[]{:S(2)}, u32[]{:S(2)}) collective-permute-start(bf16[4,2,64,256]{3,2,1,0:T(8,128)(2,1)S(1)} %pad_maximum_fusion.2.refs_5_), channel_id=1, source_target_pairs={{0,8},{8,0},{1,9},{9,1},{2,10},{10,2},{3,11},{11,3},{4,12},{12,4},... | collective-permute-start | bytes 786440 | tf_op jit(solution)/shard_map/ppermute | solution.py:229
  26.4 9.5 %collective-permute-start.3 = (bf16[4,2,64,256]{3,2,1,0:T(8,128)(2,1)S(1)}, bf16[4,2,64,256]{3,2,1,0:T(8,128)(2,1)S(1)}, u32[]{:S(2)}, u32[]{:S(2)}) collective-permute-start(bf16[4,2,64,256]{3,2,1,0:T(8,128)(2,1)S(1)} %pad_maximum_fusion.2.refs_5_), channel_id=1, source_target_pairs={{0,1},{1,2},{2,3},{3,4},{4,5},{5,6},{6,7},{7,0},{8,9},{9,10},{10,1... | collective-permute-start | bytes 786440 | tf_op jit(solution)/shard_map/ppermute | solution.py:230
  30.3 47.8 %copy-start.2 = (bf16[4,2,64,256]{3,2,1,0:T(8,128)(2,1)}, bf16[4,2,64,256]{3,2,1,0:T(8,128)(2,1)S(1)}, u32[]{:S(2)}) copy-start(bf16[4,2,64,256]{3,2,1,0:T(8,128)(2,1)S(1)} %collective-permute-done.2.refs_13_) | copy-start | bytes 786436
  32.7 45.4 %copy-start.3 = (bf16[4,2,64,256]{3,2,1,0:T(8,128)(2,1)}, bf16[4,2,64,256]{3,2,1,0:T(8,128)(2,1)S(1)}, u32[]{:S(2)}) copy-start(bf16[4,2,64,256]{3,2,1,0:T(8,128)(2,1)S(1)} %collective-permute-done.1.refs_6_) | copy-start | bytes 786436
  32.7 9.8 %collective-permute-start.9 = (bf16[4,2,64,256]{3,2,1,0:T(8,128)(2,1)S(1)}, bf16[4,2,64,256]{3,2,1,0:T(8,128)(2,1)S(1)}, u32[]{:S(2)}, u32[]{:S(2)}) collective-permute-start(bf16[4,2,64,256]{3,2,1,0:T(8,128)(2,1)S(1)} %collective-permute-done.1.refs_6_), channel_id=1, source_target_pairs={{0,7},{1,0},{2,1},{3,2},{4,3},{5,4},{6,5},{7,6},{8,15},{9,8},{10,9... | collective-permute-start | bytes 786440 | tf_op jit(solution)/shard_map/ppermute | solution.py:236
  36.0 42.1 %copy-start.4 = (bf16[4,2,64,256]{3,2,1,0:T(8,128)(2,1)}, bf16[4,2,64,256]{3,2,1,0:T(8,128)(2,1)S(1)}, u32[]{:S(2)}) copy-start(bf16[4,2,64,256]{3,2,1,0:T(8,128)(2,1)S(1)} %collective-permute-done.3.refs_7_) | copy-start | bytes 786436
  36.0 12.4 %collective-permute-start.5 = (bf16[4,2,64,256]{3,2,1,0:T(8,128)(2,1)S(1)}, bf16[4,2,64,256]{3,2,1,0:T(8,128)(2,1)S(1)}, u32[]{:S(2)}, u32[]{:S(2)}) collective-permute-start(bf16[4,2,64,256]{3,2,1,0:T(8,128)(2,1)S(1)} %collective-permute-done.3.refs_7_), channel_id=1, source_target_pairs={{0,1},{1,2},{2,3},{3,4},{4,5},{5,6},{6,7},{7,0},{8,9},{9,10},{10,1... | collective-permute-start | bytes 786440 | tf_op jit(solution)/shard_map/ppermute | solution.py:238
  40.6 13.0 %collective-permute-start.4 = (bf16[4,2,64,256]{3,2,1,0:T(8,128)(2,1)S(1)}, bf16[4,2,64,256]{3,2,1,0:T(8,128)(2,1)S(1)}, u32[]{:S(2)}, u32[]{:S(2)}) collective-permute-start(bf16[4,2,64,256]{3,2,1,0:T(8,128)(2,1)S(1)} %collective-permute-done.1.refs_6_), channel_id=1, source_target_pairs={{0,1},{1,2},{2,3},{3,4},{4,5},{5,6},{6,7},{7,0},{8,9},{9,10},{10,1... | collective-permute-start | bytes 786440 | tf_op jit(solution)/shard_map/ppermute | solution.py:235
  42.5 35.6 %copy-start.5 = (bf16[4,2,64,256]{3,2,1,0:T(8,128)(2,1)}, bf16[4,2,64,256]{3,2,1,0:T(8,128)(2,1)S(1)}, u32[]{:S(2)}) copy-start(bf16[4,2,64,256]{3,2,1,0:T(8,128)(2,1)S(1)} %collective-permute-done.9.refs_14_) | copy-start | bytes 786436
  42.5 13.0 %collective-permute-start.11 = (bf16[4,2,64,256]{3,2,1,0:T(8,128)(2,1)S(1)}, bf16[4,2,64,256]{3,2,1,0:T(8,128)(2,1)S(1)}, u32[]{:S(2)}, u32[]{:S(2)}) collective-permute-start(bf16[4,2,64,256]{3,2,1,0:T(8,128)(2,1)S(1)} %collective-permute-done.9.refs_14_), channel_id=1, source_target_pairs={{0,7},{1,0},{2,1},{3,2},{4,3},{5,4},{6,5},{7,6},{8,15},{9,8},{10,9... | collective-permute-start | bytes 786440 | tf_op jit(solution)/shard_map/ppermute | solution.py:239
  46.4 13.0 %collective-permute-start.10 = (bf16[4,2,64,256]{3,2,1,0:T(8,128)(2,1)S(1)}, bf16[4,2,64,256]{3,2,1,0:T(8,128)(2,1)S(1)}, u32[]{:S(2)}, u32[]{:S(2)}) collective-permute-start(bf16[4,2,64,256]{3,2,1,0:T(8,128)(2,1)S(1)} %collective-permute-done.2.refs_13_), channel_id=1, source_target_pairs={{0,7},{1,0},{2,1},{3,2},{4,3},{5,4},{6,5},{7,6},{8,15},{9,8},{10,9... | collective-permute-start | bytes 786440 | tf_op jit(solution)/shard_map/ppermute | solution.py:239
  48.4 13.0 %copy-start.6 = (bf16[4,2,64,256]{3,2,1,0:T(8,128)(2,1)}, bf16[4,2,64,256]{3,2,1,0:T(8,128)(2,1)S(1)}, u32[]{:S(2)}) copy-start(bf16[4,2,64,256]{3,2,1,0:T(8,128)(2,1)S(1)} %collective-permute-done.5.refs_9_) | copy-start | bytes 786436
  48.4 13.0 %collective-permute-start.7 = (bf16[4,2,64,256]{3,2,1,0:T(8,128)(2,1)S(1)}, bf16[4,2,64,256]{3,2,1,0:T(8,128)(2,1)S(1)}, u32[]{:S(2)}, u32[]{:S(2)}) collective-permute-start(bf16[4,2,64,256]{3,2,1,0:T(8,128)(2,1)S(1)} %collective-permute-done.5.refs_9_), channel_id=1, source_target_pairs={{0,1},{1,2},{2,3},{3,4},{4,5},{5,6},{6,7},{7,0},{8,9},{9,10},{10,1... | collective-permute-start | bytes 786440 | tf_op jit(solution)/shard_map/ppermute | solution.py:238
  53.5 13.0 %copy-start.7 = (bf16[4,2,64,256]{3,2,1,0:T(8,128)(2,1)}, bf16[4,2,64,256]{3,2,1,0:T(8,128)(2,1)S(1)}, u32[]{:S(2)}) copy-start(bf16[4,2,64,256]{3,2,1,0:T(8,128)(2,1)S(1)} %collective-permute-done.4.refs_8_) | copy-start | bytes 786436
  53.5 13.0 %collective-permute-start.6 = (bf16[4,2,64,256]{3,2,1,0:T(8,128)(2,1)S(1)}, bf16[4,2,64,256]{3,2,1,0:T(8,128)(2,1)S(1)}, u32[]{:S(2)}, u32[]{:S(2)}) collective-permute-start(bf16[4,2,64,256]{3,2,1,0:T(8,128)(2,1)S(1)} %collective-permute-done.4.refs_8_), channel_id=1, source_target_pairs={{0,1},{1,2},{2,3},{3,4},{4,5},{5,6},{6,7},{7,0},{8,9},{9,10},{10,1... | collective-permute-start | bytes 786440 | tf_op jit(solution)/shard_map/ppermute | solution.py:238
  55.6 13.0 %copy-start.8 = (bf16[4,2,64,256]{3,2,1,0:T(8,128)(2,1)}, bf16[4,2,64,256]{3,2,1,0:T(8,128)(2,1)S(1)}, u32[]{:S(2)}) copy-start(bf16[4,2,64,256]{3,2,1,0:T(8,128)(2,1)S(1)} %collective-permute-done.11.refs_16_) | copy-start | bytes 786436
  55.6 13.0 %collective-permute-start.13 = (bf16[4,2,64,256]{3,2,1,0:T(8,128)(2,1)S(1)}, bf16[4,2,64,256]{3,2,1,0:T(8,128)(2,1)S(1)}, u32[]{:S(2)}, u32[]{:S(2)}) collective-permute-start(bf16[4,2,64,256]{3,2,1,0:T(8,128)(2,1)S(1)} %collective-permute-done.11.refs_16_), channel_id=1, source_target_pairs={{0,7},{1,0},{2,1},{3,2},{4,3},{5,4},{6,5},{7,6},{8,15},{9,8},{10,9... | collective-permute-start | bytes 786440 | tf_op jit(solution)/shard_map/ppermute | solution.py:239
  59.4 15.6 %copy-start.9 = (bf16[4,2,64,256]{3,2,1,0:T(8,128)(2,1)}, bf16[4,2,64,256]{3,2,1,0:T(8,128)(2,1)S(1)}, u32[]{:S(2)}) copy-start(bf16[4,2,64,256]{3,2,1,0:T(8,128)(2,1)S(1)} %collective-permute-done.10.refs_15_) | copy-start | bytes 786436
  59.4 13.0 %collective-permute-start.12 = (bf16[4,2,64,256]{3,2,1,0:T(8,128)(2,1)S(1)}, bf16[4,2,64,256]{3,2,1,0:T(8,128)(2,1)S(1)}, u32[]{:S(2)}, u32[]{:S(2)}) collective-permute-start(bf16[4,2,64,256]{3,2,1,0:T(8,128)(2,1)S(1)} %collective-permute-done.10.refs_15_), channel_id=1, source_target_pairs={{0,7},{1,0},{2,1},{3,2},{4,3},{5,4},{6,5},{7,6},{8,15},{9,8},{10,9... | collective-permute-start | bytes 786440 | tf_op jit(solution)/shard_map/ppermute | solution.py:239
  61.4 13.6 %copy-start.10 = (bf16[4,2,64,256]{3,2,1,0:T(8,128)(2,1)}, bf16[4,2,64,256]{3,2,1,0:T(8,128)(2,1)S(1)}, u32[]{:S(2)}) copy-start(bf16[4,2,64,256]{3,2,1,0:T(8,128)(2,1)S(1)} %collective-permute-done.7.refs_11_) | copy-start | bytes 786436
  61.4 11.1 %collective-permute-start.14 = (bf16[4,2,64,256]{3,2,1,0:T(8,128)(2,1)S(1)}, bf16[4,2,64,256]{3,2,1,0:T(8,128)(2,1)S(1)}, u32[]{:S(2)}, u32[]{:S(2)}) collective-permute-start(bf16[4,2,64,256]{3,2,1,0:T(8,128)(2,1)S(1)} %collective-permute-done.7.refs_11_), channel_id=1, source_target_pairs={{0,1},{1,2},{2,3},{3,4},{4,5},{5,6},{6,7},{7,0},{8,9},{9,10},{10,1... | collective-permute-start | bytes 786440 | tf_op jit(solution)/shard_map/ppermute | solution.py:241
  66.6 8.5 %copy-start.11 = (bf16[4,2,64,256]{3,2,1,0:T(8,128)(2,1)}, bf16[4,2,64,256]{3,2,1,0:T(8,128)(2,1)S(1)}, u32[]{:S(2)}) copy-start(bf16[4,2,64,256]{3,2,1,0:T(8,128)(2,1)S(1)} %collective-permute-done.6.refs_10_) | copy-start | bytes 786436
  66.6 8.5 %collective-permute-start.8 = (bf16[4,2,64,256]{3,2,1,0:T(8,128)(2,1)S(1)}, bf16[4,2,64,256]{3,2,1,0:T(8,128)(2,1)S(1)}, u32[]{:S(2)}, u32[]{:S(2)}) collective-permute-start(bf16[4,2,64,256]{3,2,1,0:T(8,128)(2,1)S(1)} %collective-permute-done.6.refs_10_), channel_id=1, source_target_pairs={{0,1},{1,2},{2,3},{3,4},{4,5},{5,6},{6,7},{7,0},{8,9},{9,10},{10,1... | collective-permute-start | bytes 786440 | tf_op jit(solution)/shard_map/ppermute | solution.py:238
  68.6 6.5 %copy-start.12 = (bf16[4,2,64,256]{3,2,1,0:T(8,128)(2,1)}, bf16[4,2,64,256]{3,2,1,0:T(8,128)(2,1)S(1)}, u32[]{:S(2)}) copy-start(bf16[4,2,64,256]{3,2,1,0:T(8,128)(2,1)S(1)} %collective-permute-done.13.refs_18_) | copy-start | bytes 786436
  68.6 9.5 %collective-permute-start.15 = (bf16[4,2,64,256]{3,2,1,0:T(8,128)(2,1)S(1)}, bf16[4,2,64,256]{3,2,1,0:T(8,128)(2,1)S(1)}, u32[]{:S(2)}, u32[]{:S(2)}) collective-permute-start(bf16[4,2,64,256]{3,2,1,0:T(8,128)(2,1)S(1)} %collective-permute-done.13.refs_18_), channel_id=1, source_target_pairs={{0,7},{1,0},{2,1},{3,2},{4,3},{5,4},{6,5},{7,6},{8,15},{9,8},{10,9... | collective-permute-start | bytes 786440 | tf_op jit(solution)/shard_map/ppermute | solution.py:243
Sparse Core Ops, SparseCore 0:
  18.7 58.1 all-gather.1

commit v8 on v7

--- a/solution.py
+++ b/solution.py
@@ -229,7 +229,6 @@
     other = lax.ppermute(message, "xh", swap)
     first_up = lax.ppermute(message, "y", up)
     first_down = lax.ppermute(message, "y", down)
-    other, first_down = lax.optimization_barrier((other, first_down))
     flows = []
     for number, seed in enumerate((message, other)):
         rising = [first_up if number == 0 else lax.ppermute(seed, "y", up)]

time: 99.2 us -> 99.2 us (level)
  waiting for transfers between devices: 8.04 us -> 9.88 us
  starting transfers between devices: 54.6 us -> 52.8 us
    ppermute x1, waiting for transfers between devices: 2.41 us -> 3.66 us  [on_device(): other = lax.ppermute(message, 'xh', swap)]
    ppermute x4, starting transfers between devices: 11.6 us -> 10.5 us  [on_device(): falling.append(lax.ppermute(falling[-1], 'y', down))]
where the time goes in v8:
time: 99.2 us; the launch traced here: 97.9 us
  starting transfers between devices  52.8 us (53%)
  between operations  13.8 us (14%)
  Pallas kernels  12.8 us (13%)
  waiting for transfers between devices  9.88 us (10%)
  local copies, waits for them, and re-layouts  5.44 us (5%)
  other arithmetic  3.09 us (3%)
    ppermute x4, starting transfers between devices, on_device(): rising.append(lax.ppermute(rising[-1], 'y', up))  14 us
    pallas_call x1, Pallas kernels, run_score(): pl.pallas_call(score, in_specs=[smem, smem, hbm, hbm, vmem] + [hbm] * N_T...  12.8 us
    ppermute x4, starting transfers between devices, on_device(): falling.append(lax.ppermute(falling[-1], 'y', down))  10.5 us
    ppermute x1, starting transfers between devices, on_device(): farthest = lax.ppermute(rising[-1], 'y', up)  5.13 us
    ppermute x1, starting transfers between devices, on_device(): other = lax.ppermute(message, 'xh', swap)  4.64 us
    ppermute x1, waiting for transfers between devices, on_device(): other = lax.ppermute(message, 'xh', swap)  3.66 us
    ppermute x1, waiting for transfers between devices, on_device(): farthest = lax.ppermute(falling[-1], 'y', down)  3.6 us
    ppermute x1, starting transfers between devices, on_device(): partner_rows = lax.ppermute(own_rows, 'xl', swap)  3.4 us
  transfers between devices with their start and end apart: 17, of which 3 were waited for; matrix products, arithmetic and copies ran while one was open for 7% of the time, Pallas kernels for 0%

profile of v8, /device:TPU:56, one launch (start us, length us, event | category | flops | bytes accessed | tf_op | source)
XLA Modules:
  0.0 97.9 jit_solution(2146097461195684397)
XLA Ops:
  6.5 0.0 copy-start
  6.5 0.0 all-gather.2.cloned.1.call-start
  6.5 1.0 %copy.12 = bf16[4,28,1024]{2,1,0:T(8,128)(2,1)S(1)} copy(bf16[4,28,1024]{2,0,1:T(4,128)(2,1)} %param.9) | data formatting | bytes 458752 | tf_op args[0]
  7.6 3.4 %collective-permute-start = (bf16[112,1024]{1,0:T(8,128)(2,1)S(1)}, bf16[112,1024]{1,0:T(8,128)(2,1)S(1)}, u32[]{:S(2)}, u32[]{:S(2)}) collective-permute-start(bf16[112,1024]{1,0:T(8,128)(2,1)S(1)} %reshape.629), channel_id=1, source_target_pairs={{0,256},{256,0},{1,257},{257,1},{2,258},{258,2},{3,259},{259,3},{4... | collective-permute-start | bytes 688136 | tf_op jit(solution)/shard_map/ppermute | solution.py:209
  11.0 0.8 reshape.631
  11.8 0.8 reshape.630
  12.6 0.8 reshape.632
  13.4 1.2 %copy.13 = bf16[256,1024]{0,1:T(8,128)(2,1)S(1)} copy(bf16[256,1024]{1,0:T(8,128)(2,1)} %param.13) | data formatting | bytes 1048576 | tf_op args[4]
  14.6 0.0 copy-done
  14.7 0.8 gather_fusion
  15.4 1.0 %pad_maximum_fusion.2.refs_5_ = bf16[4,2,64,256]{3,2,1,0:T(8,128)(2,1)S(1)} fusion(bf16[4,1,64,256]{3,2,1,0:T(8,128)(2,1)} %bitcast.17, bf16[4,1,64,256]{3,2,1,0:T(8,128)(2,1)} %bitcast.18), kind=kLoop, calls=%fused_computation.3 | loop fusion | flops 131072 | bytes 524288 | tf_op jit(solution)/shard_map/stack | solution.py:206
  16.4 0.0 copy-start.1
  16.5 1.2 %pad_maximum_fusion.refs_4_ = bf16[2,1024,256]{2,1,0:T(8,128)(2,1)S(1)} fusion(bf16[1,1024,256]{2,1,0:T(8,128)(2,1)S(1)} %bitcast.14, bf16[1,1024,256]{2,1,0:T(8,128)(2,1)} %bitcast.16), kind=kLoop, calls=%fused_computation.1 | loop fusion | flops 524288 | bytes 2097152 | tf_op jit(solution)/shard_map/stack | solution.py:221
  17.7 0.0 collective-permute-done
  17.7 0.8 pad_maximum_fusion.1
  18.5 0.0 all-gather.2.cloned.1.call-update
  18.5 4.6 %collective-permute-start.1 = (bf16[4,2,64,256]{3,2,1,0:T(8,128)(2,1)S(1)}, bf16[4,2,64,256]{3,2,1,0:T(8,128)(2,1)S(1)}, u32[]{:S(2)}, u32[]{:S(2)}) collective-permute-start(bf16[4,2,64,256]{3,2,1,0:T(8,128)(2,1)S(1)} %pad_maximum_fusion.2.refs_5_), channel_id=1, source_target_pairs={{0,8},{8,0},{1,9},{9,1},{2,10},{10,2},{3,11},{11,3},{4,12},{12,4},... | collective-permute-start | bytes 786440 | tf_op jit(solution)/shard_map/ppermute | solution.py:229
  23.2 2.9 %collective-permute-start.2 = (bf16[4,2,64,256]{3,2,1,0:T(8,128)(2,1)S(1)}, bf16[4,2,64,256]{3,2,1,0:T(8,128)(2,1)S(1)}, u32[]{:S(2)}, u32[]{:S(2)}) collective-permute-start(bf16[4,2,64,256]{3,2,1,0:T(8,128)(2,1)S(1)} %pad_maximum_fusion.2.refs_5_), channel_id=1, source_target_pairs={{0,1},{1,2},{2,3},{3,4},{4,5},{5,6},{6,7},{7,0},{8,9},{9,10},{10,1... | collective-permute-start | bytes 786440 | tf_op jit(solution)/shard_map/ppermute | solution.py:230
  26.0 3.7 %collective-permute-done.1.refs_6_ = bf16[4,2,64,256]{3,2,1,0:T(8,128)(2,1)S(1)} collective-permute-done((bf16[4,2,64,256]{3,2,1,0:T(8,128)(2,1)S(1)}, bf16[4,2,64,256]{3,2,1,0:T(8,128)(2,1)S(1)}, u32[]{:S(2)}, u32[]{:S(2)}) %collective-permute-start.1) | collective-permute-done | bytes 262176 | tf_op jit(solution)/shard_map/ppermute | solution.py:229
  29.7 3.2 %collective-permute-start.9 = (bf16[4,2,64,256]{3,2,1,0:T(8,128)(2,1)S(1)}, bf16[4,2,64,256]{3,2,1,0:T(8,128)(2,1)S(1)}, u32[]{:S(2)}, u32[]{:S(2)}) collective-permute-start(bf16[4,2,64,256]{3,2,1,0:T(8,128)(2,1)S(1)} %collective-permute-done.1.refs_6_), channel_id=1, source_target_pairs={{0,7},{1,0},{2,1},{3,2},{4,3},{5,4},{6,5},{7,6},{8,15},{9,8},{10,9... | collective-permute-start | bytes 786440 | tf_op jit(solution)/shard_map/ppermute | solution.py:235
  33.0 3.3 %collective-permute-start.8 = (bf16[4,2,64,256]{3,2,1,0:T(8,128)(2,1)S(1)}, bf16[4,2,64,256]{3,2,1,0:T(8,128)(2,1)S(1)}, u32[]{:S(2)}, u32[]{:S(2)}) collective-permute-start(bf16[4,2,64,256]{3,2,1,0:T(8,128)(2,1)S(1)} %pad_maximum_fusion.2.refs_5_), channel_id=1, source_target_pairs={{0,7},{1,0},{2,1},{3,2},{4,3},{5,4},{6,5},{7,6},{8,15},{9,8},{10,9... | collective-permute-start | bytes 786440 | tf_op jit(solution)/shard_map/ppermute | solution.py:231
  36.2 0.0 collective-permute-done.2.refs_7_
  36.2 0.0 copy-start.3
  36.2 3.8 %collective-permute-start.4 = (bf16[4,2,64,256]{3,2,1,0:T(8,128)(2,1)S(1)}, bf16[4,2,64,256]{3,2,1,0:T(8,128)(2,1)S(1)}, u32[]{:S(2)}, u32[]{:S(2)}) collective-permute-start(bf16[4,2,64,256]{3,2,1,0:T(8,128)(2,1)S(1)} %collective-permute-done.2.refs_7_), channel_id=1, source_target_pairs={{0,1},{1,2},{2,3},{3,4},{4,5},{5,6},{6,7},{7,0},{8,9},{9,10},{10,1... | collective-permute-start | bytes 786440 | tf_op jit(solution)/shard_map/ppermute | solution.py:237
  40.0 2.6 %collective-permute-start.3 = (bf16[4,2,64,256]{3,2,1,0:T(8,128)(2,1)S(1)}, bf16[4,2,64,256]{3,2,1,0:T(8,128)(2,1)S(1)}, u32[]{:S(2)}, u32[]{:S(2)}) collective-permute-start(bf16[4,2,64,256]{3,2,1,0:T(8,128)(2,1)S(1)} %collective-permute-done.1.refs_6_), channel_id=1, source_target_pairs={{0,1},{1,2},{2,3},{3,4},{4,5},{5,6},{6,7},{7,0},{8,9},{9,10},{10,1... | collective-permute-start | bytes 786440 | tf_op jit(solution)/shard_map/ppermute | solution.py:234
  42.6 0.0 collective-permute-done.9.refs_14_
  42.6 0.0 copy-start.4
  42.7 3.3 %collective-permute-start.11 = (bf16[4,2,64,256]{3,2,1,0:T(8,128)(2,1)S(1)}, bf16[4,2,64,256]{3,2,1,0:T(8,128)(2,1)S(1)}, u32[]{:S(2)}, u32[]{:S(2)}) collective-permute-start(bf16[4,2,64,256]{3,2,1,0:T(8,128)(2,1)S(1)} %collective-permute-done.9.refs_14_), channel_id=1, source_target_pairs={{0,7},{1,0},{2,1},{3,2},{4,3},{5,4},{6,5},{7,6},{8,15},{9,8},{10,9... | collective-permute-start | bytes 786440 | tf_op jit(solution)/shard_map/ppermute | solution.py:238
  45.9 0.0 collective-permute-done.8.refs_13_
  45.9 0.0 copy-start.5
  45.9 2.0 %collective-permute-start.10 = (bf16[4,2,64,256]{3,2,1,0:T(8,128)(2,1)S(1)}, bf16[4,2,64,256]{3,2,1,0:T(8,128)(2,1)S(1)}, u32[]{:S(2)}, u32[]{:S(2)}) collective-permute-start(bf16[4,2,64,256]{3,2,1,0:T(8,128)(2,1)S(1)} %collective-permute-done.8.refs_13_), channel_id=1, source_target_pairs={{0,7},{1,0},{2,1},{3,2},{4,3},{5,4},{6,5},{7,6},{8,15},{9,8},{10,9... | collective-permute-start | bytes 786440 | tf_op jit(solution)/shard_map/ppermute | solution.py:238
  48.0 0.0 collective-permute-done.4.refs_9_
  48.0 0.0 copy-start.6
  48.0 5.0 %collective-permute-start.6 = (bf16[4,2,64,256]{3,2,1,0:T(8,128)(2,1)S(1)}, bf16[4,2,64,256]{3,2,1,0:T(8,128)(2,1)S(1)}, u32[]{:S(2)}, u32[]{:S(2)}) collective-permute-start(bf16[4,2,64,256]{3,2,1,0:T(8,128)(2,1)S(1)} %collective-permute-done.4.refs_9_), channel_id=1, source_target_pairs={{0,1},{1,2},{2,3},{3,4},{4,5},{5,6},{6,7},{7,0},{8,9},{9,10},{10,1... | collective-permute-start | bytes 786440 | tf_op jit(solution)/shard_map/ppermute | solution.py:237
  53.0 0.0 collective-permute-done.3.refs_8_
  53.0 0.0 copy-start.7
  53.1 2.6 %collective-permute-start.5 = (bf16[4,2,64,256]{3,2,1,0:T(8,128)(2,1)S(1)}, bf16[4,2,64,256]{3,2,1,0:T(8,128)(2,1)S(1)}, u32[]{:S(2)}, u32[]{:S(2)}) collective-permute-start(bf16[4,2,64,256]{3,2,1,0:T(8,128)(2,1)S(1)} %collective-permute-done.3.refs_8_), channel_id=1, source_target_pairs={{0,1},{1,2},{2,3},{3,4},{4,5},{5,6},{6,7},{7,0},{8,9},{9,10},{10,1... | collective-permute-start | bytes 786440 | tf_op jit(solution)/shard_map/ppermute | solution.py:237
  55.6 0.0 collective-permute-done.11.refs_16_
  55.7 0.0 copy-start.8
  55.7 3.3 %collective-permute-start.13 = (bf16[4,2,64,256]{3,2,1,0:T(8,128)(2,1)S(1)}, bf16[4,2,64,256]{3,2,1,0:T(8,128)(2,1)S(1)}, u32[]{:S(2)}, u32[]{:S(2)}) collective-permute-start(bf16[4,2,64,256]{3,2,1,0:T(8,128)(2,1)S(1)} %collective-permute-done.11.refs_16_), channel_id=1, source_target_pairs={{0,7},{1,0},{2,1},{3,2},{4,3},{5,4},{6,5},{7,6},{8,15},{9,8},{10,9... | collective-permute-start | bytes 786440 | tf_op jit(solution)/shard_map/ppermute | solution.py:238
  58.9 0.0 collective-permute-done.10.refs_15_
  58.9 0.0 copy-start.9
  59.0 1.9 %collective-permute-start.12 = (bf16[4,2,64,256]{3,2,1,0:T(8,128)(2,1)S(1)}, bf16[4,2,64,256]{3,2,1,0:T(8,128)(2,1)S(1)}, u32[]{:S(2)}, u32[]{:S(2)}) collective-permute-start(bf16[4,2,64,256]{3,2,1,0:T(8,128)(2,1)S(1)} %collective-permute-done.10.refs_15_), channel_id=1, source_target_pairs={{0,7},{1,0},{2,1},{3,2},{4,3},{5,4},{6,5},{7,6},{8,15},{9,8},{10,9... | collective-permute-start | bytes 786440 | tf_op jit(solution)/shard_map/ppermute | solution.py:238
  60.9 0.0 copy-done.6
  60.9 0.0 collective-permute-done.6.refs_11_
  60.9 0.0 copy-start.10
  60.9 5.1 %collective-permute-start.14 = (bf16[4,2,64,256]{3,2,1,0:T(8,128)(2,1)S(1)}, bf16[4,2,64,256]{3,2,1,0:T(8,128)(2,1)S(1)}, u32[]{:S(2)}, u32[]{:S(2)}) collective-permute-start(bf16[4,2,64,256]{3,2,1,0:T(8,128)(2,1)S(1)} %collective-permute-done.6.refs_11_), channel_id=1, source_target_pairs={{0,1},{1,2},{2,3},{3,4},{4,5},{5,6},{6,7},{7,0},{8,9},{9,10},{10,1... | collective-permute-start | bytes 786440 | tf_op jit(solution)/shard_map/ppermute | solution.py:240
  66.1 0.0 copy-done.7
  66.1 0.0 collective-permute-done.5.refs_10_
  66.1 0.0 copy-start.11
  66.1 2.6 %collective-permute-start.7 = (bf16[4,2,64,256]{3,2,1,0:T(8,128)(2,1)S(1)}, bf16[4,2,64,256]{3,2,1,0:T(8,128)(2,1)S(1)}, u32[]{:S(2)}, u32[]{:S(2)}) collective-permute-start(bf16[4,2,64,256]{3,2,1,0:T(8,128)(2,1)S(1)} %collective-permute-done.5.refs_10_), channel_id=1, source_target_pairs={{0,1},{1,2},{2,3},{3,4},{4,5},{5,6},{6,7},{7,0},{8,9},{9,10},{10,1... | collective-permute-start | bytes 786440 | tf_op jit(solution)/shard_map/ppermute | solution.py:237
  68.7 0.0 copy-done.8
  68.7 0.0 collective-permute-done.13.refs_18_
  68.7 0.0 copy-start.12
  68.7 3.3 %collective-permute-start.15 = (bf16[4,2,64,256]{3,2,1,0:T(8,128)(2,1)S(1)}, bf16[4,2,64,256]{3,2,1,0:T(8,128)(2,1)S(1)}, u32[]{:S(2)}, u32[]{:S(2)}) collective-permute-start(bf16[4,2,64,256]{3,2,1,0:T(8,128)(2,1)S(1)} %collective-permute-done.13.refs_18_), channel_id=1, source_target_pairs={{0,7},{1,0},{2,1},{3,2},{4,3},{5,4},{6,5},{7,6},{8,15},{9,8},{10,9... | collective-permute-start | bytes 786440 | tf_op jit(solution)/shard_map/ppermute | solution.py:242
  72.0 0.0 collective-permute-done.12.refs_17_
  72.0 0.0 collective-permute-done.14.refs_19_
  72.0 2.6 %collective-permute-done.7.refs_12_ = bf16[4,2,64,256]{3,2,1,0:T(8,128)(2,1)S(1)} collective-permute-done((bf16[4,2,64,256]{3,2,1,0:T(8,128)(2,1)S(1)}, bf16[4,2,64,256]{3,2,1,0:T(8,128)(2,1)S(1)}, u32[]{:S(2)}, u32[]{:S(2)}) %collective-permute-start.7) | collective-permute-done | bytes 262176 | tf_op jit(solution)/shard_map/ppermute | solution.py:237
  74.6 0.0 copy-done.9
  74.6 0.0 copy-done.10
  74.6 0.0 copy-done.11
  74.6 3.6 %collective-permute-done.15.refs_20_ = bf16[4,2,64,256]{3,2,1,0:T(8,128)(2,1)S(1)} collective-permute-done((bf16[4,2,64,256]{3,2,1,0:T(8,128)(2,1)S(1)}, bf16[4,2,64,256]{3,2,1,0:T(8,128)(2,1)S(1)}, u32[]{:S(2)}, u32[]{:S(2)}) %collective-permute-start.15) | collective-permute-done | bytes 262176 | tf_op jit(solution)/shard_map/ppermute | solution.py:242
  78.2 0.0 copy-done.2
  78.2 12.8 %shard_map.91 = f32[4,2,14]{2,1,0:T(2,128)} custom-call(s32[3,56]{1,0:T(4,128)S(1)} %pad_add_fusion.refs_0_, f32[1,128]{1,0:T(1,128)S(1)} %pad.4.refs_1_, bf16[3584,1024]{1,0:T(8,128)(2,1)} %all-gather.2.cloned.1.call-done.refs_2_, bf16[1000,1024]{1,0:T(8,128)(2,1)} %bitcast.15, bf16[2,1024,256]{2,1,0:T(8,128)(2,1)S(1)} %pad_maximum_fusion.refs_4_, ...), custom_call_target="tpu_custom_call" | custom-call | tf_op jit(solution)/shard_map/pallas_call | solution.py:157
  (14 shorter events, 0.1 us)
Async XLA Ops:
  6.5 8.1 %copy-start = (s32[2048]{0:T(1024)S(1)}, s32[2048]{0:T(1024)}, u32[]{:S(2)}) copy-start(s32[2048]{0:T(1024)} %param.10) | copy-start | bytes 24580
  6.5 71.6 %all-gather.2.cloned.1.call-start = ((), (), s32[]{:S(2)}) async-start(), calls=%async_computation | async-start | bytes 7798784 | tf_op jit(solution)/shard_map/all_gather | solution.py:225
  7.6 10.1 %collective-permute-start = (bf16[112,1024]{1,0:T(8,128)(2,1)S(1)}, bf16[112,1024]{1,0:T(8,128)(2,1)S(1)}, u32[]{:S(2)}, u32[]{:S(2)}) collective-permute-start(bf16[112,1024]{1,0:T(8,128)(2,1)S(1)} %reshape.629), channel_id=1, source_target_pairs={{0,256},{256,0},{1,257},{257,1},{2,258},{258,2},{3,259},{259,3},{4... | collective-permute-start | bytes 688136 | tf_op jit(solution)/shard_map/ppermute | solution.py:209
  16.4 61.8 %copy-start.1 = (bf16[4,2,64,256]{3,2,1,0:T(8,128)(2,1)}, bf16[4,2,64,256]{3,2,1,0:T(8,128)(2,1)S(1)}, u32[]{:S(2)}) copy-start(bf16[4,2,64,256]{3,2,1,0:T(8,128)(2,1)S(1)} %pad_maximum_fusion.2.refs_5_) | copy-start | bytes 786436
  18.5 11.2 %collective-permute-start.1 = (bf16[4,2,64,256]{3,2,1,0:T(8,128)(2,1)S(1)}, bf16[4,2,64,256]{3,2,1,0:T(8,128)(2,1)S(1)}, u32[]{:S(2)}, u32[]{:S(2)}) collective-permute-start(bf16[4,2,64,256]{3,2,1,0:T(8,128)(2,1)S(1)} %pad_maximum_fusion.2.refs_5_), channel_id=1, source_target_pairs={{0,8},{8,0},{1,9},{9,1},{2,10},{10,2},{3,11},{11,3},{4,12},{12,4},... | collective-permute-start | bytes 786440 | tf_op jit(solution)/shard_map/ppermute | solution.py:229
  23.2 13.0 %collective-permute-start.2 = (bf16[4,2,64,256]{3,2,1,0:T(8,128)(2,1)S(1)}, bf16[4,2,64,256]{3,2,1,0:T(8,128)(2,1)S(1)}, u32[]{:S(2)}, u32[]{:S(2)}) collective-permute-start(bf16[4,2,64,256]{3,2,1,0:T(8,128)(2,1)S(1)} %pad_maximum_fusion.2.refs_5_), channel_id=1, source_target_pairs={{0,1},{1,2},{2,3},{3,4},{4,5},{5,6},{6,7},{7,0},{8,9},{9,10},{10,1... | collective-permute-start | bytes 786440 | tf_op jit(solution)/shard_map/ppermute | solution.py:230
  29.7 48.5 %copy-start.2 = (bf16[4,2,64,256]{3,2,1,0:T(8,128)(2,1)}, bf16[4,2,64,256]{3,2,1,0:T(8,128)(2,1)S(1)}, u32[]{:S(2)}) copy-start(bf16[4,2,64,256]{3,2,1,0:T(8,128)(2,1)S(1)} %collective-permute-done.1.refs_6_) | copy-start | bytes 786436
  29.7 12.9 %collective-permute-start.9 = (bf16[4,2,64,256]{3,2,1,0:T(8,128)(2,1)S(1)}, bf16[4,2,64,256]{3,2,1,0:T(8,128)(2,1)S(1)}, u32[]{:S(2)}, u32[]{:S(2)}) collective-permute-start(bf16[4,2,64,256]{3,2,1,0:T(8,128)(2,1)S(1)} %collective-permute-done.1.refs_6_), channel_id=1, source_target_pairs={{0,7},{1,0},{2,1},{3,2},{4,3},{5,4},{6,5},{7,6},{8,15},{9,8},{10,9... | collective-permute-start | bytes 786440 | tf_op jit(solution)/shard_map/ppermute | solution.py:235
  33.0 13.0 %collective-permute-start.8 = (bf16[4,2,64,256]{3,2,1,0:T(8,128)(2,1)S(1)}, bf16[4,2,64,256]{3,2,1,0:T(8,128)(2,1)S(1)}, u32[]{:S(2)}, u32[]{:S(2)}) collective-permute-start(bf16[4,2,64,256]{3,2,1,0:T(8,128)(2,1)S(1)} %pad_maximum_fusion.2.refs_5_), channel_id=1, source_target_pairs={{0,7},{1,0},{2,1},{3,2},{4,3},{5,4},{6,5},{7,6},{8,15},{9,8},{10,9... | collective-permute-start | bytes 786440 | tf_op jit(solution)/shard_map/ppermute | solution.py:231
  36.2 42.0 %copy-start.3 = (bf16[4,2,64,256]{3,2,1,0:T(8,128)(2,1)}, bf16[4,2,64,256]{3,2,1,0:T(8,128)(2,1)S(1)}, u32[]{:S(2)}) copy-start(bf16[4,2,64,256]{3,2,1,0:T(8,128)(2,1)S(1)} %collective-permute-done.2.refs_7_) | copy-start | bytes 786436
  36.2 11.8 %collective-permute-start.4 = (bf16[4,2,64,256]{3,2,1,0:T(8,128)(2,1)S(1)}, bf16[4,2,64,256]{3,2,1,0:T(8,128)(2,1)S(1)}, u32[]{:S(2)}, u32[]{:S(2)}) collective-permute-start(bf16[4,2,64,256]{3,2,1,0:T(8,128)(2,1)S(1)} %collective-permute-done.2.refs_7_), channel_id=1, source_target_pairs={{0,1},{1,2},{2,3},{3,4},{4,5},{5,6},{6,7},{7,0},{8,9},{9,10},{10,1... | collective-permute-start | bytes 786440 | tf_op jit(solution)/shard_map/ppermute | solution.py:237
  40.0 13.0 %collective-permute-start.3 = (bf16[4,2,64,256]{3,2,1,0:T(8,128)(2,1)S(1)}, bf16[4,2,64,256]{3,2,1,0:T(8,128)(2,1)S(1)}, u32[]{:S(2)}, u32[]{:S(2)}) collective-permute-start(bf16[4,2,64,256]{3,2,1,0:T(8,128)(2,1)S(1)} %collective-permute-done.1.refs_6_), channel_id=1, source_target_pairs={{0,1},{1,2},{2,3},{3,4},{4,5},{5,6},{6,7},{7,0},{8,9},{9,10},{10,1... | collective-permute-start | bytes 786440 | tf_op jit(solution)/shard_map/ppermute | solution.py:234
  42.6 35.6 %copy-start.4 = (bf16[4,2,64,256]{3,2,1,0:T(8,128)(2,1)}, bf16[4,2,64,256]{3,2,1,0:T(8,128)(2,1)S(1)}, u32[]{:S(2)}) copy-start(bf16[4,2,64,256]{3,2,1,0:T(8,128)(2,1)S(1)} %collective-permute-done.9.refs_14_) | copy-start | bytes 786436
  42.7 13.0 %collective-permute-start.11 = (bf16[4,2,64,256]{3,2,1,0:T(8,128)(2,1)S(1)}, bf16[4,2,64,256]{3,2,1,0:T(8,128)(2,1)S(1)}, u32[]{:S(2)}, u32[]{:S(2)}) collective-permute-start(bf16[4,2,64,256]{3,2,1,0:T(8,128)(2,1)S(1)} %collective-permute-done.9.refs_14_), channel_id=1, source_target_pairs={{0,7},{1,0},{2,1},{3,2},{4,3},{5,4},{6,5},{7,6},{8,15},{9,8},{10,9... | collective-permute-start | bytes 786440 | tf_op jit(solution)/shard_map/ppermute | solution.py:238
  45.9 32.3 %copy-start.5 = (bf16[4,2,64,256]{3,2,1,0:T(8,128)(2,1)}, bf16[4,2,64,256]{3,2,1,0:T(8,128)(2,1)S(1)}, u32[]{:S(2)}) copy-start(bf16[4,2,64,256]{3,2,1,0:T(8,128)(2,1)S(1)} %collective-permute-done.8.refs_13_) | copy-start | bytes 786436
  45.9 13.0 %collective-permute-start.10 = (bf16[4,2,64,256]{3,2,1,0:T(8,128)(2,1)S(1)}, bf16[4,2,64,256]{3,2,1,0:T(8,128)(2,1)S(1)}, u32[]{:S(2)}, u32[]{:S(2)}) collective-permute-start(bf16[4,2,64,256]{3,2,1,0:T(8,128)(2,1)S(1)} %collective-permute-done.8.refs_13_), channel_id=1, source_target_pairs={{0,7},{1,0},{2,1},{3,2},{4,3},{5,4},{6,5},{7,6},{8,15},{9,8},{10,9... | collective-permute-start | bytes 786440 | tf_op jit(solution)/shard_map/ppermute | solution.py:238
  48.0 12.9 %copy-start.6 = (bf16[4,2,64,256]{3,2,1,0:T(8,128)(2,1)}, bf16[4,2,64,256]{3,2,1,0:T(8,128)(2,1)S(1)}, u32[]{:S(2)}) copy-start(bf16[4,2,64,256]{3,2,1,0:T(8,128)(2,1)S(1)} %collective-permute-done.4.refs_9_) | copy-start | bytes 786436
  48.0 12.9 %collective-permute-start.6 = (bf16[4,2,64,256]{3,2,1,0:T(8,128)(2,1)S(1)}, bf16[4,2,64,256]{3,2,1,0:T(8,128)(2,1)S(1)}, u32[]{:S(2)}, u32[]{:S(2)}) collective-permute-start(bf16[4,2,64,256]{3,2,1,0:T(8,128)(2,1)S(1)} %collective-permute-done.4.refs_9_), channel_id=1, source_target_pairs={{0,1},{1,2},{2,3},{3,4},{4,5},{5,6},{6,7},{7,0},{8,9},{9,10},{10,1... | collective-permute-start | bytes 786440 | tf_op jit(solution)/shard_map/ppermute | solution.py:237
  53.0 13.0 %copy-start.7 = (bf16[4,2,64,256]{3,2,1,0:T(8,128)(2,1)}, bf16[4,2,64,256]{3,2,1,0:T(8,128)(2,1)S(1)}, u32[]{:S(2)}) copy-start(bf16[4,2,64,256]{3,2,1,0:T(8,128)(2,1)S(1)} %collective-permute-done.3.refs_8_) | copy-start | bytes 786436
  53.1 13.0 %collective-permute-start.5 = (bf16[4,2,64,256]{3,2,1,0:T(8,128)(2,1)S(1)}, bf16[4,2,64,256]{3,2,1,0:T(8,128)(2,1)S(1)}, u32[]{:S(2)}, u32[]{:S(2)}) collective-permute-start(bf16[4,2,64,256]{3,2,1,0:T(8,128)(2,1)S(1)} %collective-permute-done.3.refs_8_), channel_id=1, source_target_pairs={{0,1},{1,2},{2,3},{3,4},{4,5},{5,6},{6,7},{7,0},{8,9},{9,10},{10,1... | collective-permute-start | bytes 786440 | tf_op jit(solution)/shard_map/ppermute | solution.py:237
  55.7 13.0 %copy-start.8 = (bf16[4,2,64,256]{3,2,1,0:T(8,128)(2,1)}, bf16[4,2,64,256]{3,2,1,0:T(8,128)(2,1)S(1)}, u32[]{:S(2)}) copy-start(bf16[4,2,64,256]{3,2,1,0:T(8,128)(2,1)S(1)} %collective-permute-done.11.refs_16_) | copy-start | bytes 786436
  55.7 13.0 %collective-permute-start.13 = (bf16[4,2,64,256]{3,2,1,0:T(8,128)(2,1)S(1)}, bf16[4,2,64,256]{3,2,1,0:T(8,128)(2,1)S(1)}, u32[]{:S(2)}, u32[]{:S(2)}) collective-permute-start(bf16[4,2,64,256]{3,2,1,0:T(8,128)(2,1)S(1)} %collective-permute-done.11.refs_16_), channel_id=1, source_target_pairs={{0,7},{1,0},{2,1},{3,2},{4,3},{5,4},{6,5},{7,6},{8,15},{9,8},{10,9... | collective-permute-start | bytes 786440 | tf_op jit(solution)/shard_map/ppermute | solution.py:238
  58.9 15.6 %copy-start.9 = (bf16[4,2,64,256]{3,2,1,0:T(8,128)(2,1)}, bf16[4,2,64,256]{3,2,1,0:T(8,128)(2,1)S(1)}, u32[]{:S(2)}) copy-start(bf16[4,2,64,256]{3,2,1,0:T(8,128)(2,1)S(1)} %collective-permute-done.10.refs_15_) | copy-start | bytes 786436
  59.0 13.0 %collective-permute-start.12 = (bf16[4,2,64,256]{3,2,1,0:T(8,128)(2,1)S(1)}, bf16[4,2,64,256]{3,2,1,0:T(8,128)(2,1)S(1)}, u32[]{:S(2)}, u32[]{:S(2)}) collective-permute-start(bf16[4,2,64,256]{3,2,1,0:T(8,128)(2,1)S(1)} %collective-permute-done.10.refs_15_), channel_id=1, source_target_pairs={{0,7},{1,0},{2,1},{3,2},{4,3},{5,4},{6,5},{7,6},{8,15},{9,8},{10,9... | collective-permute-start | bytes 786440 | tf_op jit(solution)/shard_map/ppermute | solution.py:238
  60.9 13.7 %copy-start.10 = (bf16[4,2,64,256]{3,2,1,0:T(8,128)(2,1)}, bf16[4,2,64,256]{3,2,1,0:T(8,128)(2,1)S(1)}, u32[]{:S(2)}) copy-start(bf16[4,2,64,256]{3,2,1,0:T(8,128)(2,1)S(1)} %collective-permute-done.6.refs_11_) | copy-start | bytes 786436
  60.9 11.1 %collective-permute-start.14 = (bf16[4,2,64,256]{3,2,1,0:T(8,128)(2,1)S(1)}, bf16[4,2,64,256]{3,2,1,0:T(8,128)(2,1)S(1)}, u32[]{:S(2)}, u32[]{:S(2)}) collective-permute-start(bf16[4,2,64,256]{3,2,1,0:T(8,128)(2,1)S(1)} %collective-permute-done.6.refs_11_), channel_id=1, source_target_pairs={{0,1},{1,2},{2,3},{3,4},{4,5},{5,6},{6,7},{7,0},{8,9},{9,10},{10,1... | collective-permute-start | bytes 786440 | tf_op jit(solution)/shard_map/ppermute | solution.py:240
  66.1 8.5 %copy-start.11 = (bf16[4,2,64,256]{3,2,1,0:T(8,128)(2,1)}, bf16[4,2,64,256]{3,2,1,0:T(8,128)(2,1)S(1)}, u32[]{:S(2)}) copy-start(bf16[4,2,64,256]{3,2,1,0:T(8,128)(2,1)S(1)} %collective-permute-done.5.refs_10_) | copy-start | bytes 786436
  66.1 8.5 %collective-permute-start.7 = (bf16[4,2,64,256]{3,2,1,0:T(8,128)(2,1)S(1)}, bf16[4,2,64,256]{3,2,1,0:T(8,128)(2,1)S(1)}, u32[]{:S(2)}, u32[]{:S(2)}) collective-permute-start(bf16[4,2,64,256]{3,2,1,0:T(8,128)(2,1)S(1)} %collective-permute-done.5.refs_10_), channel_id=1, source_target_pairs={{0,1},{1,2},{2,3},{3,4},{4,5},{5,6},{6,7},{7,0},{8,9},{9,10},{10,1... | collective-permute-start | bytes 786440 | tf_op jit(solution)/shard_map/ppermute | solution.py:237
  68.7 5.9 %copy-start.12 = (bf16[4,2,64,256]{3,2,1,0:T(8,128)(2,1)}, bf16[4,2,64,256]{3,2,1,0:T(8,128)(2,1)S(1)}, u32[]{:S(2)}) copy-start(bf16[4,2,64,256]{3,2,1,0:T(8,128)(2,1)S(1)} %collective-permute-done.13.refs_18_) | copy-start | bytes 786436
  68.7 9.5 %collective-permute-start.15 = (bf16[4,2,64,256]{3,2,1,0:T(8,128)(2,1)S(1)}, bf16[4,2,64,256]{3,2,1,0:T(8,128)(2,1)S(1)}, u32[]{:S(2)}, u32[]{:S(2)}) collective-permute-start(bf16[4,2,64,256]{3,2,1,0:T(8,128)(2,1)S(1)} %collective-permute-done.13.refs_18_), channel_id=1, source_target_pairs={{0,7},{1,0},{2,1},{3,2},{4,3},{5,4},{6,5},{7,6},{8,15},{9,8},{10,9... | collective-permute-start | bytes 786440 | tf_op jit(solution)/shard_map/ppermute | solution.py:242
Sparse Core Ops, SparseCore 0:
  18.7 58.1 all-gather.1
